TPU v7x, 128 devices: a whole 4x4x4 slice. The times are simulated.
128 devices in a mesh: gx: 16 (over x, z), gy: 8 (over y, core).
Axes of the slice: x: 4, y: 4, z: 4, core: 2. Of those that a mesh axis runs over, the one named last changes fastest.
Arguments:
- populations: float32 [4096, 19, 512], P(('gx', 'gy')), may hold values from 0.6 to 1.4
- neighbours: int32 [4096, 6], P(('gx', 'gy')), may hold values from -1 to 4095, as said below
- positions: float32 [16384, 3, 642], P(('gx', 'gy')), may hold values from 0.5 to 7.5
- stiffness: float32 [16384], P(('gx', 'gy')), may hold values from 0.005 to 0.02
- cell_owner: int32 [16384, 1], P(('gx', 'gy')), may hold values from 0 to 127; in each aligned block of 128 rows (0 to 127, 128 to 255, ...) at most 2 rows name the same one
- cell_block: int32 [16384], P(('gx', 'gy')), may hold values from 0 to 31
- triangles: int32 [1280, 3], replicated, may hold values from 0 to 641, all different within a row
Outputs:
- read_pops: float32 [4096, 19, 512], P(('gx', 'gy'))
Inputs may be any that keep to these rules, and one draw needn't show every extreme that they name: Each entry is -1 or a block id whose owner (id // 32, an index in the order gx+gy) lies at most one step away, cyclically, along gx and along gy from the owner of the block in that row. Faces are reciprocal: neighbours[b, 2a+1] = c exactly when neighbours[c, 2a] = b. `cell_owner`: among the rows of one device at most 2 cells name the same owner; owners are device indices in the order gx+gy. `triangles`: the three vertices of a row differ; every vertex appears in some row.
All inputs are finite; a program needn't handle non-finite values.
Results may differ from a plain program's by a relative error of at most 0.0003.
Values sent between devices are 32-bit elements; how exact they have to be, the bound alone decides.
No kernel may reach another device: no remote copies, remote signals or barrier semaphores. Data moves between devices by JAX's collectives and lax.ppermute only.
A program may use at most 128 MiB of HBM per device.

v0:
```python
import functools

import jax
import jax.numpy as jnp
import numpy as np
from jax import lax
from jax.experimental import pallas as pl
from jax.experimental.pallas import tpu as pltpu
from jax.sharding import PartitionSpec as P

vel = [
    (0, 0, 0), (1, 0, 0), (-1, 0, 0), (0, 1, 0), (0, -1, 0), (0, 0, 1), (0, 0, -1),
    (1, 1, 0), (-1, -1, 0), (1, -1, 0), (-1, 1, 0),
    (1, 0, 1), (-1, 0, -1), (1, 0, -1), (-1, 0, 1),
    (0, 1, 1), (0, -1, -1), (0, 1, -1), (0, -1, 1),
]
wts = [1.0 / 3.0] + [1.0 / 18.0] * 6 + [1.0 / 36.0] * 12
opposite = [0, 2, 1, 4, 3, 6, 5, 8, 7, 10, 9, 12, 11, 14, 13, 16, 15, 18, 17]
relax_time = 0.6
NEG, POS = {}, {}
for ax in range(3):
    NEG[ax] = [q for q in range(19) if vel[q][ax] == -1]
    POS[ax] = [q for q in range(19) if vel[q][ax] == 1]
EDGE_Q = list(range(7, 19))
FACE_TILES = 15
EDGE_TILE = 15
NT = 16
BOTH = ("gx", "gy")
f32, bf16, i32 = jnp.float32, jnp.bfloat16, jnp.int32


def split(x):
    high = x.astype(bf16).astype(f32)
    return high, x - high


def nt_dot(a, b):
    return lax.dot_general(a, b, (((1,), (1,)), ((), ())), preferred_element_type=f32)


def hat(x, grid):
    return jnp.maximum(0.0, 1.0 - jnp.abs(x - grid))


def spread_kernel(owner, block, pos, stiff, tri, out, st, force, count):
    nv = pos.shape[2]
    cells = pos.shape[1]
    for r in range(0, nv, 128):
        ids = lax.broadcasted_iota(i32, (128, tri.shape[1]), 0) + r
        hit = (ids == tri[0:1, :]) | (ids == tri[1:2, :]) | (ids == tri[2:3, :])
        st[r : r + 128, :] = hit.astype(f32).astype(bf16)
    links = nt_dot(st[...], st[...])
    rows = lax.broadcasted_iota(i32, (nv, nv), 0)
    cols = lax.broadcasted_iota(i32, (nv, nv), 1)
    springs = jnp.where(rows == cols, -2.0 * links, links)
    s_hi, s_lo = split(springs)
    s_hi, s_lo = s_hi.astype(bf16), s_lo.astype(bf16)
    for d in range(3):
        x_hi, x_lo = split(pos[d])
        x_hi, x_lo = x_hi.astype(bf16), x_lo.astype(bf16)
        total = (
            jnp.dot(x_hi, s_hi, preferred_element_type=f32)
            + jnp.dot(x_lo, s_hi, preferred_element_type=f32)
            + jnp.dot(x_hi, s_lo, preferred_element_type=f32)
        )
        force[d] = total * stiff[...]
    out[:, 0:3072] = jnp.zeros((out.shape[0], 3072), f32)
    out[:, 3072:3200] = jnp.full((out.shape[0], 128), -1.0, f32)

    def clear(t, carry):
        count[t] = 0
        return carry

    lax.fori_loop(0, out.shape[0], clear, 0)
    sub8 = lax.broadcasted_iota(i32, (8, nv), 0)
    g_even = (2 * (sub8 % 4)).astype(f32)
    g_odd = g_even + 1.0
    g_all = sub8.astype(f32)
    first4 = sub8 < 4
    lane8 = lax.broadcasted_iota(i32, (8, 128), 1)
    sub = lax.broadcasted_iota(i32, (8, 128), 0)

    def one(c):
        x = jnp.broadcast_to(pos[0, pl.ds(c, 1), :], (8, nv))
        y = jnp.broadcast_to(pos[1, pl.ds(c, 1), :], (8, nv))
        z = jnp.broadcast_to(pos[2, pl.ds(c, 1), :], (8, nv))
        f0 = jnp.broadcast_to(force[0, pl.ds(c, 1), :], (8, nv))
        f1 = jnp.broadcast_to(force[1, pl.ds(c, 1), :], (8, nv))
        f2 = jnp.broadcast_to(force[2, pl.ds(c, 1), :], (8, nv))
        h_even = hat(x, g_even)
        h_odd = hat(x, g_odd)
        f01 = jnp.where(first4, f0, f1)
        left = jnp.concatenate(
            [h_even * f01, jnp.where(first4, h_even, h_odd) * f2, h_odd * f01], axis=0
        )
        l_hi, l_lo = split(left)
        left2 = jnp.concatenate([l_hi, l_lo], axis=0).astype(bf16)
        hz = hat(z, g_all)
        plane = jnp.concatenate([hat(y, float(j)) * hz for j in range(8)], axis=0)
        p_hi, p_lo = split(plane)
        plane2 = jnp.concatenate([p_hi, p_lo], axis=0).astype(bf16)
        prod = nt_dot(left2, plane2)
        both = prod[0:24] + prod[24:48]
        res = both + pltpu.roll(both, 64, 1)
        main = jnp.where(lane8 < 64, res[0:8], res[16:24])
        mid = res[8:16]
        tail = jnp.where(lane8 < 64, mid, pltpu.roll(mid, 4, 0))
        t = owner[c]
        r = count[t]
        count[t] = r + 1
        base = pl.multiple_of((t // 8) * 8, 8)
        mine = sub == t % 8
        for k in range(12):
            row = main[k : k + 1] if k < 8 else tail[k - 8 : k - 7]
            at = pl.multiple_of(r * 1536 + 128 * k, 128)
            pltpu.store(out.at[pl.ds(base, 8), pl.ds(at, 128)], jnp.broadcast_to(row, (8, 128)), mask=mine)
        label = jnp.full((8, 128), block[c].astype(f32))
        pltpu.store(out.at[pl.ds(base, 8), 3072:3200], label, mask=mine & (lane8 == r))

    def step(n, carry):
        for m in range(4):
            one(n * 4 + m)
        return carry

    lax.fori_loop(0, cells // 4, step, 0)


def spread(owner, block, positions, stiffness, triangles, devices):
    cells, _, verts = positions.shape
    nv = -(-verts // 256) * 256
    pos = jnp.pad(
        jnp.transpose(positions, (1, 0, 2)), ((0, 0), (0, 0), (0, nv - verts)), constant_values=-100.0
    )
    tri = jnp.transpose(triangles)
    smem = pl.BlockSpec(memory_space=pltpu.SMEM)
    vmem = pl.BlockSpec(memory_space=pltpu.VMEM)
    return pl.pallas_call(
        spread_kernel,
        out_shape=jax.ShapeDtypeStruct((devices, 3200), f32),
        in_specs=[smem, smem, vmem, vmem, vmem],
        out_specs=vmem,
        scratch_shapes=[
            pltpu.VMEM((nv, triangles.shape[0]), bf16),
            pltpu.VMEM((3, cells, nv), f32),
            pltpu.SMEM((devices,), i32),
        ],
        compiler_params=pltpu.CompilerParams(vmem_limit_bytes=48 << 20),
        name="spread",
    )(owner, block, pos, stiffness[:, None], tri)


def lane_take(x, index):
    return jnp.take_along_axis(x, index, axis=1)


def collide_kernel(got, pops, post, table, body):
    slots = got.shape[0]
    lane = lax.broadcasted_iota(i32, (slots, 128), 1)
    ids = got[:, 3072:3200]
    picks = []
    for r in range(2):
        col = jnp.broadcast_to(ids[:, r : r + 1], (slots, 128))
        hit = (col == lane.astype(f32)).astype(f32)
        picks.append(jnp.transpose(hit)[0:32].astype(bf16))
    for n in range(3):
        total = jnp.zeros((32, 512), f32)
        for r in range(2):
            part = got[:, r * 1536 + n * 512 : r * 1536 + (n + 1) * 512]
            hi, lo = split(part)
            total = total + jnp.dot(picks[r], hi.astype(bf16), preferred_element_type=f32)
            total = total + jnp.dot(picks[r], lo.astype(bf16), preferred_element_type=f32)
        body[n] = total

    lanes = lax.broadcasted_iota(i32, (8, 128), 1)
    low = lanes < 64
    keep = 1.0 - 1.0 / relax_time
    gain = 1.0 - 0.5 / relax_time

    def group(g, carry):
        rows = pl.ds(pl.multiple_of(g * 8, 8), 8)
        for a in range(4):
            cut = slice(128 * a, 128 * (a + 1))
            f = [pops[rows, q, cut] * wts[q] for q in range(19)]
            force = [body[d, rows, cut] for d in range(3)]
            rho = f[0]
            for q in range(1, 19):
                rho = rho + f[q]
            u = []
            for d in range(3):
                m = 0.5 * force[d]
                for q in range(1, 19):
                    if vel[q][d] == 1:
                        m = m + f[q]
                    elif vel[q][d] == -1:
                        m = m - f[q]
                u.append(m / rho)
            speed = u[0] * u[0] + u[1] * u[1] + u[2] * u[2]
            work = u[0] * force[0] + u[1] * force[1] + u[2] * force[2]
            rho_t = rho * (1.0 / relax_time)
            flat = rho_t * (1.0 - 1.5 * speed) - (3.0 * gain) * work
            post[0, rows, cut] = keep * f[0] + wts[0] * flat
            for q in range(1, 19, 2):
                along = push = None
                for d in range(3):
                    e = vel[q][d]
                    if e:
                        along = e * u[d] if along is None else along + e * u[d]
                        push = e * force[d] if push is None else push + e * force[d]
                even = wts[q] * (flat + along * (4.5 * rho_t * along + (9.0 * gain) * push))
                odd = wts[q] * (3.0 * rho_t * along + (3.0 * gain) * push)
                post[q, rows, cut] = keep * f[q] + (even + odd)
                post[q + 1, rows, cut] = keep * f[q + 1] + (even - odd)
        for n in range(5):
            table[n, rows, :] = jnp.where(low, post[NEG[0][n], rows, 0:128], post[POS[0][n], rows, 384:512])
            m = lanes % 64
            first, second = m // 8, m % 8
            for ax in (1, 2):
                picked = None
                for a in range(4):
                    inside = (first % 2) * 64
                    if ax == 1:
                        at_low, at_high = inside + second, inside + 56 + second
                    else:
                        at_low, at_high = inside + second * 8, inside + second * 8 + 7
                    cut = slice(128 * a, 128 * (a + 1))
                    val = jnp.where(
                        low, lane_take(post[NEG[ax][n], rows, cut], at_low), lane_take(post[POS[ax][n], rows, cut], at_high)
                    )
                    picked = val if picked is None else jnp.where(first // 2 == a, val, picked)
                table[5 * ax + n, rows, :] = picked
        line = jnp.zeros((8, 128), f32)
        w = lanes % 8
        for n, q in enumerate(EDGE_Q):
            ex, ey, ez = vel[q]
            at = [7 if e == 1 else 0 for e in vel[q]]
            mine = lanes // 8 == n
            if ex:
                a = 3 if ex == 1 else 0
                base = 64 if ex == 1 else 0
                where_ = base + (at[1] * 8 + w if ey else w * 8 + at[2])
                val = lane_take(post[q, rows, 128 * a : 128 * (a + 1)], where_)
                line = jnp.where(mine, val, line)
            else:
                where_ = (w % 2) * 64 + at[1] * 8 + at[2]
                for a in range(4):
                    val = lane_take(post[q, rows, 128 * a : 128 * (a + 1)], where_)
                    line = jnp.where(mine & (w // 2 == a), val, line)
        table[EDGE_TILE, rows, :] = line
        return carry

    lax.fori_loop(0, 4, group, 0)


def collide(got, populations):
    vmem = pl.BlockSpec(memory_space=pltpu.VMEM)
    return pl.pallas_call(
        collide_kernel,
        out_shape=(jax.ShapeDtypeStruct((19, 32, 512), f32), jax.ShapeDtypeStruct((NT, 32, 128), f32)),
        in_specs=[vmem, vmem],
        out_specs=(vmem, vmem),
        scratch_shapes=[pltpu.VMEM((3, 32, 512), f32)],
        compiler_params=pltpu.CompilerParams(vmem_limit_bytes=48 << 20),
        name="collide",
    )(got, populations)


def stream_kernel(where_face, where_edge, post, there, mid, down, up, down2, up2, out, table, ghost, sem):
    parts = [(mid, 50, 50), (down, 0, 50), (up, 100, 50), (down2, 150, 5), (up2, 155, 5)]
    copies = [
        pltpu.make_async_copy(ref, table.at[pl.ds(at, size)], sem.at[n]) for n, (ref, at, size) in enumerate(parts)
    ]
    for c in copies:
        c.start()
    for c in copies:
        c.wait()
    lanes = lax.broadcasted_iota(i32, (8, 128), 1)
    sub = lax.broadcasted_iota(i32, (8, 128), 0)

    def row_of(at, tile):
        return table[at // 32 + tile, pl.ds(at % 32, 8, stride=0), :]

    def fetch(g, carry):
        rows = pl.ds(pl.multiple_of(g * 8, 8), 8)
        for ax in range(3):
            made = [jnp.zeros((8, 128), f32)] * 5
            for i in range(8):
                low_at = where_face[(g * 8 + i) * 6 + 2 * ax]
                high_at = where_face[(g * 8 + i) * 6 + 2 * ax + 1]
                for n in range(5):
                    t = 5 * ax + n
                    both = jnp.where(lanes < 64, row_of(high_at, t), row_of(low_at, t))
                    made[n] = jnp.where(sub == i, both, made[n])
            for n in range(5):
                ghost[5 * ax + n, rows, :] = made[n]
        line = jnp.zeros((8, 128), f32)
        for i in range(8):
            for n in range(12):
                at = where_edge[(g * 8 + i) * 12 + n]
                line = jnp.where((lanes // 8 == n) & (sub == i), row_of(at, 0), line)
        ghost[EDGE_TILE, rows, :] = line
        return carry

    lax.fori_loop(0, 4, fetch, 0)
    jj = (lanes // 8) % 8
    kk = lanes % 8

    def group(g, carry):
        rows = pl.ds(pl.multiple_of(g * 8, 8), 8)
        flags = there[rows, :]

        def flag(n):
            return jnp.broadcast_to(flags[:, n : n + 1], (8, 128)) > 0.5

        face_on = [flag(n) for n in range(6)]
        edge_on = [flag(6 + n) for n in range(12)]
        edges = ghost[EDGE_TILE, rows, :]
        out[rows, 0, :] = post[0, rows, :]
        for q in range(1, 19):
            e = vel[q]
            ex, ey, ez = e
            shift = ex * 64 + ey * 8 + ez
            tiles = [post[q, rows, 128 * a : 128 * (a + 1)] for a in range(4)]
            rolled = [pltpu.roll(t, shift % 128, 1) for t in tiles]
            for a in range(4):
                if shift > 0:
                    val = jnp.where(lanes < shift, rolled[(a - 1) % 4], rolled[a])
                else:
                    val = jnp.where(lanes >= 128 + shift, rolled[(a + 1) % 4], rolled[a])
                ii = 2 * a + lanes // 64
                back = post[opposite[q], rows, 128 * a : 128 * (a + 1)]
                coords = (ii, jj, kk)
                crossing = [None if e[d] == 0 else coords[d] == (0 if e[d] == 1 else 7) for d in range(3)]
                if ex == 1 and a != 0 or ex == -1 and a != 3:
                    crossing[0] = None
                axes = [d for d in range(3) if crossing[d] is not None]
                if axes:
                    out_of = crossing[axes[0]]
                    for d in axes[1:]:
                        out_of = out_of | crossing[d]
                    val = jnp.where(out_of, back, val)
                for d in axes:
                    face = 2 * d + (0 if e[d] == 1 else 1)
                    n = (POS[d] if e[d] == 1 else NEG[d]).index(q)
                    source = ghost[5 * d + n, rows, :]
                    base = 64 if e[d] == 1 else 0
                    if d == 0:
                        brought = pltpu.roll(source, (64 + ey * 8 + ez) % 128, 1)
                    elif d == 1:
                        brought = lane_take(source, base + ((ii - ex) * 8 + kk - ez) % 64)
                    else:
                        brought = lane_take(source, base + ((ii - ex) * 8 + jj - ey) % 64)
                    use = crossing[d] & face_on[face]
                    for other in axes:
                        if other != d:
                            use = use & ~crossing[other]
                    val = jnp.where(use, brought, val)
                if len(axes) == 2:
                    n = q - 7
                    along = kk if ez == 0 else (jj if ey == 0 else ii)
                    brought = lane_take(edges, 8 * n + along)
                    val = jnp.where(crossing[axes[0]] & crossing[axes[1]] & edge_on[n], brought, val)
                out[rows, q, 128 * a : 128 * (a + 1)] = val
        return carry

    lax.fori_loop(0, 4, group, 0)


def stream(where_face, where_edge, post, there, mid, down, up, down2, up2):
    smem = pl.BlockSpec(memory_space=pltpu.SMEM)
    vmem = pl.BlockSpec(memory_space=pltpu.VMEM)
    hbm = pl.BlockSpec(memory_space=pl.ANY)
    return pl.pallas_call(
        stream_kernel,
        out_shape=jax.ShapeDtypeStruct((32, 19, 512), f32),
        in_specs=[smem, smem, vmem, vmem] + [hbm] * 5,
        out_specs=vmem,
        scratch_shapes=[
            pltpu.VMEM((160, 32, 128), f32),
            pltpu.VMEM((NT, 32, 128), f32),
            pltpu.SemaphoreType.DMA((5,)),
        ],
        compiler_params=pltpu.CompilerParams(vmem_limit_bytes=48 << 20),
        name="stream",
    )(where_face, where_edge, post, there, mid, down, up, down2, up2)


def send(array, axis, step):
    size = lax.axis_size(axis)
    return lax.ppermute(array, axis, [(i, (i + step) % size) for i in range(size)])


def look_up(neighbours):
    rows_gx, rows_gy = lax.axis_size("gx"), lax.axis_size("gy")
    me_x, me_y = lax.axis_index("gx"), lax.axis_index("gy")
    column = jnp.concatenate([send(neighbours, "gx", 1), neighbours, send(neighbours, "gx", -1)], axis=0)
    near = jnp.concatenate([send(column, "gy", 1), column, send(column, "gy", -1)], axis=0)

    def place(ids, reach):
        safe = jnp.maximum(ids, 0)
        owner = safe // 32
        x = (owner // rows_gy - me_x + reach) % rows_gx
        y = (owner % rows_gy - me_y + reach) % rows_gy
        return x, y, safe % 32

    x, y, slot = place(neighbours, 1)
    on_face = neighbours >= 0
    where_face = jnp.where(on_face, (y * 50 + x * 16) * 32 + slot, 0)
    near_row = (y * 3 + x) * 32 + slot
    second = jnp.take(near, jnp.where(on_face, near_row, 0)[:, 2:6].reshape(-1), axis=0).reshape(32, 4, 6)
    two = []
    for q in EDGE_Q:
        e = vel[q]
        axes = [d for d in range(3) if e[d]]
        f1 = 2 * axes[1] + (0 if e[axes[1]] == 1 else 1)
        f2 = 2 * axes[0] + (0 if e[axes[0]] == 1 else 1)
        two.append(jnp.where(on_face[:, f1], second[:, f1 - 2, f2], -1))
    two = jnp.stack(two, axis=1)
    x, y, slot = place(two, 2)
    on_edge = two >= 0
    inner = (y - 1) * 50 + jnp.where(x == 0, 48, jnp.where(x == 4, 49, (x - 1) * 16 + EDGE_TILE))
    tile = jnp.where(y == 0, 150 + x, jnp.where(y == 4, 155 + x, inner))
    where_edge = jnp.where(on_edge, tile * 32 + slot, 0)
    there = jnp.concatenate([on_face, on_edge], axis=1).astype(f32)
    there = jnp.pad(there, ((0, 0), (0, 128 - 18)))
    return where_face.reshape(-1), where_edge.reshape(-1), there


def exchange(table):
    edge = table[EDGE_TILE : EDGE_TILE + 1]
    left, right = send(table, "gx", 1), send(table, "gx", -1)
    left2, right2 = send(edge, "gx", 2), send(edge, "gx", -2)
    mid = jnp.concatenate([left, table, right, left2, right2], axis=0)
    edges = jnp.concatenate([left2, left[EDGE_TILE:], edge, right[EDGE_TILE:], right2], axis=0)
    return mid, send(mid, "gy", 1), send(mid, "gy", -1), send(edges, "gy", 2), send(edges, "gy", -2)


def body(populations, neighbours, positions, stiffness, cell_owner, cell_block, triangles):
    devices = lax.axis_size("gx") * lax.axis_size("gy")
    where_face, where_edge, there = look_up(neighbours)
    slots = spread(cell_owner[:, 0], cell_block, positions, stiffness, triangles, devices)
    got = lax.all_to_all(slots, BOTH, split_axis=0, concat_axis=0, tiled=True)
    post, table = collide(got, populations)
    return stream(where_face, where_edge, post, there, *exchange(table))


def solution(mesh):
    placed = (
        P(BOTH, None, None),
        P(BOTH, None),
        P(BOTH, None, None),
        P(BOTH),
        P(BOTH, None),
        P(BOTH),
        P(),
    )
    return jax.shard_map(
        body, mesh=mesh, in_specs=placed, out_specs=P(BOTH, None, None), check_vma=False
    )
```

profile of v0, /device:TPU:1, one launch (start us, length us, event | category | flops | bytes accessed | tf_op | source)
XLA Modules:
  0.0 116.5 jit_solution(684402502715445544)
XLA Ops:
  0.0 0.8 copy.74.stiff
  0.8 1.6 %copy.73 = f32[128,3,642]{2,0,1:T(8,128)S(1)} copy(f32[128,3,642]{0,2,1:T(8,128)} %param.9) | data formatting | bytes 1972224 | tf_op args[2]
  2.3 0.0 copy-start
  2.4 0.0 copy-start.1
  2.4 0.0 copy-start.2
  2.4 0.1 pad.10.pos
  2.5 0.6 copy-done
  3.1 23.0 %spread.1 = f32[128,3200]{1,0:T(8,128)S(1)} custom-call(s32[128]{0:T(128)S(1)} %bitcast.38, s32[128]{0:T(128)S(1)} %copy-done.2, f32[3,128,768]{2,1,0:T(8,128)S(1)} %pad.10.pos, f32[128,1]{1,0:T(8,128)S(1)} %copy.74.stiff, s32[3,1280]{1,0:T(4,128)S(1)} %bitcast.37), custom_call_target="tpu_custom_call" | custom-call | tf_op jit(solution)/shard_map/spread/pallas_call | solution.py:137
  26.1 2.8 %copy.75 = f32[128,1,3200]{2,1,0:T(1,128)} copy(f32[128,1,3200]{2,0,1:T(8,128)S(1)} %bitcast.36) | data formatting | bytes 3276800 | tf_op jit(solution)/shard_map/all_to_all | solution.py:441
  29.0 11.9 %all-to-all-start = ((f32[128,1,3200]{2,1,0:T(1,128)}), f32[128,1,3200]{2,1,0:T(1,128)}, u32[]{:S(2)}, u32[]{:S(2)}) async-start(f32[128,1,3200]{2,1,0:T(1,128)} %copy.75), calls=%async_computation | async-start | bytes 3276800 | tf_op jit(solution)/shard_map/all_to_all | solution.py:441
  40.9 1.6 %collective-permute-start = (s32[32,6]{0,1:T(8,128)S(1)}, s32[32,6]{0,1:T(8,128)S(1)}, u32[]{:S(2)}, u32[]{:S(2)}) collective-permute-start(s32[32,6]{0,1:T(8,128)S(1)} %copy-done.4), channel_id=1, source_target_pairs={{0,8},{8,16},{16,24},{24,32},{32,40},{40,48},{48,56},{56,64},{64,7... | collective-permute-start | bytes 2312 | tf_op jit(solution)/shard_map/ppermute | solution.py:389
  42.5 4.0 %collective-permute-start.1 = (s32[32,6]{0,1:T(8,128)S(1)}, s32[32,6]{0,1:T(8,128)S(1)}, u32[]{:S(2)}, u32[]{:S(2)}) collective-permute-start(s32[32,6]{0,1:T(8,128)S(1)} %copy-done.4), channel_id=1, source_target_pairs={{0,120},{8,0},{16,8},{24,16},{32,24},{40,32},{48,40},{56,48},{64,5... | collective-permute-start | bytes 2312 | tf_op jit(solution)/shard_map/ppermute | solution.py:389
  46.4 0.1 copy.56
  46.5 0.1 add_select_fusion.6
  46.6 0.1 compare_and_fusion
  46.7 0.1 reshape.74
  46.8 16.2 %collective-permute-done = s32[32,6]{0,1:T(8,128)S(1)} collective-permute-done((s32[32,6]{0,1:T(8,128)S(1)}, s32[32,6]{0,1:T(8,128)S(1)}, u32[]{:S(2)}, u32[]{:S(2)}) %collective-permute-start) | collective-permute-done | bytes 800 | tf_op jit(solution)/shard_map/ppermute | solution.py:389
  63.1 0.1 pad_add_fusion.1
  63.1 1.6 %collective-permute-start.3 = (s32[96,6]{0,1:T(8,128)S(1)}, s32[96,6]{0,1:T(8,128)S(1)}, u32[]{:S(2)}, u32[]{:S(2)}) collective-permute-start(s32[96,6]{0,1:T(8,128)S(1)} %pad_add_fusion.1), channel_id=1, source_target_pairs={{0,7},{1,0},{2,1},{3,2},{4,3},{5,4},{6,5},{7,6},{8,15},{9,8},{10,9... | collective-permute-start | bytes 6920 | tf_op jit(solution)/shard_map/ppermute | solution.py:389
  64.7 0.9 collective-permute-start.2
  65.7 0.1 reshape.73.where_face
  65.8 0.1 copy.58
  65.9 0.7 copy.76.pops
  66.6 0.3 collective-permute-done.3
  67.0 0.5 collective-permute-done.2
  67.4 0.1 concatenate.17
  67.5 0.1 copy.59
  67.6 0.6 gather_fusion
  68.3 0.1 copy.60
  68.4 0.1 copy.72
  68.5 0.1 copy.71
  68.6 0.1 copy.70
  68.7 0.1 copy.69
  68.8 0.1 copy.67
  68.9 0.1 copy.66
  68.9 0.1 copy.65
  69.0 0.1 copy.64
  69.1 0.1 copy.63
  69.2 1.5 %copy.80 = f32[128,1,3200]{2,0,1:T(8,128)S(1)} copy(f32[128,1,3200]{2,1,0:T(1,128)} %all-to-all-done) | data formatting | bytes 3276800
  70.8 4.6 %collide.1 = (f32[19,32,512]{2,1,0:T(8,128)S(1)}, f32[16,32,128]{2,1,0:T(8,128)S(1)}) custom-call(f32[128,3200]{1,0:T(8,128)S(1)} %bitcast.35, f32[32,19,512]{2,1,0:T(8,128)S(1)} %copy.76.pops), custom_call_target="tpu_custom_call" | custom-call | tf_op jit(solution)/shard_map/collide/pallas_call | solution.py:256
  75.3 0.1 collective-permute-start.4
  75.4 0.1 broadcast_select_fusion
  75.5 0.1 copy.68
  75.6 0.1 copy.62
  75.7 0.1 copy.61
  75.8 4.8 %collective-permute-start.5 = (f32[16,32,128]{2,1,0:T(8,128)S(1)}, f32[16,32,128]{2,1,0:T(8,128)S(1)}, u32[]{:S(2)}, u32[]{:S(2)}) collective-permute-start(f32[16,32,128]{2,1,0:T(8,128)S(1)} %get-tuple-element.8), channel_id=1, source_target_pairs={{0,120},{8,0},{16,8},{24,16},{32,24},{40,32},{48,40},{56,48},{64,5... | collective-permute-start | bytes 786440 | tf_op jit(solution)/shard_map/ppermute | solution.py:389
  80.5 0.1 broadcast_select_fusion.4
  80.6 0.1 stack.2
  80.7 0.3 collective-permute-start.7
  81.0 3.0 %collective-permute-start.6 = (f32[1,32,128]{2,1,0:T(8,128)S(1)}, f32[1,32,128]{2,1,0:T(8,128)S(1)}, u32[]{:S(2)}, u32[]{:S(2)}) collective-permute-start(f32[1,32,128]{2,1,0:T(8,128)S(1)} %slice.85), channel_id=1, source_target_pairs={{0,16},{8,24},{16,32},{24,40},{32,48},{40,56},{48,64},{56,72},{64,... | collective-permute-start | bytes 49160 | tf_op jit(solution)/shard_map/ppermute | solution.py:389
  84.1 3.3 %collective-permute-done.6 = f32[1,32,128]{2,1,0:T(8,128)S(1)} collective-permute-done((f32[1,32,128]{2,1,0:T(8,128)S(1)}, f32[1,32,128]{2,1,0:T(8,128)S(1)}, u32[]{:S(2)}, u32[]{:S(2)}) %collective-permute-start.6) | collective-permute-done | bytes 16416 | tf_op jit(solution)/shard_map/ppermute | solution.py:389
  87.4 0.0 collective-permute-done.7
  87.4 5.2 %collective-permute-start.9 = (f32[50,32,128]{2,1,0:T(8,128)S(1)}, f32[50,32,128]{2,1,0:T(8,128)}, u32[]{:S(2)}, u32[]{:S(2)}) collective-permute-start(f32[50,32,128]{2,1,0:T(8,128)S(1)} %get-tuple-element.16.mid), channel_id=1, source_target_pairs={{0,7},{1,0},{2,1},{3,2},{4,3},{5,4},{6,5},{7,6},{8,15},{9,8},{10,9... | collective-permute-start | bytes 2457608 | tf_op jit(solution)/shard_map/ppermute | solution.py:389
  92.6 0.0 collective-permute-start.8
  92.6 0.1 ne.108
  92.8 0.1 ge.23
  92.9 0.1 div.46
  93.0 0.1 rem.165
  93.1 0.1 pad_add_fusion
  93.2 2.7 %collective-permute-start.11 = (f32[5,32,128]{2,1,0:T(8,128)S(1)}, f32[5,32,128]{2,1,0:T(8,128)S(1)}, u32[]{:S(2)}, u32[]{:S(2)}) collective-permute-start(f32[5,32,128]{2,1,0:T(8,128)S(1)} %get-tuple-element.15), channel_id=1, source_target_pairs={{0,6},{1,7},{2,0},{3,1},{4,2},{5,3},{6,4},{7,5},{8,14},{9,15},{10,... | collective-permute-start | bytes 245768 | tf_op jit(solution)/shard_map/ppermute | solution.py:389
  95.9 2.3 %collective-permute-done.11.up2 = f32[5,32,128]{2,1,0:T(8,128)S(1)} collective-permute-done((f32[5,32,128]{2,1,0:T(8,128)S(1)}, f32[5,32,128]{2,1,0:T(8,128)S(1)}, u32[]{:S(2)}, u32[]{:S(2)}) %collective-permute-start.11) | collective-permute-done | bytes 81952 | tf_op jit(solution)/shard_map/ppermute | solution.py:389
  98.2 8.5 %collective-permute-done.10.down2 = f32[5,32,128]{2,1,0:T(8,128)S(1)} collective-permute-done((f32[5,32,128]{2,1,0:T(8,128)S(1)}, f32[5,32,128]{2,1,0:T(8,128)S(1)}, u32[]{:S(2)}, u32[]{:S(2)}) %collective-permute-start.10) | collective-permute-done | bytes 81952 | tf_op jit(solution)/shard_map/ppermute | solution.py:389
  106.7 8.0 %stream.1 = f32[32,19,512]{2,1,0:T(8,128)S(1)} custom-call(s32[192]{0:T(256)S(1)} %reshape.73.where_face, s32[384]{0:T(512)S(1)} %fusion.18.where_edge, f32[19,32,512]{2,1,0:T(8,128)S(1)} %get-tuple-element.7.post, f32[32,128]{1,0:T(8,128)S(1)} %pad_convert_fusion.there, f32[50,32,128]{2,1,0:T(8,128)S(1)} %get-tuple-element.16.mid, ...), custom_call_target="tpu_custom_call" | custom-call | tf_op jit(solution)/shard_map/stream/pallas_call | solution.py:372
  114.7 1.8 %copy.77 = f32[32,19,512]{2,0,1:T(8,128)} copy(f32[32,19,512]{2,1,0:T(8,128)S(1)} %stream.1) | data formatting | bytes 2490368 | tf_op jit(solution)/shard_map/stream/pallas_call | solution.py:372
  (30 shorter events, 0.2 us)
Async XLA Ops:
  2.3 0.7 copy-start
  2.4 0.7 copy-start.1
  2.4 0.7 copy-start.2
  29.0 11.9 %copy-start.4 = (s32[32,6]{0,1:T(8,128)S(1)}, s32[32,6]{0,1:T(8,128)}, u32[]{:S(2)}) copy-start(s32[32,6]{0,1:T(8,128)} %param.8) | copy-start | bytes 2308
  29.0 36.9 %copy-start.3 = (f32[32,19,512]{2,0,1:T(8,128)S(1)}, f32[32,19,512]{2,0,1:T(8,128)}, u32[]{:S(2)}) copy-start(f32[32,19,512]{2,0,1:T(8,128)} %param.7) | copy-start | bytes 3735556
  29.0 40.2 %all-to-all-start = ((f32[128,1,3200]{2,1,0:T(1,128)}), f32[128,1,3200]{2,1,0:T(1,128)}, u32[]{:S(2)}, u32[]{:S(2)}) async-start(f32[128,1,3200]{2,1,0:T(1,128)} %copy.75), calls=%async_computation | async-start | bytes 3276800 | tf_op jit(solution)/shard_map/all_to_all | solution.py:441
  40.9 22.2 %collective-permute-start = (s32[32,6]{0,1:T(8,128)S(1)}, s32[32,6]{0,1:T(8,128)S(1)}, u32[]{:S(2)}, u32[]{:S(2)}) collective-permute-start(s32[32,6]{0,1:T(8,128)S(1)} %copy-done.4), channel_id=1, source_target_pairs={{0,8},{8,16},{16,24},{24,32},{32,40},{40,48},{48,56},{56,64},{64,7... | collective-permute-start | bytes 2312 | tf_op jit(solution)/shard_map/ppermute | solution.py:389
  42.5 20.6 %collective-permute-start.1 = (s32[32,6]{0,1:T(8,128)S(1)}, s32[32,6]{0,1:T(8,128)S(1)}, u32[]{:S(2)}, u32[]{:S(2)}) collective-permute-start(s32[32,6]{0,1:T(8,128)S(1)} %copy-done.4), channel_id=1, source_target_pairs={{0,120},{8,0},{16,8},{24,16},{32,24},{40,32},{48,40},{56,48},{64,5... | collective-permute-start | bytes 2312 | tf_op jit(solution)/shard_map/ppermute | solution.py:389
  63.1 3.8 %collective-permute-start.3 = (s32[96,6]{0,1:T(8,128)S(1)}, s32[96,6]{0,1:T(8,128)S(1)}, u32[]{:S(2)}, u32[]{:S(2)}) collective-permute-start(s32[96,6]{0,1:T(8,128)S(1)} %pad_add_fusion.1), channel_id=1, source_target_pairs={{0,7},{1,0},{2,1},{3,2},{4,3},{5,4},{6,5},{7,6},{8,15},{9,8},{10,9... | collective-permute-start | bytes 6920 | tf_op jit(solution)/shard_map/ppermute | solution.py:389
  64.7 2.7 %collective-permute-start.2 = (s32[96,6]{0,1:T(8,128)S(1)}, s32[96,6]{0,1:T(8,128)S(1)}, u32[]{:S(2)}, u32[]{:S(2)}) collective-permute-start(s32[96,6]{0,1:T(8,128)S(1)} %pad_add_fusion.1), channel_id=1, source_target_pairs={{0,1},{1,2},{2,3},{3,4},{4,5},{5,6},{6,7},{7,0},{8,9},{9,10},{10,1... | collective-permute-start | bytes 6920 | tf_op jit(solution)/shard_map/ppermute | solution.py:389
  75.3 8.6 %collective-permute-start.4 = (f32[16,32,128]{2,1,0:T(8,128)S(1)}, f32[16,32,128]{2,1,0:T(8,128)S(1)}, u32[]{:S(2)}, u32[]{:S(2)}) collective-permute-start(f32[16,32,128]{2,1,0:T(8,128)S(1)} %get-tuple-element.8), channel_id=1, source_target_pairs={{0,8},{8,16},{16,24},{24,32},{32,40},{40,48},{48,56},{56,64},{64,7... | collective-permute-start | bytes 786440 | tf_op jit(solution)/shard_map/ppermute | solution.py:389
  75.8 8.3 %collective-permute-start.5 = (f32[16,32,128]{2,1,0:T(8,128)S(1)}, f32[16,32,128]{2,1,0:T(8,128)S(1)}, u32[]{:S(2)}, u32[]{:S(2)}) collective-permute-start(f32[16,32,128]{2,1,0:T(8,128)S(1)} %get-tuple-element.8), channel_id=1, source_target_pairs={{0,120},{8,0},{16,8},{24,16},{32,24},{40,32},{48,40},{56,48},{64,5... | collective-permute-start | bytes 786440 | tf_op jit(solution)/shard_map/ppermute | solution.py:389
  80.7 6.7 %collective-permute-start.7 = (f32[1,32,128]{2,1,0:T(8,128)S(1)}, f32[1,32,128]{2,1,0:T(8,128)S(1)}, u32[]{:S(2)}, u32[]{:S(2)}) collective-permute-start(f32[1,32,128]{2,1,0:T(8,128)S(1)} %slice.85), channel_id=1, source_target_pairs={{0,112},{8,120},{16,0},{24,8},{32,16},{40,24},{48,32},{56,40},{64,... | collective-permute-start | bytes 49160 | tf_op jit(solution)/shard_map/ppermute | solution.py:389
  81.0 6.4 %collective-permute-start.6 = (f32[1,32,128]{2,1,0:T(8,128)S(1)}, f32[1,32,128]{2,1,0:T(8,128)S(1)}, u32[]{:S(2)}, u32[]{:S(2)}) collective-permute-start(f32[1,32,128]{2,1,0:T(8,128)S(1)} %slice.85), channel_id=1, source_target_pairs={{0,16},{8,24},{16,32},{24,40},{32,48},{40,56},{48,64},{56,72},{64,... | collective-permute-start | bytes 49160 | tf_op jit(solution)/shard_map/ppermute | solution.py:389
  87.4 19.3 %collective-permute-start.9 = (f32[50,32,128]{2,1,0:T(8,128)S(1)}, f32[50,32,128]{2,1,0:T(8,128)}, u32[]{:S(2)}, u32[]{:S(2)}) collective-permute-start(f32[50,32,128]{2,1,0:T(8,128)S(1)} %get-tuple-element.16.mid), channel_id=1, source_target_pairs={{0,7},{1,0},{2,1},{3,2},{4,3},{5,4},{6,5},{7,6},{8,15},{9,8},{10,9... | collective-permute-start | bytes 2457608 | tf_op jit(solution)/shard_map/ppermute | solution.py:389
  92.6 14.1 %collective-permute-start.8 = (f32[50,32,128]{2,1,0:T(8,128)S(1)}, f32[50,32,128]{2,1,0:T(8,128)}, u32[]{:S(2)}, u32[]{:S(2)}) collective-permute-start(f32[50,32,128]{2,1,0:T(8,128)S(1)} %get-tuple-element.16.mid), channel_id=1, source_target_pairs={{0,1},{1,2},{2,3},{3,4},{4,5},{5,6},{6,7},{7,0},{8,9},{9,10},{10,1... | collective-permute-start | bytes 2457608 | tf_op jit(solution)/shard_map/ppermute | solution.py:389
  93.2 5.0 %collective-permute-start.11 = (f32[5,32,128]{2,1,0:T(8,128)S(1)}, f32[5,32,128]{2,1,0:T(8,128)S(1)}, u32[]{:S(2)}, u32[]{:S(2)}) collective-permute-start(f32[5,32,128]{2,1,0:T(8,128)S(1)} %get-tuple-element.15), channel_id=1, source_target_pairs={{0,6},{1,7},{2,0},{3,1},{4,2},{5,3},{6,4},{7,5},{8,14},{9,15},{10,... | collective-permute-start | bytes 245768 | tf_op jit(solution)/shard_map/ppermute | solution.py:389
  95.9 10.8 %collective-permute-start.10 = (f32[5,32,128]{2,1,0:T(8,128)S(1)}, f32[5,32,128]{2,1,0:T(8,128)S(1)}, u32[]{:S(2)}, u32[]{:S(2)}) collective-permute-start(f32[5,32,128]{2,1,0:T(8,128)S(1)} %get-tuple-element.15), channel_id=1, source_target_pairs={{0,2},{1,3},{2,4},{3,5},{4,6},{5,7},{6,0},{7,1},{8,10},{9,11},{10,... | collective-permute-start | bytes 245768 | tf_op jit(solution)/shard_map/ppermute | solution.py:389
where the time goes:
time: 117 us; the launch traced here: 116 us
  starting transfers between devices  35.9 us (31%)
  Pallas kernels  35.6 us (30%)
  waiting for transfers between devices  31.2 us (27%)
  local copies, waits for them, and re-layouts  12.9 us (11%)
    ppermute x12, waiting for transfers between devices, send(): lax.ppermute(array, axis, [(i, (i + step) % size) for i in range(size)])  31.2 us
    ppermute x12, starting transfers between devices, send(): lax.ppermute(array, axis, [(i, (i + step) % size) for i in range(size)])  24 us
    pallas_call x1, Pallas kernels, spread(): pl.pallas_call(spread_kernel, out_shape=jax.ShapeDtypeStruct((devices, 32...  23 us
    all_to_all x1, starting transfers between devices, body(): got = lax.all_to_all(slots, BOTH, split_axis=0, concat_axis=0, tiled=True)  11.9 us
    pallas_call x1, Pallas kernels, stream(): pl.pallas_call(stream_kernel, out_shape=jax.ShapeDtypeStruct((32, 19, 512...  8.02 us
    unnamed x21, local copies, waits for them, and re-layouts  4.62 us
    pallas_call x1, Pallas kernels, collide(): pl.pallas_call(collide_kernel, out_shape=(jax.ShapeDtypeStruct((19, 32, 5...  4.56 us
    all_to_all x1, local copies, waits for them, and re-layouts, body(): got = lax.all_to_all(slots, BOTH, split_axis=0, concat_axis=0, tiled=True)  2.85 us
  transfers between devices with their start and end apart: 13, of which 6 were waited for; matrix products, arithmetic and copies ran while one was open for 4% of the time, Pallas kernels for 0%

commit v1 on v0

--- a/solution.py
+++ b/solution.py
@@ -25,15 +25,12 @@
 FACE_TILES = 15
 EDGE_TILE = 15
 NT = 16
+NOWHERE = 160 * 32
+WIDE = 3328
 BOTH = ("gx", "gy")
 f32, bf16, i32 = jnp.float32, jnp.bfloat16, jnp.int32
 
 
-def split(x):
-    high = x.astype(bf16).astype(f32)
-    return high, x - high
-
-
 def nt_dot(a, b):
     return lax.dot_general(a, b, (((1,), (1,)), ((), ())), preferred_element_type=f32)
 
@@ -42,45 +39,67 @@
     return jnp.maximum(0.0, 1.0 - jnp.abs(x - grid))
 
 
-def spread_kernel(owner, block, pos, stiff, tri, out, st, force, count):
-    nv = pos.shape[2]
-    cells = pos.shape[1]
+def spread_kernel(owner_in, block_in, stiff_in, raw_in, tri_in, near_in, out, owner, block, stiff, raw, tri, near, sem, st, pos, force, hats, count):
+    cells, nv = pos.shape[1:]
+    verts = raw.shape[1]
+    pairs = ((tri_in, tri), (raw_in, raw), (near_in, near), (owner_in, owner), (block_in, block), (stiff_in, stiff))
+    copies = [pltpu.make_async_copy(a, b, sem.at[n]) for n, (a, b) in enumerate(pairs)]
+    for c in copies:
+        c.start()
+    for c in copies:
+        c.wait()
     for r in range(0, nv, 128):
         ids = lax.broadcasted_iota(i32, (128, tri.shape[1]), 0) + r
         hit = (ids == tri[0:1, :]) | (ids == tri[1:2, :]) | (ids == tri[2:3, :])
         st[r : r + 128, :] = hit.astype(f32).astype(bf16)
+        for d in range(3):
+            have = min(verts - r, 128)
+            piece = raw[d, r : r + have, :]
+            if have < 128:
+                piece = jnp.concatenate([piece, jnp.full((128 - have, cells), -100.0, f32)], axis=0)
+            pos[d, :, r : r + 128] = jnp.transpose(piece)
     links = nt_dot(st[...], st[...])
     rows = lax.broadcasted_iota(i32, (nv, nv), 0)
     cols = lax.broadcasted_iota(i32, (nv, nv), 1)
     springs = jnp.where(rows == cols, -2.0 * links, links)
-    s_hi, s_lo = split(springs)
-    s_hi, s_lo = s_hi.astype(bf16), s_lo.astype(bf16)
+    s_hi = springs.astype(bf16)
+    s_lo = (springs - s_hi.astype(f32)).astype(bf16)
     for d in range(3):
-        x_hi, x_lo = split(pos[d])
-        x_hi, x_lo = x_hi.astype(bf16), x_lo.astype(bf16)
-        total = (
+        x = pos[d]
+        x_hi = x.astype(bf16)
+        x_lo = (x - x_hi.astype(f32)).astype(bf16)
+        force[d] = (
             jnp.dot(x_hi, s_hi, preferred_element_type=f32)
             + jnp.dot(x_lo, s_hi, preferred_element_type=f32)
             + jnp.dot(x_hi, s_lo, preferred_element_type=f32)
         )
-        force[d] = total * stiff[...]
-    out[:, 0:3072] = jnp.zeros((out.shape[0], 3072), f32)
-    out[:, 3072:3200] = jnp.full((out.shape[0], 128), -1.0, f32)
+    sub = lax.broadcasted_iota(i32, (8, 128), 0)
+    lane = lax.broadcasted_iota(i32, (8, 128), 1)
+    slots = out.shape[0]
+    tail_row = jnp.full((8, 128), -1.0, f32)
+    table_row = jnp.zeros((8, 128), f32)
+    for f in range(4):
+        one_face = jnp.concatenate([near[f : f + 1, :].astype(f32), jnp.zeros((1, 96), f32)], axis=1)
+        one_face = jnp.broadcast_to(one_face, (8, 128))
+        table_row = jnp.where(lane // 32 == f, pltpu.roll(one_face, 32 * f, 1) if f else one_face, table_row)
+    out[:, 0:3072] = jnp.zeros((slots, 3072), f32)
 
     def clear(t, carry):
-        count[t] = 0
+        base = pl.ds(pl.multiple_of(t * 8, 8), 8)
+        out[base, 3072:3200] = tail_row
+        out[base, 3200:3328] = table_row
+        for m in range(8):
+            count[t * 8 + m] = 0
         return carry
 
-    lax.fori_loop(0, out.shape[0], clear, 0)
+    lax.fori_loop(0, slots // 8, clear, 0)
     sub8 = lax.broadcasted_iota(i32, (8, nv), 0)
     g_even = (2 * (sub8 % 4)).astype(f32)
     g_odd = g_even + 1.0
     g_all = sub8.astype(f32)
     first4 = sub8 < 4
-    lane8 = lax.broadcasted_iota(i32, (8, 128), 1)
-    sub = lax.broadcasted_iota(i32, (8, 128), 0)
-
-    def one(c):
+
+    def one(c, m):
         x = jnp.broadcast_to(pos[0, pl.ds(c, 1), :], (8, nv))
         y = jnp.broadcast_to(pos[1, pl.ds(c, 1), :], (8, nv))
         z = jnp.broadcast_to(pos[2, pl.ds(c, 1), :], (8, nv))
@@ -93,18 +112,21 @@
         left = jnp.concatenate(
             [h_even * f01, jnp.where(first4, h_even, h_odd) * f2, h_odd * f01], axis=0
         )
-        l_hi, l_lo = split(left)
-        left2 = jnp.concatenate([l_hi, l_lo], axis=0).astype(bf16)
+        l_lo = left - left.astype(bf16).astype(f32)
+        left2 = jnp.concatenate([left, l_lo], axis=0).astype(bf16)
+        hats[m] = hat(y, g_all)
         hz = hat(z, g_all)
-        plane = jnp.concatenate([hat(y, float(j)) * hz for j in range(8)], axis=0)
-        p_hi, p_lo = split(plane)
-        plane2 = jnp.concatenate([p_hi, p_lo], axis=0).astype(bf16)
-        prod = nt_dot(left2, plane2)
+        plane = jnp.concatenate(
+            [jnp.broadcast_to(hats[m, j : j + 1, :], (8, nv)) * hz for j in range(8)], axis=0
+        )
+        p_hi = plane.astype(bf16)
+        p_lo = (plane - p_hi.astype(f32)).astype(bf16)
+        prod = nt_dot(left2, jnp.concatenate([p_hi, p_lo], axis=0))
         both = prod[0:24] + prod[24:48]
-        res = both + pltpu.roll(both, 64, 1)
-        main = jnp.where(lane8 < 64, res[0:8], res[16:24])
+        res = (both + pltpu.roll(both, 64, 1)) * stiff[c]
+        main = jnp.where(lane < 64, res[0:8], res[16:24])
         mid = res[8:16]
-        tail = jnp.where(lane8 < 64, mid, pltpu.roll(mid, 4, 0))
+        tail = jnp.where(lane < 64, mid, pltpu.roll(mid, 4, 0))
         t = owner[c]
         r = count[t]
         count[t] = r + 1
@@ -115,46 +137,89 @@
             at = pl.multiple_of(r * 1536 + 128 * k, 128)
             pltpu.store(out.at[pl.ds(base, 8), pl.ds(at, 128)], jnp.broadcast_to(row, (8, 128)), mask=mine)
         label = jnp.full((8, 128), block[c].astype(f32))
-        pltpu.store(out.at[pl.ds(base, 8), 3072:3200], label, mask=mine & (lane8 == r))
+        pltpu.store(out.at[pl.ds(base, 8), 3072:3200], label, mask=mine & (lane == r))
 
     def step(n, carry):
-        for m in range(4):
-            one(n * 4 + m)
+        for m in range(16):
+            one(n * 16 + m, m)
         return carry
 
-    lax.fori_loop(0, cells // 4, step, 0)
-
-
-def spread(owner, block, positions, stiffness, triangles, devices):
+    lax.fori_loop(0, cells // 16, step, 0)
+
+
+def spread(owner, block, positions, stiffness, triangles, neighbours, devices):
     cells, _, verts = positions.shape
     nv = -(-verts // 256) * 256
-    pos = jnp.pad(
-        jnp.transpose(positions, (1, 0, 2)), ((0, 0), (0, 0), (0, nv - verts)), constant_values=-100.0
-    )
-    tri = jnp.transpose(triangles)
-    smem = pl.BlockSpec(memory_space=pltpu.SMEM)
+    inputs = (owner, block, stiffness, jnp.transpose(positions, (1, 2, 0)), jnp.transpose(triangles), jnp.transpose(neighbours))
+    hbm = pl.BlockSpec(memory_space=pltpu.HBM)
     vmem = pl.BlockSpec(memory_space=pltpu.VMEM)
     return pl.pallas_call(
         spread_kernel,
-        out_shape=jax.ShapeDtypeStruct((devices, 3200), f32),
-        in_specs=[smem, smem, vmem, vmem, vmem],
+        out_shape=jax.ShapeDtypeStruct((devices, WIDE), f32),
+        in_specs=[hbm] * 6,
         out_specs=vmem,
         scratch_shapes=[
+            pltpu.SMEM((cells,), i32),
+            pltpu.SMEM((cells,), i32),
+            pltpu.SMEM((cells,), f32),
+            pltpu.VMEM((3, verts, cells), f32),
+            pltpu.VMEM((3, triangles.shape[0]), i32),
+            pltpu.VMEM((6, 32), i32),
+            pltpu.SemaphoreType.DMA((6,)),
             pltpu.VMEM((nv, triangles.shape[0]), bf16),
             pltpu.VMEM((3, cells, nv), f32),
+            pltpu.VMEM((3, cells, nv), f32),
+            pltpu.VMEM((16, 8, nv), f32),
             pltpu.SMEM((devices,), i32),
         ],
         compiler_params=pltpu.CompilerParams(vmem_limit_bytes=48 << 20),
         name="spread",
-    )(owner, block, pos, stiffness[:, None], tri)
+    )(*[pltpu.with_memory_space_constraint(x, pltpu.HBM) for x in inputs])
 
 
 def lane_take(x, index):
     return jnp.take_along_axis(x, index, axis=1)
 
 
-def collide_kernel(got, pops, post, table, body):
+def find(n_gx, n_gy, me_x, me_y, near, got, square):
+    square[...] = jnp.full((128, 128), -1.0, f32)
+    square[0:6, 0:32] = near[...].astype(f32)
+    ids = jnp.transpose(square[...])[0:32]
+    known = got[:, 3200:3328]
+    k_hi = known.astype(bf16)
+    k_lo = (known - k_hi.astype(f32)).astype(bf16)
+    lane = lax.broadcasted_iota(i32, (32, 128), 1)
+    hop = ids.astype(i32)
+    for f1 in range(2, 6):
+        first = jnp.broadcast_to(ids[:, f1 : f1 + 1], (32, 128)).astype(i32)
+        safe = jnp.maximum(first, 0)
+        owner = lax.shift_right_logical(safe, 5)
+        pick = (owner == lane).astype(f32).astype(bf16)
+        rows = jnp.dot(pick, k_hi, preferred_element_type=f32) + jnp.dot(pick, k_lo, preferred_element_type=f32)
+        for n, q in enumerate(EDGE_Q):
+            d1, d2 = [d for d in range(3) if vel[q][d]]
+            if f1 == 2 * d2 + (0 if vel[q][d2] == 1 else 1):
+                f2 = 2 * d1 + (0 if vel[q][d1] == 1 else 1)
+                second = jnp.take_along_axis(rows, f2 * 32 + lax.bitwise_and(safe, 31), axis=1)
+                second = jnp.where(first >= 0, second.astype(i32), -1)
+                hop = jnp.where(lane == 6 + n, second, hop)
+    safe = jnp.maximum(hop, 0)
+    owner = lax.shift_right_logical(safe, 5)
+    slot = lax.bitwise_and(safe, 31)
+    reach = jnp.where(lane < 6, 1, 2)
+    x = lax.rem(lax.div(owner, n_gy) - me_x + reach + n_gx, n_gx)
+    y = lax.rem(lax.rem(owner, n_gy) - me_y + reach + n_gy, n_gy)
+    column = jnp.where(x == 0, 48, jnp.where(x == 4, 49, (x - 1) * 16 + EDGE_TILE))
+    edge = jnp.where(y == 0, 150 + x, jnp.where(y == 4, 155 + x, (y - 1) * 50 + column))
+    tile = jnp.where(lane < 6, y * 50 + x * 16, edge)
+    return jnp.where(hop >= 0, tile * 32 + slot, NOWHERE)
+
+
+def collide_kernel(sizes, near, got, pops, post, table, where_, body, square):
     slots = got.shape[0]
+    n_gx, n_gy = sizes
+    me_x, me_y = lax.axis_index("gx"), lax.axis_index("gy")
+    where_[...] = find(n_gx, n_gy, me_x, me_y, near, got, square)
     lane = lax.broadcasted_iota(i32, (slots, 128), 1)
     ids = got[:, 3072:3200]
     picks = []
@@ -166,11 +231,11 @@
         total = jnp.zeros((32, 512), f32)
         for r in range(2):
             part = got[:, r * 1536 + n * 512 : r * 1536 + (n + 1) * 512]
-            hi, lo = split(part)
-            total = total + jnp.dot(picks[r], hi.astype(bf16), preferred_element_type=f32)
-            total = total + jnp.dot(picks[r], lo.astype(bf16), preferred_element_type=f32)
+            hi = part.astype(bf16)
+            lo = (part - hi.astype(f32)).astype(bf16)
+            total = total + jnp.dot(picks[r], hi, preferred_element_type=f32)
+            total = total + jnp.dot(picks[r], lo, preferred_element_type=f32)
         body[n] = total
-
     lanes = lax.broadcasted_iota(i32, (8, 128), 1)
     low = lanes < 64
     keep = 1.0 - 1.0 / relax_time
@@ -180,7 +245,7 @@
         rows = pl.ds(pl.multiple_of(g * 8, 8), 8)
         for a in range(4):
             cut = slice(128 * a, 128 * (a + 1))
-            f = [pops[rows, q, cut] * wts[q] for q in range(19)]
+            f = [pops[q, rows, cut] * wts[q] for q in range(19)]
             force = [body[d, rows, cut] for d in range(3)]
             rho = f[0]
             for q in range(1, 19):
@@ -251,41 +316,51 @@
     lax.fori_loop(0, 4, group, 0)
 
 
-def collide(got, populations):
+def collide(got, populations, neighbours):
     vmem = pl.BlockSpec(memory_space=pltpu.VMEM)
+    sizes = (lax.axis_size("gx"), lax.axis_size("gy"))
     return pl.pallas_call(
-        collide_kernel,
-        out_shape=(jax.ShapeDtypeStruct((19, 32, 512), f32), jax.ShapeDtypeStruct((NT, 32, 128), f32)),
-        in_specs=[vmem, vmem],
-        out_specs=(vmem, vmem),
-        scratch_shapes=[pltpu.VMEM((3, 32, 512), f32)],
+        functools.partial(collide_kernel, sizes),
+        out_shape=(
+            jax.ShapeDtypeStruct((19, 32, 512), f32),
+            jax.ShapeDtypeStruct((NT, 32, 128), f32),
+            jax.ShapeDtypeStruct((32, 128), i32),
+        ),
+        in_specs=[vmem, vmem, vmem],
+        out_specs=(vmem, vmem, vmem),
+        scratch_shapes=[
+            pltpu.VMEM((3, 32, 512), f32),
+            pltpu.VMEM((128, 128), f32),
+        ],
         compiler_params=pltpu.CompilerParams(vmem_limit_bytes=48 << 20),
         name="collide",
-    )(got, populations)
-
-
-def stream_kernel(where_face, where_edge, post, there, mid, down, up, down2, up2, out, table, ghost, sem):
+    )(jnp.transpose(neighbours), got, jnp.transpose(populations, (1, 0, 2)))
+
+
+def stream_kernel(where_in, post, mid, down, up, down2, up2, out, table, ghost, where_, sem):
     parts = [(mid, 50, 50), (down, 0, 50), (up, 100, 50), (down2, 150, 5), (up2, 155, 5)]
-    copies = [
-        pltpu.make_async_copy(ref, table.at[pl.ds(at, size)], sem.at[n]) for n, (ref, at, size) in enumerate(parts)
+    copies = [pltpu.make_async_copy(where_in, where_, sem.at[5])] + [
+        pltpu.make_async_copy(ref, table.at[pl.ds(at * 32, size * 32)], sem.at[n])
+        for n, (ref, at, size) in enumerate(parts)
     ]
     for c in copies:
         c.start()
+    table[NOWHERE:, :] = jnp.full((NT * 32, 128), jnp.nan, f32)
     for c in copies:
         c.wait()
     lanes = lax.broadcasted_iota(i32, (8, 128), 1)
     sub = lax.broadcasted_iota(i32, (8, 128), 0)
 
     def row_of(at, tile):
-        return table[at // 32 + tile, pl.ds(at % 32, 8, stride=0), :]
+        return table[pl.ds(at + 32 * tile, 8, stride=0), :]
 
     def fetch(g, carry):
         rows = pl.ds(pl.multiple_of(g * 8, 8), 8)
         for ax in range(3):
             made = [jnp.zeros((8, 128), f32)] * 5
             for i in range(8):
-                low_at = where_face[(g * 8 + i) * 6 + 2 * ax]
-                high_at = where_face[(g * 8 + i) * 6 + 2 * ax + 1]
+                low_at = where_[g * 8 + i, 2 * ax]
+                high_at = where_[g * 8 + i, 2 * ax + 1]
                 for n in range(5):
                     t = 5 * ax + n
                     both = jnp.where(lanes < 64, row_of(high_at, t), row_of(low_at, t))
@@ -295,7 +370,7 @@
         line = jnp.zeros((8, 128), f32)
         for i in range(8):
             for n in range(12):
-                at = where_edge[(g * 8 + i) * 12 + n]
+                at = where_[g * 8 + i, 6 + n]
                 line = jnp.where((lanes // 8 == n) & (sub == i), row_of(at, 0), line)
         ghost[EDGE_TILE, rows, :] = line
         return carry
@@ -306,15 +381,8 @@
 
     def group(g, carry):
         rows = pl.ds(pl.multiple_of(g * 8, 8), 8)
-        flags = there[rows, :]
-
-        def flag(n):
-            return jnp.broadcast_to(flags[:, n : n + 1], (8, 128)) > 0.5
-
-        face_on = [flag(n) for n in range(6)]
-        edge_on = [flag(6 + n) for n in range(12)]
         edges = ghost[EDGE_TILE, rows, :]
-        out[rows, 0, :] = post[0, rows, :]
+        out[0, rows, :] = post[0, rows, :]
         for q in range(1, 19):
             e = vel[q]
             ex, ey, ez = e
@@ -339,7 +407,6 @@
                         out_of = out_of | crossing[d]
                     val = jnp.where(out_of, back, val)
                 for d in axes:
-                    face = 2 * d + (0 if e[d] == 1 else 1)
                     n = (POS[d] if e[d] == 1 else NEG[d]).index(q)
                     source = ghost[5 * d + n, rows, :]
                     base = 64 if e[d] == 1 else 0
@@ -349,7 +416,7 @@
                         brought = lane_take(source, base + ((ii - ex) * 8 + kk - ez) % 64)
                     else:
                         brought = lane_take(source, base + ((ii - ex) * 8 + jj - ey) % 64)
-                    use = crossing[d] & face_on[face]
+                    use = crossing[d] & (brought == brought)
                     for other in axes:
                         if other != d:
                             use = use & ~crossing[other]
@@ -358,71 +425,35 @@
                     n = q - 7
                     along = kk if ez == 0 else (jj if ey == 0 else ii)
                     brought = lane_take(edges, 8 * n + along)
-                    val = jnp.where(crossing[axes[0]] & crossing[axes[1]] & edge_on[n], brought, val)
-                out[rows, q, 128 * a : 128 * (a + 1)] = val
+                    val = jnp.where(crossing[axes[0]] & crossing[axes[1]] & (brought == brought), brought, val)
+                out[q, rows, 128 * a : 128 * (a + 1)] = val
         return carry
 
     lax.fori_loop(0, 4, group, 0)
 
 
-def stream(where_face, where_edge, post, there, mid, down, up, down2, up2):
-    smem = pl.BlockSpec(memory_space=pltpu.SMEM)
+def stream(where_, post, *parts):
     vmem = pl.BlockSpec(memory_space=pltpu.VMEM)
-    hbm = pl.BlockSpec(memory_space=pl.ANY)
+    anywhere = pl.BlockSpec(memory_space=pl.ANY)
     return pl.pallas_call(
         stream_kernel,
-        out_shape=jax.ShapeDtypeStruct((32, 19, 512), f32),
-        in_specs=[smem, smem, vmem, vmem] + [hbm] * 5,
+        out_shape=jax.ShapeDtypeStruct((19, 32, 512), f32),
+        in_specs=[anywhere, vmem] + [anywhere] * 5,
         out_specs=vmem,
         scratch_shapes=[
-            pltpu.VMEM((160, 32, 128), f32),
+            pltpu.VMEM(((160 + NT) * 32, 128), f32),
             pltpu.VMEM((NT, 32, 128), f32),
-            pltpu.SemaphoreType.DMA((5,)),
+            pltpu.SMEM((32, 128), i32),
+            pltpu.SemaphoreType.DMA((6,)),
         ],
         compiler_params=pltpu.CompilerParams(vmem_limit_bytes=48 << 20),
         name="stream",
-    )(where_face, where_edge, post, there, mid, down, up, down2, up2)
+    )(where_, post, *[p.reshape(-1, 128) for p in parts])
 
 
 def send(array, axis, step):
     size = lax.axis_size(axis)
     return lax.ppermute(array, axis, [(i, (i + step) % size) for i in range(size)])
-
-
-def look_up(neighbours):
-    rows_gx, rows_gy = lax.axis_size("gx"), lax.axis_size("gy")
-    me_x, me_y = lax.axis_index("gx"), lax.axis_index("gy")
-    column = jnp.concatenate([send(neighbours, "gx", 1), neighbours, send(neighbours, "gx", -1)], axis=0)
-    near = jnp.concatenate([send(column, "gy", 1), column, send(column, "gy", -1)], axis=0)
-
-    def place(ids, reach):
-        safe = jnp.maximum(ids, 0)
-        owner = safe // 32
-        x = (owner // rows_gy - me_x + reach) % rows_gx
-        y = (owner % rows_gy - me_y + reach) % rows_gy
-        return x, y, safe % 32
-
-    x, y, slot = place(neighbours, 1)
-    on_face = neighbours >= 0
-    where_face = jnp.where(on_face, (y * 50 + x * 16) * 32 + slot, 0)
-    near_row = (y * 3 + x) * 32 + slot
-    second = jnp.take(near, jnp.where(on_face, near_row, 0)[:, 2:6].reshape(-1), axis=0).reshape(32, 4, 6)
-    two = []
-    for q in EDGE_Q:
-        e = vel[q]
-        axes = [d for d in range(3) if e[d]]
-        f1 = 2 * axes[1] + (0 if e[axes[1]] == 1 else 1)
-        f2 = 2 * axes[0] + (0 if e[axes[0]] == 1 else 1)
-        two.append(jnp.where(on_face[:, f1], second[:, f1 - 2, f2], -1))
-    two = jnp.stack(two, axis=1)
-    x, y, slot = place(two, 2)
-    on_edge = two >= 0
-    inner = (y - 1) * 50 + jnp.where(x == 0, 48, jnp.where(x == 4, 49, (x - 1) * 16 + EDGE_TILE))
-    tile = jnp.where(y == 0, 150 + x, jnp.where(y == 4, 155 + x, inner))
-    where_edge = jnp.where(on_edge, tile * 32 + slot, 0)
-    there = jnp.concatenate([on_face, on_edge], axis=1).astype(f32)
-    there = jnp.pad(there, ((0, 0), (0, 128 - 18)))
-    return where_face.reshape(-1), where_edge.reshape(-1), there
 
 
 def exchange(table):
@@ -436,11 +467,11 @@
 
 def body(populations, neighbours, positions, stiffness, cell_owner, cell_block, triangles):
     devices = lax.axis_size("gx") * lax.axis_size("gy")
-    where_face, where_edge, there = look_up(neighbours)
-    slots = spread(cell_owner[:, 0], cell_block, positions, stiffness, triangles, devices)
+    slots = spread(cell_owner[:, 0], cell_block, positions, stiffness, triangles, neighbours, devices)
     got = lax.all_to_all(slots, BOTH, split_axis=0, concat_axis=0, tiled=True)
-    post, table = collide(got, populations)
-    return stream(where_face, where_edge, post, there, *exchange(table))
+    post, table, where_ = collide(got, populations, neighbours)
+    result = stream(where_, post, *exchange(table))
+    return jnp.transpose(result, (1, 0, 2))
 
 
 def solution(mesh):

time: 117 us -> 92 us (0.79)
  blocking collectives: 0 us -> 37.4 us
  starting transfers between devices: 35.9 us -> 13 us
  waiting for transfers between devices: 31.2 us -> 14.9 us
  Pallas kernels: 35.6 us -> 23.3 us
  local copies, waits for them, and re-layouts: 12.9 us -> 3.12 us
    all_to_all x0 -> x1, blocking collectives: none -> 37.4 us  [body(): got = lax.all_to_all(slots, BOTH, split_axis=0, concat_axis=0, tiled=True)]
    ppermute x12 -> x8, waiting for transfers between devices: 31.2 us -> 14.9 us  [send(): lax.ppermute(array, axis, [(i, (i + step) % size) for i in range(size)])]
    pallas_call x3, Pallas kernels: 35.6 us -> 23.3 us  [the longest x1 16.3 us: spread(): pl.pallas_call(spread_kernel, out_shape=jax.ShapeDtypeStruct((devices, WI...]
    all_to_all x1 -> x0, starting transfers between devices: 11.9 us -> none  [body(): got = lax.all_to_all(slots, BOTH, split_axis=0, concat_axis=0, tiled=True)]
    ppermute x12 -> x8, starting transfers between devices: 24 us -> 13 us  [send(): lax.ppermute(array, axis, [(i, (i + step) % size) for i in range(size)])]
    unnamed x21 -> x12, local copies, waits for them, and re-layouts: 4.62 us -> 1.36 us
    pallas_call x1 -> x0, local copies, waits for them, and re-layouts: 1.76 us -> none  [stream(): pl.pallas_call(stream_kernel, out_shape=jax.ShapeDtypeStruct((32, 19, 512...]
  transfers between devices with their start and end apart: 13 -> 8, of which waited for: 6 -> 4; matrix products, arithmetic and copies ran while one was open for 4% -> 0% of each run, Pallas kernels for 0% -> 0%
where the time goes in v1:
time: 92 us; the launch traced here: 91.8 us
  blocking collectives  37.4 us (41%)
  Pallas kernels  23.3 us (25%)
  waiting for transfers between devices  14.9 us (16%)
  starting transfers between devices  13 us (14%)
  local copies, waits for them, and re-layouts  3.12 us (3%)
    all_to_all x1, blocking collectives, body(): got = lax.all_to_all(slots, BOTH, split_axis=0, concat_axis=0, tiled=True)  37.4 us
    pallas_call x1, Pallas kernels, spread(): pl.pallas_call(spread_kernel, out_shape=jax.ShapeDtypeStruct((devices, WI...  16.3 us
    ppermute x8, waiting for transfers between devices, send(): lax.ppermute(array, axis, [(i, (i + step) % size) for i in range(size)])  14.9 us
    ppermute x8, starting transfers between devices, send(): lax.ppermute(array, axis, [(i, (i + step) % size) for i in range(size)])  13 us
    pallas_call x1, Pallas kernels, stream(): pl.pallas_call(stream_kernel, out_shape=jax.ShapeDtypeStruct((19, 32, 512...  4.73 us
    pallas_call x1, Pallas kernels, collide(): pl.pallas_call(functools.partial(collide_kernel, sizes), out_shape=(jax.S...  2.24 us
  transfers between devices with their start and end apart: 8, of which 4 were waited for; matrix products, arithmetic and copies ran while one was open for 0% of the time, Pallas kernels for 0%

profile of v1, /device:TPU:1, one launch (start us, length us, event | category | flops | bytes accessed | tf_op | source)
XLA Modules:
  0.0 91.8 jit_solution(9872213894048190561)
XLA Ops:
  0.0 16.3 %spread.1 = f32[128,3328]{1,0:T(8,128)S(1)} custom-call(s32[128]{0:T(128)} %bitcast.27, s32[128]{0:T(128)} %block_in.1, f32[128]{0:T(128)} %stiff_in.1, f32[3,642,128]{2,1,0:T(8,128)} %bitcast.25, s32[3,1280]{1,0:T(4,128)} %bitcast.26, s32[6,32]{1,0:T(8,128)} %bitcast.23), custom_call_target="tpu_custom_call" | custom-call | tf_op jit(solution)/shard_map/spread/pallas_call | solution.py:156
  16.3 1.8 %copy.8 = f32[128,1,3328]{2,1,0:T(1,128)S(1)} copy(f32[128,1,3328]{2,0,1:T(8,128)S(1)} %bitcast.16) | data formatting | bytes 3407872 | tf_op jit(solution)/shard_map/all_to_all | solution.py:471
  18.1 37.4 %all_to_all.11 = f32[128,1,3328]{2,1,0:T(1,128)S(1)} all-to-all(f32[128,1,3328]{2,1,0:T(1,128)S(1)} %copy.8), channel_id=1, replica_groups=mesh['gx'=16,'gy'=8] {'gx','gy'}, dimensions={0} | all-to-all | bytes 3407872 | tf_op jit(solution)/shard_map/all_to_all | solution.py:471
  55.5 0.0 copy-start
  55.5 0.0 copy-start.1
  55.5 0.1 copy.11
  55.6 1.2 %copy-done = f32[32,19,512]{2,0,1:T(8,128)S(1)} copy-done((f32[32,19,512]{2,0,1:T(8,128)S(1)}, f32[32,19,512]{2,0,1:T(8,128)}, u32[]{:S(2)}) %copy-start) | copy-done | bytes 1245208
  56.8 0.0 copy-done.1
  56.8 2.2 %collide.1 = (f32[19,32,512]{2,1,0:T(8,128)S(1)}, f32[16,32,128]{2,1,0:T(8,128)S(1)}, s32[32,128]{1,0:T(8,128)S(1)}) custom-call(s32[6,32]{1,0:T(8,128)S(1)} %bitcast.24, f32[128,3328]{1,0:T(8,128)S(1)} %bitcast.15, f32[19,32,512]{2,1,0:T(8,128)S(1)} %bitcast.18), custom_call_target="tpu_custom_call" | custom-call | tf_op jit(solution)/shard_map/collide/pallas_call | solution.py:322
  59.0 0.3 collective-permute-start
  59.4 4.5 %collective-permute-start.1 = (f32[16,32,128]{2,1,0:T(8,128)S(1)}, f32[16,32,128]{2,1,0:T(8,128)S(1)}, u32[]{:S(2)}, u32[]{:S(2)}) collective-permute-start(f32[16,32,128]{2,1,0:T(8,128)S(1)} %get-tuple-element.10), channel_id=1, source_target_pairs={{0,120},{8,0},{16,8},{24,16},{32,24},{40,32},{48,40},{56,48},{64,5... | collective-permute-start | bytes 786440 | tf_op jit(solution)/shard_map/ppermute | solution.py:456
  63.9 0.0 collective-permute-start.3
  63.9 3.0 %collective-permute-start.2 = (f32[1,32,128]{2,1,0:T(8,128)S(1)}, f32[1,32,128]{2,1,0:T(8,128)S(1)}, u32[]{:S(2)}, u32[]{:S(2)}) collective-permute-start(f32[1,32,128]{2,1,0:T(8,128)S(1)} %slice.9), channel_id=1, source_target_pairs={{0,16},{8,24},{16,32},{24,40},{32,48},{40,56},{48,64},{56,72},{64,... | collective-permute-start | bytes 49160 | tf_op jit(solution)/shard_map/ppermute | solution.py:456
  66.9 2.2 %collective-permute-done = f32[16,32,128]{2,1,0:T(8,128)S(1)} collective-permute-done((f32[16,32,128]{2,1,0:T(8,128)S(1)}, f32[16,32,128]{2,1,0:T(8,128)S(1)}, u32[]{:S(2)}, u32[]{:S(2)}) %collective-permute-start) | collective-permute-done | bytes 262176 | tf_op jit(solution)/shard_map/ppermute | solution.py:456
  69.1 0.0 collective-permute-done.1
  69.2 1.3 %collective-permute-done.2 = f32[1,32,128]{2,1,0:T(8,128)S(1)} collective-permute-done((f32[1,32,128]{2,1,0:T(8,128)S(1)}, f32[1,32,128]{2,1,0:T(8,128)S(1)}, u32[]{:S(2)}, u32[]{:S(2)}) %collective-permute-start.2) | collective-permute-done | bytes 16416 | tf_op jit(solution)/shard_map/ppermute | solution.py:456
  70.5 0.0 collective-permute-done.3
  70.5 2.6 %collective-permute-start.5 = (f32[50,32,128]{2,1,0:T(8,128)S(1)}, f32[50,32,128]{2,1,0:T(8,128)S(1)}, u32[]{:S(2)}, u32[]{:S(2)}) collective-permute-start(f32[50,32,128]{2,1,0:T(8,128)S(1)} %get-tuple-element.12), channel_id=1, source_target_pairs={{0,7},{1,0},{2,1},{3,2},{4,3},{5,4},{6,5},{7,6},{8,15},{9,8},{10,9... | collective-permute-start | bytes 2457608 | tf_op jit(solution)/shard_map/ppermute | solution.py:456
  73.0 0.0 collective-permute-start.4
  73.1 2.5 %collective-permute-start.7 = (f32[5,32,128]{2,1,0:T(8,128)S(1)}, f32[5,32,128]{2,1,0:T(8,128)S(1)}, u32[]{:S(2)}, u32[]{:S(2)}) collective-permute-start(f32[5,32,128]{2,1,0:T(8,128)S(1)} %get-tuple-element.11), channel_id=1, source_target_pairs={{0,6},{1,7},{2,0},{3,1},{4,2},{5,3},{6,4},{7,5},{8,14},{9,15},{10,... | collective-permute-start | bytes 245768 | tf_op jit(solution)/shard_map/ppermute | solution.py:456
  75.6 0.0 collective-permute-start.6
  75.6 2.3 %collective-permute-done.7 = f32[5,32,128]{2,1,0:T(8,128)S(1)} collective-permute-done((f32[5,32,128]{2,1,0:T(8,128)S(1)}, f32[5,32,128]{2,1,0:T(8,128)S(1)}, u32[]{:S(2)}, u32[]{:S(2)}) %collective-permute-start.7) | collective-permute-done | bytes 81952 | tf_op jit(solution)/shard_map/ppermute | solution.py:456
  78.0 9.2 %collective-permute-done.6 = f32[5,32,128]{2,1,0:T(8,128)S(1)} collective-permute-done((f32[5,32,128]{2,1,0:T(8,128)S(1)}, f32[5,32,128]{2,1,0:T(8,128)S(1)}, u32[]{:S(2)}, u32[]{:S(2)}) %collective-permute-start.6) | collective-permute-done | bytes 81952 | tf_op jit(solution)/shard_map/ppermute | solution.py:456
  87.1 0.0 collective-permute-done.5
  87.1 0.0 collective-permute-done.4
  87.1 4.7 %stream.1 = f32[19,32,512]{2,1,0:T(8,128)} custom-call(s32[32,128]{1,0:T(8,128)S(1)} %get-tuple-element.8.where_in, f32[19,32,512]{2,1,0:T(8,128)S(1)} %get-tuple-element.9.post, f32[1600,128]{1,0:T(8,128)S(1)} %bitcast.17, f32[1600,128]{1,0:T(8,128)S(1)} %bitcast.20, f32[1600,128]{1,0:T(8,128)S(1)} %bitcast.19, f32[160,128]{1,0:T(8,128)S(1)} %bitcast.22, ...), custom_call_target="tpu_custom_call" | custom-call | tf_op jit(solution)/shard_map/stream/pallas_call | solution.py:438
  (9 shorter events, 0.1 us)
Async XLA Ops:
  55.5 1.3 %copy-start = (f32[32,19,512]{2,0,1:T(8,128)S(1)}, f32[32,19,512]{2,0,1:T(8,128)}, u32[]{:S(2)}) copy-start(f32[32,19,512]{2,0,1:T(8,128)} %param.7) | copy-start | bytes 3735556
  55.5 1.3 %copy-start.1 = (s32[32,6]{0,1:T(8,128)S(1)}, s32[32,6]{0,1:T(8,128)}, u32[]{:S(2)}) copy-start(s32[32,6]{0,1:T(8,128)} %param.8) | copy-start | bytes 2308
  59.0 10.0 %collective-permute-start = (f32[16,32,128]{2,1,0:T(8,128)S(1)}, f32[16,32,128]{2,1,0:T(8,128)S(1)}, u32[]{:S(2)}, u32[]{:S(2)}) collective-permute-start(f32[16,32,128]{2,1,0:T(8,128)S(1)} %get-tuple-element.10), channel_id=1, source_target_pairs={{0,8},{8,16},{16,24},{24,32},{32,40},{40,48},{48,56},{56,64},{64,7... | collective-permute-start | bytes 786440 | tf_op jit(solution)/shard_map/ppermute | solution.py:456
  59.4 9.8 %collective-permute-start.1 = (f32[16,32,128]{2,1,0:T(8,128)S(1)}, f32[16,32,128]{2,1,0:T(8,128)S(1)}, u32[]{:S(2)}, u32[]{:S(2)}) collective-permute-start(f32[16,32,128]{2,1,0:T(8,128)S(1)} %get-tuple-element.10), channel_id=1, source_target_pairs={{0,120},{8,0},{16,8},{24,16},{32,24},{40,32},{48,40},{56,48},{64,5... | collective-permute-start | bytes 786440 | tf_op jit(solution)/shard_map/ppermute | solution.py:456
  63.9 6.5 %collective-permute-start.3 = (f32[1,32,128]{2,1,0:T(8,128)S(1)}, f32[1,32,128]{2,1,0:T(8,128)S(1)}, u32[]{:S(2)}, u32[]{:S(2)}) collective-permute-start(f32[1,32,128]{2,1,0:T(8,128)S(1)} %slice.9), channel_id=1, source_target_pairs={{0,112},{8,120},{16,0},{24,8},{32,16},{40,24},{48,32},{56,40},{64,... | collective-permute-start | bytes 49160 | tf_op jit(solution)/shard_map/ppermute | solution.py:456
  63.9 6.5 %collective-permute-start.2 = (f32[1,32,128]{2,1,0:T(8,128)S(1)}, f32[1,32,128]{2,1,0:T(8,128)S(1)}, u32[]{:S(2)}, u32[]{:S(2)}) collective-permute-start(f32[1,32,128]{2,1,0:T(8,128)S(1)} %slice.9), channel_id=1, source_target_pairs={{0,16},{8,24},{16,32},{24,40},{32,48},{40,56},{48,64},{56,72},{64,... | collective-permute-start | bytes 49160 | tf_op jit(solution)/shard_map/ppermute | solution.py:456
  70.5 16.6 %collective-permute-start.5 = (f32[50,32,128]{2,1,0:T(8,128)S(1)}, f32[50,32,128]{2,1,0:T(8,128)S(1)}, u32[]{:S(2)}, u32[]{:S(2)}) collective-permute-start(f32[50,32,128]{2,1,0:T(8,128)S(1)} %get-tuple-element.12), channel_id=1, source_target_pairs={{0,7},{1,0},{2,1},{3,2},{4,3},{5,4},{6,5},{7,6},{8,15},{9,8},{10,9... | collective-permute-start | bytes 2457608 | tf_op jit(solution)/shard_map/ppermute | solution.py:456
  73.0 14.1 %collective-permute-start.4 = (f32[50,32,128]{2,1,0:T(8,128)S(1)}, f32[50,32,128]{2,1,0:T(8,128)S(1)}, u32[]{:S(2)}, u32[]{:S(2)}) collective-permute-start(f32[50,32,128]{2,1,0:T(8,128)S(1)} %get-tuple-element.12), channel_id=1, source_target_pairs={{0,1},{1,2},{2,3},{3,4},{4,5},{5,6},{6,7},{7,0},{8,9},{9,10},{10,1... | collective-permute-start | bytes 2457608 | tf_op jit(solution)/shard_map/ppermute | solution.py:456
  73.1 4.9 %collective-permute-start.7 = (f32[5,32,128]{2,1,0:T(8,128)S(1)}, f32[5,32,128]{2,1,0:T(8,128)S(1)}, u32[]{:S(2)}, u32[]{:S(2)}) collective-permute-start(f32[5,32,128]{2,1,0:T(8,128)S(1)} %get-tuple-element.11), channel_id=1, source_target_pairs={{0,6},{1,7},{2,0},{3,1},{4,2},{5,3},{6,4},{7,5},{8,14},{9,15},{10,... | collective-permute-start | bytes 245768 | tf_op jit(solution)/shard_map/ppermute | solution.py:456
  75.6 11.5 %collective-permute-start.6 = (f32[5,32,128]{2,1,0:T(8,128)S(1)}, f32[5,32,128]{2,1,0:T(8,128)S(1)}, u32[]{:S(2)}, u32[]{:S(2)}) collective-permute-start(f32[5,32,128]{2,1,0:T(8,128)S(1)} %get-tuple-element.11), channel_id=1, source_target_pairs={{0,2},{1,3},{2,4},{3,5},{4,6},{5,7},{6,0},{7,1},{8,10},{9,11},{10,... | collective-permute-start | bytes 245768 | tf_op jit(solution)/shard_map/ppermute | solution.py:456

commit v2 on v1

--- a/solution.py
+++ b/solution.py
@@ -25,7 +25,8 @@
 FACE_TILES = 15
 EDGE_TILE = 15
 NT = 16
-NOWHERE = 160 * 32
+IDS = 96
+HAVE = 114
 WIDE = 3328
 BOTH = ("gx", "gy")
 f32, bf16, i32 = jnp.float32, jnp.bfloat16, jnp.int32
@@ -79,7 +80,7 @@
     tail_row = jnp.full((8, 128), -1.0, f32)
     table_row = jnp.zeros((8, 128), f32)
     for f in range(4):
-        one_face = jnp.concatenate([near[f : f + 1, :].astype(f32), jnp.zeros((1, 96), f32)], axis=1)
+        one_face = jnp.concatenate([near[f + 2 : f + 3, :].astype(f32), jnp.zeros((1, 96), f32)], axis=1)
         one_face = jnp.broadcast_to(one_face, (8, 128))
         table_row = jnp.where(lane // 32 == f, pltpu.roll(one_face, 32 * f, 1) if f else one_face, table_row)
     out[:, 0:3072] = jnp.zeros((slots, 3072), f32)
@@ -181,45 +182,31 @@
     return jnp.take_along_axis(x, index, axis=1)
 
 
-def find(n_gx, n_gy, me_x, me_y, near, got, square):
+def find(near, got, square):
     square[...] = jnp.full((128, 128), -1.0, f32)
     square[0:6, 0:32] = near[...].astype(f32)
-    ids = jnp.transpose(square[...])[0:32]
+    goal = jnp.transpose(square[...])[0:32]
     known = got[:, 3200:3328]
     k_hi = known.astype(bf16)
     k_lo = (known - k_hi.astype(f32)).astype(bf16)
     lane = lax.broadcasted_iota(i32, (32, 128), 1)
-    hop = ids.astype(i32)
-    for f1 in range(2, 6):
-        first = jnp.broadcast_to(ids[:, f1 : f1 + 1], (32, 128)).astype(i32)
+    for f1 in range(4):
+        first = jnp.broadcast_to(goal[:, f1 : f1 + 1], (32, 128)).astype(i32)
         safe = jnp.maximum(first, 0)
-        owner = lax.shift_right_logical(safe, 5)
-        pick = (owner == lane).astype(f32).astype(bf16)
+        pick = (lax.shift_right_logical(safe, 5) == lane).astype(f32).astype(bf16)
         rows = jnp.dot(pick, k_hi, preferred_element_type=f32) + jnp.dot(pick, k_lo, preferred_element_type=f32)
         for n, q in enumerate(EDGE_Q):
             d1, d2 = [d for d in range(3) if vel[q][d]]
-            if f1 == 2 * d2 + (0 if vel[q][d2] == 1 else 1):
-                f2 = 2 * d1 + (0 if vel[q][d1] == 1 else 1)
-                second = jnp.take_along_axis(rows, f2 * 32 + lax.bitwise_and(safe, 31), axis=1)
-                second = jnp.where(first >= 0, second.astype(i32), -1)
-                hop = jnp.where(lane == 6 + n, second, hop)
-    safe = jnp.maximum(hop, 0)
-    owner = lax.shift_right_logical(safe, 5)
-    slot = lax.bitwise_and(safe, 31)
-    reach = jnp.where(lane < 6, 1, 2)
-    x = lax.rem(lax.div(owner, n_gy) - me_x + reach + n_gx, n_gx)
-    y = lax.rem(lax.rem(owner, n_gy) - me_y + reach + n_gy, n_gy)
-    column = jnp.where(x == 0, 48, jnp.where(x == 4, 49, (x - 1) * 16 + EDGE_TILE))
-    edge = jnp.where(y == 0, 150 + x, jnp.where(y == 4, 155 + x, (y - 1) * 50 + column))
-    tile = jnp.where(lane < 6, y * 50 + x * 16, edge)
-    return jnp.where(hop >= 0, tile * 32 + slot, NOWHERE)
-
-
-def collide_kernel(sizes, near, got, pops, post, table, where_, body, square):
+            if f1 == 2 * d1 + (1 if vel[q][d1] == 1 else 0):
+                f2 = 2 * d2 + (1 if vel[q][d2] == 1 else 0)
+                second = jnp.take_along_axis(rows, (f2 - 2) * 32 + lax.bitwise_and(safe, 31), axis=1)
+                goal = jnp.where(lane == 6 + n, jnp.where(first >= 0, second, -1.0), goal)
+    return goal
+
+
+def collide_kernel(near, got, pops, post, table, goal, body, square):
     slots = got.shape[0]
-    n_gx, n_gy = sizes
-    me_x, me_y = lax.axis_index("gx"), lax.axis_index("gy")
-    where_[...] = find(n_gx, n_gy, me_x, me_y, near, got, square)
+    goal[...] = find(near, got, square)
     lane = lax.broadcasted_iota(i32, (slots, 128), 1)
     ids = got[:, 3072:3200]
     picks = []
@@ -293,7 +280,7 @@
                     )
                     picked = val if picked is None else jnp.where(first // 2 == a, val, picked)
                 table[5 * ax + n, rows, :] = picked
-        line = jnp.zeros((8, 128), f32)
+        line = jnp.where(lanes < HAVE, pltpu.roll(goal[rows, :], IDS, 1), 1.0)
         w = lanes % 8
         for n, q in enumerate(EDGE_Q):
             ex, ey, ez = vel[q]
@@ -318,13 +305,12 @@
 
 def collide(got, populations, neighbours):
     vmem = pl.BlockSpec(memory_space=pltpu.VMEM)
-    sizes = (lax.axis_size("gx"), lax.axis_size("gy"))
     return pl.pallas_call(
-        functools.partial(collide_kernel, sizes),
+        collide_kernel,
         out_shape=(
             jax.ShapeDtypeStruct((19, 32, 512), f32),
             jax.ShapeDtypeStruct((NT, 32, 128), f32),
-            jax.ShapeDtypeStruct((32, 128), i32),
+            jax.ShapeDtypeStruct((32, 128), f32),
         ),
         in_specs=[vmem, vmem, vmem],
         out_specs=(vmem, vmem, vmem),
@@ -337,51 +323,93 @@
     )(jnp.transpose(neighbours), got, jnp.transpose(populations, (1, 0, 2)))
 
 
-def stream_kernel(where_in, post, mid, down, up, down2, up2, out, table, ghost, where_, sem):
-    parts = [(mid, 50, 50), (down, 0, 50), (up, 100, 50), (down2, 150, 5), (up2, 155, 5)]
-    copies = [pltpu.make_async_copy(where_in, where_, sem.at[5])] + [
-        pltpu.make_async_copy(ref, table.at[pl.ds(at * 32, size * 32)], sem.at[n])
-        for n, (ref, at, size) in enumerate(parts)
-    ]
-    for c in copies:
-        c.start()
-    table[NOWHERE:, :] = jnp.full((NT * 32, 128), jnp.nan, f32)
-    for c in copies:
-        c.wait()
+def route_kernel(sizes, left2, left, mine, right, right2, down, own, up, down2, up2, lines):
+    n_gy = sizes[1]
+    me_x, me_y = lax.axis_index("gx"), lax.axis_index("gy")
+    for n, part in enumerate((left[EDGE_TILE], mine[EDGE_TILE], right[EDGE_TILE], left2[0], right2[0])):
+        lines[32 * n : 32 * (n + 1), :] = part
+    lines[160:256, :] = jnp.full((96, 128), -1.0, f32)
+    ids = [jnp.transpose(lines[0:128, :]), jnp.transpose(lines[128:256, :])]
+    slot = lax.broadcasted_iota(i32, (32, 128), 0).astype(f32)
+    low = lax.broadcasted_iota(i32, (32, 128), 1) < 64
+    named = {}
+    for dy in range(-2, 3):
+        owner = me_x * n_gy + lax.rem(me_y + (dy + n_gy), n_gy)
+        named[dy] = slot + (owner * 32).astype(f32)
+
+    def hot(half, row, dy):
+        picked = jnp.broadcast_to(ids[half][IDS + row : IDS + row + 1, :], (32, 128)) == named[dy]
+        return picked.astype(f32)
+
+    none = jnp.zeros((32, 128), f32)
+    for ax in range(3):
+        planes = jnp.concatenate(
+            [
+                jnp.concatenate([left[t], mine[t], right[t], none], axis=0)
+                for t in range(5 * ax, 5 * ax + 5)
+            ],
+            axis=1,
+        )
+        p_hi = planes.astype(bf16)
+        p_lo = (planes - p_hi.astype(f32)).astype(bf16)
+        picks = jnp.concatenate([hot(0, 2 * ax + s, dy) for s in range(2) for dy in (-1, 0, 1)], axis=0).astype(bf16)
+        moved = jnp.dot(picks, p_hi, preferred_element_type=f32) + jnp.dot(picks, p_lo, preferred_element_type=f32)
+        for k, goal in enumerate((down, own, up)):
+            for n in range(5):
+                cut = slice(128 * n, 128 * (n + 1))
+                goal[5 * ax + n] = jnp.where(
+                    low, moved[32 * k : 32 * (k + 1), cut], moved[96 + 32 * k : 96 + 32 * (k + 1), cut]
+                )
+    e_hi = lines[...].astype(bf16)
+    e_lo = (lines[...] - e_hi.astype(f32)).astype(bf16)
+    both = jnp.concatenate([e_hi, e_lo], axis=1)
+    lane = lax.broadcasted_iota(i32, (160, 128), 1)
+    total = jnp.zeros((160, 128), f32)
+    for n in range(12):
+        picks = jnp.concatenate(
+            [jnp.concatenate([hot(h, 6 + n, dy) for dy in range(-2, 3)], axis=0) for h in range(2)], axis=1
+        ).astype(bf16)
+        moved = jnp.dot(picks, both, preferred_element_type=f32)
+        wanted = (lane // 8 == n) | (lane == HAVE + n)
+        total = jnp.where(wanted, moved[:, 0:128] + moved[:, 128:256], total)
+    for k, goal in enumerate((down2, down, own, up, up2)):
+        goal[goal.shape[0] - 1] = total[32 * k : 32 * (k + 1)]
+
+
+def route(left2, left, mine, right, right2):
+    vmem = pl.BlockSpec(memory_space=pltpu.VMEM)
+    sizes = (lax.axis_size("gx"), lax.axis_size("gy"))
+    big = jax.ShapeDtypeStruct(mine.shape, f32)
+    small = jax.ShapeDtypeStruct(left2.shape, f32)
+    return pl.pallas_call(
+        functools.partial(route_kernel, sizes),
+        out_shape=(big, big, big, small, small),
+        in_specs=[vmem] * 5,
+        out_specs=(vmem,) * 5,
+        scratch_shapes=[pltpu.VMEM((256, 128), f32)],
+        compiler_params=pltpu.CompilerParams(vmem_limit_bytes=48 << 20),
+        name="route",
+    )(left2, left, mine, right, right2)
+
+
+def stream_kernel(goal, post, own, below, above, below2, above2, out):
     lanes = lax.broadcasted_iota(i32, (8, 128), 1)
-    sub = lax.broadcasted_iota(i32, (8, 128), 0)
-
-    def row_of(at, tile):
-        return table[pl.ds(at + 32 * tile, 8, stride=0), :]
-
-    def fetch(g, carry):
-        rows = pl.ds(pl.multiple_of(g * 8, 8), 8)
-        for ax in range(3):
-            made = [jnp.zeros((8, 128), f32)] * 5
-            for i in range(8):
-                low_at = where_[g * 8 + i, 2 * ax]
-                high_at = where_[g * 8 + i, 2 * ax + 1]
-                for n in range(5):
-                    t = 5 * ax + n
-                    both = jnp.where(lanes < 64, row_of(high_at, t), row_of(low_at, t))
-                    made[n] = jnp.where(sub == i, both, made[n])
-            for n in range(5):
-                ghost[5 * ax + n, rows, :] = made[n]
-        line = jnp.zeros((8, 128), f32)
-        for i in range(8):
-            for n in range(12):
-                at = where_[g * 8 + i, 6 + n]
-                line = jnp.where((lanes // 8 == n) & (sub == i), row_of(at, 0), line)
-        ghost[EDGE_TILE, rows, :] = line
-        return carry
-
-    lax.fori_loop(0, 4, fetch, 0)
     jj = (lanes // 8) % 8
     kk = lanes % 8
 
     def group(g, carry):
         rows = pl.ds(pl.multiple_of(g * 8, 8), 8)
-        edges = ghost[EDGE_TILE, rows, :]
+        near = goal[rows, :]
+        ghost = []
+        for ax in range(3):
+            have = lane_take(near, jnp.where(lanes < 64, 2 * ax + 1, 2 * ax)) >= 0.0
+            for t in range(5 * ax, 5 * ax + 5):
+                came = own[t, rows, :] + below[t, rows, :] + above[t, rows, :]
+                ghost.append(jnp.where(have, came, jnp.nan))
+        came = own[EDGE_TILE, rows, :] + below[EDGE_TILE, rows, :] + above[EDGE_TILE, rows, :]
+        came = came + below2[0, rows, :] + above2[0, rows, :]
+        have = lane_take(came, jnp.minimum(HAVE + lanes // 8, 127)) > 0.5
+        edges = jnp.where(have, came, jnp.nan)
         out[0, rows, :] = post[0, rows, :]
         for q in range(1, 19):
             e = vel[q]
@@ -408,7 +436,7 @@
                     val = jnp.where(out_of, back, val)
                 for d in axes:
                     n = (POS[d] if e[d] == 1 else NEG[d]).index(q)
-                    source = ghost[5 * d + n, rows, :]
+                    source = ghost[5 * d + n]
                     base = 64 if e[d] == 1 else 0
                     if d == 0:
                         brought = pltpu.roll(source, (64 + ey * 8 + ez) % 128, 1)
@@ -432,23 +460,16 @@
     lax.fori_loop(0, 4, group, 0)
 
 
-def stream(where_, post, *parts):
+def stream(goal, post, *parts):
     vmem = pl.BlockSpec(memory_space=pltpu.VMEM)
-    anywhere = pl.BlockSpec(memory_space=pl.ANY)
     return pl.pallas_call(
         stream_kernel,
         out_shape=jax.ShapeDtypeStruct((19, 32, 512), f32),
-        in_specs=[anywhere, vmem] + [anywhere] * 5,
+        in_specs=[vmem] * 7,
         out_specs=vmem,
-        scratch_shapes=[
-            pltpu.VMEM(((160 + NT) * 32, 128), f32),
-            pltpu.VMEM((NT, 32, 128), f32),
-            pltpu.SMEM((32, 128), i32),
-            pltpu.SemaphoreType.DMA((6,)),
-        ],
         compiler_params=pltpu.CompilerParams(vmem_limit_bytes=48 << 20),
         name="stream",
-    )(where_, post, *[p.reshape(-1, 128) for p in parts])
+    )(goal, post, *parts)
 
 
 def send(array, axis, step):
@@ -460,17 +481,16 @@
     edge = table[EDGE_TILE : EDGE_TILE + 1]
     left, right = send(table, "gx", 1), send(table, "gx", -1)
     left2, right2 = send(edge, "gx", 2), send(edge, "gx", -2)
-    mid = jnp.concatenate([left, table, right, left2, right2], axis=0)
-    edges = jnp.concatenate([left2, left[EDGE_TILE:], edge, right[EDGE_TILE:], right2], axis=0)
-    return mid, send(mid, "gy", 1), send(mid, "gy", -1), send(edges, "gy", 2), send(edges, "gy", -2)
+    down, own, up, down2, up2 = route(left2, left, table, right, right2)
+    return own, send(up, "gy", 1), send(down, "gy", -1), send(up2, "gy", 2), send(down2, "gy", -2)
 
 
 def body(populations, neighbours, positions, stiffness, cell_owner, cell_block, triangles):
     devices = lax.axis_size("gx") * lax.axis_size("gy")
     slots = spread(cell_owner[:, 0], cell_block, positions, stiffness, triangles, neighbours, devices)
     got = lax.all_to_all(slots, BOTH, split_axis=0, concat_axis=0, tiled=True)
-    post, table, where_ = collide(got, populations, neighbours)
-    result = stream(where_, post, *exchange(table))
+    post, table, goal = collide(got, populations, neighbours)
+    result = stream(goal, post, *exchange(table))
     return jnp.transpose(result, (1, 0, 2))
 
 

time: 92 us -> 84.7 us (0.921)
  starting transfers between devices: 13 us -> 9.23 us
  waiting for transfers between devices: 14.9 us -> 11.4 us
    ppermute x8, starting transfers between devices: 13 us -> 9.23 us  [send(): lax.ppermute(array, axis, [(i, (i + step) % size) for i in range(size)])]
    ppermute x8, waiting for transfers between devices: 14.9 us -> 11.4 us  [send(): lax.ppermute(array, axis, [(i, (i + step) % size) for i in range(size)])]
    pallas_call x1 -> x2, Pallas kernels: 2.24 us -> 4.01 us  [the longest x1 3.14 us: collide(): pl.pallas_call(collide_kernel, out_shape=(jax.ShapeDtypeStruct((19, 32, 5...]
    pallas_call x1, Pallas kernels: 4.73 us -> 3.05 us  [stream(): pl.pallas_call(stream_kernel, out_shape=jax.ShapeDtypeStruct((19, 32, 512...]
where the time goes in v2:
time: 84.7 us; the launch traced here: 84.5 us
  blocking collectives  37.4 us (44%)
  Pallas kernels  23.4 us (28%)
  waiting for transfers between devices  11.4 us (13%)
  starting transfers between devices  9.23 us (11%)
  local copies, waits for them, and re-layouts  3.05 us (4%)
    all_to_all x1, blocking collectives, body(): got = lax.all_to_all(slots, BOTH, split_axis=0, concat_axis=0, tiled=True)  37.4 us
    pallas_call x1, Pallas kernels, spread(): pl.pallas_call(spread_kernel, out_shape=jax.ShapeDtypeStruct((devices, WI...  16.3 us
    ppermute x8, waiting for transfers between devices, send(): lax.ppermute(array, axis, [(i, (i + step) % size) for i in range(size)])  11.4 us
    ppermute x8, starting transfers between devices, send(): lax.ppermute(array, axis, [(i, (i + step) % size) for i in range(size)])  9.23 us
    pallas_call x1, Pallas kernels, collide(): pl.pallas_call(collide_kernel, out_shape=(jax.ShapeDtypeStruct((19, 32, 5...  3.14 us
    pallas_call x1, Pallas kernels, stream(): pl.pallas_call(stream_kernel, out_shape=jax.ShapeDtypeStruct((19, 32, 512...  3.05 us
    all_to_all x1, local copies, waits for them, and re-layouts, body(): got = lax.all_to_all(slots, BOTH, split_axis=0, concat_axis=0, tiled=True)  1.75 us
  transfers between devices with their start and end apart: 8, of which 4 were waited for; matrix products, arithmetic and copies ran while one was open for 0% of the time, Pallas kernels for 0%

profile of v2, /device:TPU:1, one launch (start us, length us, event | category | flops | bytes accessed | tf_op | source)
XLA Modules:
  0.0 84.5 jit_solution(11081654849137962851)
XLA Ops:
  0.0 16.3 %spread.1 = f32[128,3328]{1,0:T(8,128)S(1)} custom-call(s32[128]{0:T(128)} %bitcast.17, s32[128]{0:T(128)} %block_in.1, f32[128]{0:T(128)} %stiff_in.1, f32[3,642,128]{2,1,0:T(8,128)} %bitcast.15, s32[3,1280]{1,0:T(4,128)} %bitcast.16, s32[6,32]{1,0:T(8,128)} %bitcast.13), custom_call_target="tpu_custom_call" | custom-call | tf_op jit(solution)/shard_map/spread/pallas_call | solution.py:157
  16.3 1.8 %copy.8 = f32[128,1,3328]{2,1,0:T(1,128)S(1)} copy(f32[128,1,3328]{2,0,1:T(8,128)S(1)} %bitcast.11) | data formatting | bytes 3407872 | tf_op jit(solution)/shard_map/all_to_all | solution.py:491
  18.1 37.4 %all_to_all.11 = f32[128,1,3328]{2,1,0:T(1,128)S(1)} all-to-all(f32[128,1,3328]{2,1,0:T(1,128)S(1)} %copy.8), channel_id=1, replica_groups=mesh['gx'=16,'gy'=8] {'gx','gy'}, dimensions={0} | all-to-all | bytes 3407872 | tf_op jit(solution)/shard_map/all_to_all | solution.py:491
  55.5 0.0 copy-start
  55.5 0.0 copy-start.1
  55.5 0.1 copy.11
  55.6 1.2 %copy-done = f32[32,19,512]{2,0,1:T(8,128)S(1)} copy-done((f32[32,19,512]{2,0,1:T(8,128)S(1)}, f32[32,19,512]{2,0,1:T(8,128)}, u32[]{:S(2)}) %copy-start) | copy-done | bytes 1245208
  56.8 0.0 copy-done.1
  56.8 3.1 %collide.1 = (f32[19,32,512]{2,1,0:T(8,128)S(1)}, f32[16,32,128]{2,1,0:T(8,128)S(1)}, f32[32,128]{1,0:T(8,128)S(1)}) custom-call(s32[6,32]{1,0:T(8,128)S(1)} %bitcast.14, f32[128,3328]{1,0:T(8,128)S(1)} %bitcast.10, f32[19,32,512]{2,1,0:T(8,128)S(1)} %bitcast.12), custom_call_target="tpu_custom_call" | custom-call | tf_op jit(solution)/shard_map/collide/pallas_call | solution.py:308
  60.0 1.4 %collective-permute-start.2 = (f32[16,32,128]{2,1,0:T(8,128)S(1)}, f32[16,32,128]{2,1,0:T(8,128)S(1)}, u32[]{:S(2)}, u32[]{:S(2)}) collective-permute-start(f32[16,32,128]{2,1,0:T(8,128)S(1)} %get-tuple-element.15.mine), channel_id=1, source_target_pairs={{0,120},{8,0},{16,8},{24,16},{32,24},{40,32},{48,40},{56,48},{64,5... | collective-permute-start | bytes 786440 | tf_op jit(solution)/shard_map/ppermute | solution.py:477
  61.4 0.1 collective-permute-start.1
  61.5 1.5 %collective-permute-start.3 = (f32[1,32,128]{2,1,0:T(8,128)S(1)}, f32[1,32,128]{2,1,0:T(8,128)S(1)}, u32[]{:S(2)}, u32[]{:S(2)}) collective-permute-start(f32[1,32,128]{2,1,0:T(8,128)S(1)} %slice.3), channel_id=1, source_target_pairs={{0,112},{8,120},{16,0},{24,8},{32,16},{40,24},{48,32},{56,40},{64,... | collective-permute-start | bytes 49160 | tf_op jit(solution)/shard_map/ppermute | solution.py:477
  63.0 1.5 %collective-permute-start = (f32[1,32,128]{2,1,0:T(8,128)S(1)}, f32[1,32,128]{2,1,0:T(8,128)S(1)}, u32[]{:S(2)}, u32[]{:S(2)}) collective-permute-start(f32[1,32,128]{2,1,0:T(8,128)S(1)} %slice.3), channel_id=1, source_target_pairs={{0,16},{8,24},{16,32},{24,40},{32,48},{40,56},{48,64},{56,72},{64,... | collective-permute-start | bytes 49160 | tf_op jit(solution)/shard_map/ppermute | solution.py:477
  64.5 2.7 %collective-permute-done.3.right2 = f32[1,32,128]{2,1,0:T(8,128)S(1)} collective-permute-done((f32[1,32,128]{2,1,0:T(8,128)S(1)}, f32[1,32,128]{2,1,0:T(8,128)S(1)}, u32[]{:S(2)}, u32[]{:S(2)}) %collective-permute-start.3) | collective-permute-done | bytes 16416 | tf_op jit(solution)/shard_map/ppermute | solution.py:477
  67.1 2.4 %collective-permute-done.left2 = f32[1,32,128]{2,1,0:T(8,128)S(1)} collective-permute-done((f32[1,32,128]{2,1,0:T(8,128)S(1)}, f32[1,32,128]{2,1,0:T(8,128)S(1)}, u32[]{:S(2)}, u32[]{:S(2)}) %collective-permute-start) | collective-permute-done | bytes 16416 | tf_op jit(solution)/shard_map/ppermute | solution.py:477
  69.5 0.0 collective-permute-done.2.right
  69.5 2.4 %collective-permute-done.1.left = f32[16,32,128]{2,1,0:T(8,128)S(1)} collective-permute-done((f32[16,32,128]{2,1,0:T(8,128)S(1)}, f32[16,32,128]{2,1,0:T(8,128)S(1)}, u32[]{:S(2)}, u32[]{:S(2)}) %collective-permute-start.1) | collective-permute-done | bytes 262176 | tf_op jit(solution)/shard_map/ppermute | solution.py:477
  71.9 0.9 %route.1 = (f32[16,32,128]{2,1,0:T(8,128)S(1)}, f32[16,32,128]{2,1,0:T(8,128)S(1)}, f32[16,32,128]{2,1,0:T(8,128)S(1)}, f32[1,32,128]{2,1,0:T(8,128)S(1)}, f32[1,32,128]{2,1,0:T(8,128)S(1)}) custom-call(f32[1,32,128]{2,1,0:T(8,128)S(1)} %collective-permute-done.left2, f32[16,32,128]{2,1,0:T(8,128)S(1)} %collective-permute-done.1.left, ...), custom_call_target="tpu_custom_call" | custom-call | tf_op jit(solution)/shard_map/route/pallas_call | solution.py:384
  72.8 1.9 %collective-permute-start.4 = (f32[16,32,128]{2,1,0:T(8,128)S(1)}, f32[16,32,128]{2,1,0:T(8,128)S(1)}, u32[]{:S(2)}, u32[]{:S(2)}) collective-permute-start(f32[16,32,128]{2,1,0:T(8,128)S(1)} %get-tuple-element.17), channel_id=1, source_target_pairs={{0,1},{1,2},{2,3},{3,4},{4,5},{5,6},{6,7},{7,0},{8,9},{9,10},{10,1... | collective-permute-start | bytes 786440 | tf_op jit(solution)/shard_map/ppermute | solution.py:477
  74.7 0.2 collective-permute-start.5
  74.9 0.1 collective-permute-start.6
  75.0 2.5 %collective-permute-start.7 = (f32[1,32,128]{2,1,0:T(8,128)S(1)}, f32[1,32,128]{2,1,0:T(8,128)S(1)}, u32[]{:S(2)}, u32[]{:S(2)}) collective-permute-start(f32[1,32,128]{2,1,0:T(8,128)S(1)} %get-tuple-element.20), channel_id=1, source_target_pairs={{0,6},{1,7},{2,0},{3,1},{4,2},{5,3},{6,4},{7,5},{8,14},{9,15},{10,... | collective-permute-start | bytes 49160 | tf_op jit(solution)/shard_map/ppermute | solution.py:477
  77.5 3.9 %collective-permute-done.6.below2 = f32[1,32,128]{2,1,0:T(8,128)S(1)} collective-permute-done((f32[1,32,128]{2,1,0:T(8,128)S(1)}, f32[1,32,128]{2,1,0:T(8,128)S(1)}, u32[]{:S(2)}, u32[]{:S(2)}) %collective-permute-start.6) | collective-permute-done | bytes 16416 | tf_op jit(solution)/shard_map/ppermute | solution.py:477
  81.5 0.0 collective-permute-done.7.above2
  81.5 0.0 collective-permute-done.4.below
  81.5 0.0 collective-permute-done.5.above
  81.5 3.0 %stream.1 = f32[19,32,512]{2,1,0:T(8,128)} custom-call(f32[32,128]{1,0:T(8,128)S(1)} %get-tuple-element.13.goal, f32[19,32,512]{2,1,0:T(8,128)S(1)} %get-tuple-element.14.post, f32[16,32,128]{2,1,0:T(8,128)S(1)} %get-tuple-element.16.own, f32[16,32,128]{2,1,0:T(8,128)S(1)} %collective-permute-done.4.below, f32[16,32,128]{2,1,0:T(8,128)S(1)} %collective-permute-done.5.above, ...), custom_call_target="tpu_custom_call" | custom-call | tf_op jit(solution)/shard_map/stream/pallas_call | solution.py:465
  (1 shorter events, 0.0 us)
Async XLA Ops:
  55.5 1.3 %copy-start = (f32[32,19,512]{2,0,1:T(8,128)S(1)}, f32[32,19,512]{2,0,1:T(8,128)}, u32[]{:S(2)}) copy-start(f32[32,19,512]{2,0,1:T(8,128)} %param.7) | copy-start | bytes 3735556
  55.5 1.3 %copy-start.1 = (s32[32,6]{0,1:T(8,128)S(1)}, s32[32,6]{0,1:T(8,128)}, u32[]{:S(2)}) copy-start(s32[32,6]{0,1:T(8,128)} %param.8) | copy-start | bytes 2308
  60.0 9.6 %collective-permute-start.2 = (f32[16,32,128]{2,1,0:T(8,128)S(1)}, f32[16,32,128]{2,1,0:T(8,128)S(1)}, u32[]{:S(2)}, u32[]{:S(2)}) collective-permute-start(f32[16,32,128]{2,1,0:T(8,128)S(1)} %get-tuple-element.15.mine), channel_id=1, source_target_pairs={{0,120},{8,0},{16,8},{24,16},{32,24},{40,32},{48,40},{56,48},{64,5... | collective-permute-start | bytes 786440 | tf_op jit(solution)/shard_map/ppermute | solution.py:477
  61.4 10.6 %collective-permute-start.1 = (f32[16,32,128]{2,1,0:T(8,128)S(1)}, f32[16,32,128]{2,1,0:T(8,128)S(1)}, u32[]{:S(2)}, u32[]{:S(2)}) collective-permute-start(f32[16,32,128]{2,1,0:T(8,128)S(1)} %get-tuple-element.15.mine), channel_id=1, source_target_pairs={{0,8},{8,16},{16,24},{24,32},{32,40},{40,48},{48,56},{56,64},{64,7... | collective-permute-start | bytes 786440 | tf_op jit(solution)/shard_map/ppermute | solution.py:477
  61.5 5.7 %collective-permute-start.3 = (f32[1,32,128]{2,1,0:T(8,128)S(1)}, f32[1,32,128]{2,1,0:T(8,128)S(1)}, u32[]{:S(2)}, u32[]{:S(2)}) collective-permute-start(f32[1,32,128]{2,1,0:T(8,128)S(1)} %slice.3), channel_id=1, source_target_pairs={{0,112},{8,120},{16,0},{24,8},{32,16},{40,24},{48,32},{56,40},{64,... | collective-permute-start | bytes 49160 | tf_op jit(solution)/shard_map/ppermute | solution.py:477
  63.0 6.6 %collective-permute-start = (f32[1,32,128]{2,1,0:T(8,128)S(1)}, f32[1,32,128]{2,1,0:T(8,128)S(1)}, u32[]{:S(2)}, u32[]{:S(2)}) collective-permute-start(f32[1,32,128]{2,1,0:T(8,128)S(1)} %slice.3), channel_id=1, source_target_pairs={{0,16},{8,24},{16,32},{24,40},{32,48},{40,56},{48,64},{56,72},{64,... | collective-permute-start | bytes 49160 | tf_op jit(solution)/shard_map/ppermute | solution.py:477
  72.8 8.6 %collective-permute-start.4 = (f32[16,32,128]{2,1,0:T(8,128)S(1)}, f32[16,32,128]{2,1,0:T(8,128)S(1)}, u32[]{:S(2)}, u32[]{:S(2)}) collective-permute-start(f32[16,32,128]{2,1,0:T(8,128)S(1)} %get-tuple-element.17), channel_id=1, source_target_pairs={{0,1},{1,2},{2,3},{3,4},{4,5},{5,6},{6,7},{7,0},{8,9},{9,10},{10,1... | collective-permute-start | bytes 786440 | tf_op jit(solution)/shard_map/ppermute | solution.py:477
  74.7 6.8 %collective-permute-start.5 = (f32[16,32,128]{2,1,0:T(8,128)S(1)}, f32[16,32,128]{2,1,0:T(8,128)S(1)}, u32[]{:S(2)}, u32[]{:S(2)}) collective-permute-start(f32[16,32,128]{2,1,0:T(8,128)S(1)} %get-tuple-element.18), channel_id=1, source_target_pairs={{0,7},{1,0},{2,1},{3,2},{4,3},{5,4},{6,5},{7,6},{8,15},{9,8},{10,9... | collective-permute-start | bytes 786440 | tf_op jit(solution)/shard_map/ppermute | solution.py:477
  74.9 6.6 %collective-permute-start.6 = (f32[1,32,128]{2,1,0:T(8,128)S(1)}, f32[1,32,128]{2,1,0:T(8,128)S(1)}, u32[]{:S(2)}, u32[]{:S(2)}) collective-permute-start(f32[1,32,128]{2,1,0:T(8,128)S(1)} %get-tuple-element.19), channel_id=1, source_target_pairs={{0,2},{1,3},{2,4},{3,5},{4,6},{5,7},{6,0},{7,1},{8,10},{9,11},{10,... | collective-permute-start | bytes 49160 | tf_op jit(solution)/shard_map/ppermute | solution.py:477
  75.0 6.4 %collective-permute-start.7 = (f32[1,32,128]{2,1,0:T(8,128)S(1)}, f32[1,32,128]{2,1,0:T(8,128)S(1)}, u32[]{:S(2)}, u32[]{:S(2)}) collective-permute-start(f32[1,32,128]{2,1,0:T(8,128)S(1)} %get-tuple-element.20), channel_id=1, source_target_pairs={{0,6},{1,7},{2,0},{3,1},{4,2},{5,3},{6,4},{7,5},{8,14},{9,15},{10,... | collective-permute-start | bytes 49160 | tf_op jit(solution)/shard_map/ppermute | solution.py:477

commit v3 on v2

--- a/solution.py
+++ b/solution.py
@@ -47,33 +47,34 @@
     copies = [pltpu.make_async_copy(a, b, sem.at[n]) for n, (a, b) in enumerate(pairs)]
     for c in copies:
         c.start()
-    for c in copies:
-        c.wait()
+    copies[0].wait()
     for r in range(0, nv, 128):
         ids = lax.broadcasted_iota(i32, (128, tri.shape[1]), 0) + r
         hit = (ids == tri[0:1, :]) | (ids == tri[1:2, :]) | (ids == tri[2:3, :])
         st[r : r + 128, :] = hit.astype(f32).astype(bf16)
+    links = nt_dot(st[...], st[...])
+    for c in copies[1:]:
+        c.wait()
+    for r in range(0, nv, 128):
         for d in range(3):
             have = min(verts - r, 128)
             piece = raw[d, r : r + have, :]
             if have < 128:
                 piece = jnp.concatenate([piece, jnp.full((128 - have, cells), -100.0, f32)], axis=0)
             pos[d, :, r : r + 128] = jnp.transpose(piece)
-    links = nt_dot(st[...], st[...])
     rows = lax.broadcasted_iota(i32, (nv, nv), 0)
     cols = lax.broadcasted_iota(i32, (nv, nv), 1)
     springs = jnp.where(rows == cols, -2.0 * links, links)
     s_hi = springs.astype(bf16)
     s_lo = (springs - s_hi.astype(f32)).astype(bf16)
+    x = jnp.concatenate([pos[0], pos[1], pos[2]], axis=0)
+    x_hi = x.astype(bf16)
+    x_lo = (x - x_hi.astype(f32)).astype(bf16)
+    most = jnp.dot(jnp.concatenate([x_hi, x_lo], axis=0), s_hi, preferred_element_type=f32)
+    rest = jnp.dot(x_hi, s_lo, preferred_element_type=f32)
     for d in range(3):
-        x = pos[d]
-        x_hi = x.astype(bf16)
-        x_lo = (x - x_hi.astype(f32)).astype(bf16)
-        force[d] = (
-            jnp.dot(x_hi, s_hi, preferred_element_type=f32)
-            + jnp.dot(x_lo, s_hi, preferred_element_type=f32)
-            + jnp.dot(x_hi, s_lo, preferred_element_type=f32)
-        )
+        lo, hi = d * cells, (d + 1) * cells
+        force[d] = most[lo:hi] + most[3 * cells + lo : 3 * cells + hi] + rest[lo:hi]
     sub = lax.broadcasted_iota(i32, (8, 128), 0)
     lane = lax.broadcasted_iota(i32, (8, 128), 1)
     slots = out.shape[0]
@@ -83,13 +84,12 @@
         one_face = jnp.concatenate([near[f + 2 : f + 3, :].astype(f32), jnp.zeros((1, 96), f32)], axis=1)
         one_face = jnp.broadcast_to(one_face, (8, 128))
         table_row = jnp.where(lane // 32 == f, pltpu.roll(one_face, 32 * f, 1) if f else one_face, table_row)
-    out[:, 0:3072] = jnp.zeros((slots, 3072), f32)
 
     def clear(t, carry):
-        base = pl.ds(pl.multiple_of(t * 8, 8), 8)
-        out[base, 3072:3200] = tail_row
-        out[base, 3200:3328] = table_row
         for m in range(8):
+            out[t * 8 + m, :, 0:3072] = jnp.zeros((1, 3072), f32)
+            out[t * 8 + m, :, 3072:3200] = tail_row[0:1]
+            out[t * 8 + m, :, 3200:3328] = table_row[0:1]
             count[t * 8 + m] = 0
         return carry
 
@@ -100,13 +100,15 @@
     g_all = sub8.astype(f32)
     first4 = sub8 < 4
 
-    def one(c, m):
-        x = jnp.broadcast_to(pos[0, pl.ds(c, 1), :], (8, nv))
-        y = jnp.broadcast_to(pos[1, pl.ds(c, 1), :], (8, nv))
-        z = jnp.broadcast_to(pos[2, pl.ds(c, 1), :], (8, nv))
-        f0 = jnp.broadcast_to(force[0, pl.ds(c, 1), :], (8, nv))
-        f1 = jnp.broadcast_to(force[1, pl.ds(c, 1), :], (8, nv))
-        f2 = jnp.broadcast_to(force[2, pl.ds(c, 1), :], (8, nv))
+    def product(first, m):
+        c = first + m
+        near8 = pl.ds(pl.multiple_of(first + m // 8 * 8, 8), 8)
+        x = jnp.broadcast_to(pos[0, near8, :][m % 8 : m % 8 + 1], (8, nv))
+        y = jnp.broadcast_to(pos[1, near8, :][m % 8 : m % 8 + 1], (8, nv))
+        z = jnp.broadcast_to(pos[2, near8, :][m % 8 : m % 8 + 1], (8, nv))
+        f0 = jnp.broadcast_to(force[0, near8, :][m % 8 : m % 8 + 1], (8, nv))
+        f1 = jnp.broadcast_to(force[1, near8, :][m % 8 : m % 8 + 1], (8, nv))
+        f2 = jnp.broadcast_to(force[2, near8, :][m % 8 : m % 8 + 1], (8, nv))
         h_even = hat(x, g_even)
         h_odd = hat(x, g_odd)
         f01 = jnp.where(first4, f0, f1)
@@ -115,15 +117,18 @@
         )
         l_lo = left - left.astype(bf16).astype(f32)
         left2 = jnp.concatenate([left, l_lo], axis=0).astype(bf16)
-        hats[m] = hat(y, g_all)
+        hy = hat(y, g_all)
         hz = hat(z, g_all)
         plane = jnp.concatenate(
-            [jnp.broadcast_to(hats[m, j : j + 1, :], (8, nv)) * hz for j in range(8)], axis=0
+            [jnp.broadcast_to(hy[j : j + 1], (8, nv)) * hz for j in range(8)], axis=0
         )
         p_hi = plane.astype(bf16)
         p_lo = (plane - p_hi.astype(f32)).astype(bf16)
         prod = nt_dot(left2, jnp.concatenate([p_hi, p_lo], axis=0))
-        both = prod[0:24] + prod[24:48]
+        hats[m] = prod[0:24] + prod[24:48]
+
+    def place(c, m):
+        both = hats[m]
         res = (both + pltpu.roll(both, 64, 1)) * stiff[c]
         main = jnp.where(lane < 64, res[0:8], res[16:24])
         mid = res[8:16]
@@ -131,21 +136,29 @@
         t = owner[c]
         r = count[t]
         count[t] = r + 1
-        base = pl.multiple_of((t // 8) * 8, 8)
-        mine = sub == t % 8
         for k in range(12):
             row = main[k : k + 1] if k < 8 else tail[k - 8 : k - 7]
-            at = pl.multiple_of(r * 1536 + 128 * k, 128)
-            pltpu.store(out.at[pl.ds(base, 8), pl.ds(at, 128)], jnp.broadcast_to(row, (8, 128)), mask=mine)
-        label = jnp.full((8, 128), block[c].astype(f32))
-        pltpu.store(out.at[pl.ds(base, 8), 3072:3200], label, mask=mine & (lane == r))
+            out[t, :, pl.ds(pl.multiple_of(r * 1536 + 128 * k, 128), 128)] = row
+        old = out[t, :, 3072:3200]
+        out[t, :, 3072:3200] = jnp.where(lane[0:1] == r, block[c].astype(f32), old)
+
+    group = hats.shape[0]
+
+    def finish(first):
+        for m in range(group):
+            place(first + m, m)
+
+    for m in range(group):
+        product(0, m)
 
     def step(n, carry):
-        for m in range(16):
-            one(n * 16 + m, m)
+        finish((n - 1) * group)
+        for m in range(group):
+            product(n * group, m)
         return carry
 
-    lax.fori_loop(0, cells // 16, step, 0)
+    lax.fori_loop(1, cells // group, step, 0)
+    finish(cells - group)
 
 
 def spread(owner, block, positions, stiffness, triangles, neighbours, devices):
@@ -156,7 +169,7 @@
     vmem = pl.BlockSpec(memory_space=pltpu.VMEM)
     return pl.pallas_call(
         spread_kernel,
-        out_shape=jax.ShapeDtypeStruct((devices, WIDE), f32),
+        out_shape=jax.ShapeDtypeStruct((devices, 1, WIDE), f32),
         in_specs=[hbm] * 6,
         out_specs=vmem,
         scratch_shapes=[
@@ -170,7 +183,7 @@
             pltpu.VMEM((nv, triangles.shape[0]), bf16),
             pltpu.VMEM((3, cells, nv), f32),
             pltpu.VMEM((3, cells, nv), f32),
-            pltpu.VMEM((16, 8, nv), f32),
+            pltpu.VMEM((16, 24, 128), f32),
             pltpu.SMEM((devices,), i32),
         ],
         compiler_params=pltpu.CompilerParams(vmem_limit_bytes=48 << 20),
@@ -489,7 +502,7 @@
     devices = lax.axis_size("gx") * lax.axis_size("gy")
     slots = spread(cell_owner[:, 0], cell_block, positions, stiffness, triangles, neighbours, devices)
     got = lax.all_to_all(slots, BOTH, split_axis=0, concat_axis=0, tiled=True)
-    post, table, goal = collide(got, populations, neighbours)
+    post, table, goal = collide(got.reshape(devices, WIDE), populations, neighbours)
     result = stream(goal, post, *exchange(table))
     return jnp.transpose(result, (1, 0, 2))
 

time: 84.7 us -> 81.5 us (0.962)
  local copies, waits for them, and re-layouts: 3.05 us -> 1.29 us
  Pallas kernels: 23.4 us -> 22 us
    all_to_all x1 -> x0, local copies, waits for them, and re-layouts: 1.75 us -> none  [body(): got = lax.all_to_all(slots, BOTH, split_axis=0, concat_axis=0, tiled=True)]
    pallas_call x1, Pallas kernels: 16.3 us -> 14.9 us  [spread(): pl.pallas_call(spread_kernel, out_shape=jax.ShapeDtypeStruct((devices, 1,...]
where the time goes in v3:
time: 81.5 us; the launch traced here: 81.3 us
  blocking collectives  37.4 us (46%)
  Pallas kernels  22 us (27%)
  waiting for transfers between devices  11.4 us (14%)
  starting transfers between devices  9.22 us (11%)
  local copies, waits for them, and re-layouts  1.29 us (2%)
    all_to_all x1, blocking collectives, body(): got = lax.all_to_all(slots, BOTH, split_axis=0, concat_axis=0, tiled=True)  37.4 us
    pallas_call x1, Pallas kernels, spread(): pl.pallas_call(spread_kernel, out_shape=jax.ShapeDtypeStruct((devices, 1,...  14.9 us
    ppermute x8, waiting for transfers between devices, send(): lax.ppermute(array, axis, [(i, (i + step) % size) for i in range(size)])  11.4 us
    ppermute x8, starting transfers between devices, send(): lax.ppermute(array, axis, [(i, (i + step) % size) for i in range(size)])  9.22 us
    pallas_call x1, Pallas kernels, collide(): pl.pallas_call(collide_kernel, out_shape=(jax.ShapeDtypeStruct((19, 32, 5...  3.14 us
    pallas_call x1, Pallas kernels, stream(): pl.pallas_call(stream_kernel, out_shape=jax.ShapeDtypeStruct((19, 32, 512...  3.05 us
  transfers between devices with their start and end apart: 8, of which 4 were waited for; matrix products, arithmetic and copies ran while one was open for 0% of the time, Pallas kernels for 0%

profile of v3, /device:TPU:1, one launch (start us, length us, event | category | flops | bytes accessed | tf_op | source)
XLA Modules:
  0.0 81.3 jit_solution(8846292266426653765)
XLA Ops:
  0.0 14.9 %spread.1 = f32[128,1,3328]{2,1,0:T(1,128)S(1)} custom-call(s32[128]{0:T(128)} %bitcast.15, s32[128]{0:T(128)} %block_in.1, f32[128]{0:T(128)} %stiff_in.1, f32[3,642,128]{2,1,0:T(8,128)} %bitcast.13, s32[3,1280]{1,0:T(4,128)} %bitcast.14, s32[6,32]{1,0:T(8,128)} %bitcast.11), custom_call_target="tpu_custom_call" | custom-call | tf_op jit(solution)/shard_map/spread/pallas_call | solution.py:170
  14.9 37.4 %all_to_all.5 = f32[128,1,3328]{2,1,0:T(1,128)S(1)} all-to-all(f32[128,1,3328]{2,1,0:T(1,128)S(1)} %spread.1), channel_id=1, replica_groups=mesh['gx'=16,'gy'=8] {'gx','gy'}, dimensions={0} | all-to-all | bytes 3407872 | tf_op jit(solution)/shard_map/all_to_all | solution.py:504
  52.3 0.0 copy-start
  52.3 0.0 copy-start.1
  52.3 0.1 copy.11
  52.4 1.2 %copy-done = f32[32,19,512]{2,0,1:T(8,128)S(1)} copy-done((f32[32,19,512]{2,0,1:T(8,128)S(1)}, f32[32,19,512]{2,0,1:T(8,128)}, u32[]{:S(2)}) %copy-start) | copy-done | bytes 1245208
  53.6 0.0 copy-done.1
  53.6 3.1 %collide.1 = (f32[19,32,512]{2,1,0:T(8,128)S(1)}, f32[16,32,128]{2,1,0:T(8,128)S(1)}, f32[32,128]{1,0:T(8,128)S(1)}) custom-call(s32[6,32]{1,0:T(8,128)S(1)} %bitcast.12, f32[128,3328]{1,0:T(8,128)S(1)} %bitcast.9, f32[19,32,512]{2,1,0:T(8,128)S(1)} %bitcast.10), custom_call_target="tpu_custom_call" | custom-call | tf_op jit(solution)/shard_map/collide/pallas_call | solution.py:321
  56.8 1.4 %collective-permute-start.2 = (f32[16,32,128]{2,1,0:T(8,128)S(1)}, f32[16,32,128]{2,1,0:T(8,128)S(1)}, u32[]{:S(2)}, u32[]{:S(2)}) collective-permute-start(f32[16,32,128]{2,1,0:T(8,128)S(1)} %get-tuple-element.15.mine), channel_id=1, source_target_pairs={{0,120},{8,0},{16,8},{24,16},{32,24},{40,32},{48,40},{56,48},{64,5... | collective-permute-start | bytes 786440 | tf_op jit(solution)/shard_map/ppermute | solution.py:490
  58.2 0.1 collective-permute-start.1
  58.3 1.5 %collective-permute-start.3 = (f32[1,32,128]{2,1,0:T(8,128)S(1)}, f32[1,32,128]{2,1,0:T(8,128)S(1)}, u32[]{:S(2)}, u32[]{:S(2)}) collective-permute-start(f32[1,32,128]{2,1,0:T(8,128)S(1)} %slice.3), channel_id=1, source_target_pairs={{0,112},{8,120},{16,0},{24,8},{32,16},{40,24},{48,32},{56,40},{64,... | collective-permute-start | bytes 49160 | tf_op jit(solution)/shard_map/ppermute | solution.py:490
  59.8 1.5 %collective-permute-start = (f32[1,32,128]{2,1,0:T(8,128)S(1)}, f32[1,32,128]{2,1,0:T(8,128)S(1)}, u32[]{:S(2)}, u32[]{:S(2)}) collective-permute-start(f32[1,32,128]{2,1,0:T(8,128)S(1)} %slice.3), channel_id=1, source_target_pairs={{0,16},{8,24},{16,32},{24,40},{32,48},{40,56},{48,64},{56,72},{64,... | collective-permute-start | bytes 49160 | tf_op jit(solution)/shard_map/ppermute | solution.py:490
  61.3 2.7 %collective-permute-done.3.right2 = f32[1,32,128]{2,1,0:T(8,128)S(1)} collective-permute-done((f32[1,32,128]{2,1,0:T(8,128)S(1)}, f32[1,32,128]{2,1,0:T(8,128)S(1)}, u32[]{:S(2)}, u32[]{:S(2)}) %collective-permute-start.3) | collective-permute-done | bytes 16416 | tf_op jit(solution)/shard_map/ppermute | solution.py:490
  63.9 2.4 %collective-permute-done.left2 = f32[1,32,128]{2,1,0:T(8,128)S(1)} collective-permute-done((f32[1,32,128]{2,1,0:T(8,128)S(1)}, f32[1,32,128]{2,1,0:T(8,128)S(1)}, u32[]{:S(2)}, u32[]{:S(2)}) %collective-permute-start) | collective-permute-done | bytes 16416 | tf_op jit(solution)/shard_map/ppermute | solution.py:490
  66.3 0.0 collective-permute-done.2.right
  66.3 2.4 %collective-permute-done.1.left = f32[16,32,128]{2,1,0:T(8,128)S(1)} collective-permute-done((f32[16,32,128]{2,1,0:T(8,128)S(1)}, f32[16,32,128]{2,1,0:T(8,128)S(1)}, u32[]{:S(2)}, u32[]{:S(2)}) %collective-permute-start.1) | collective-permute-done | bytes 262176 | tf_op jit(solution)/shard_map/ppermute | solution.py:490
  68.7 0.9 %route.1 = (f32[16,32,128]{2,1,0:T(8,128)S(1)}, f32[16,32,128]{2,1,0:T(8,128)S(1)}, f32[16,32,128]{2,1,0:T(8,128)S(1)}, f32[1,32,128]{2,1,0:T(8,128)S(1)}, f32[1,32,128]{2,1,0:T(8,128)S(1)}) custom-call(f32[1,32,128]{2,1,0:T(8,128)S(1)} %collective-permute-done.left2, f32[16,32,128]{2,1,0:T(8,128)S(1)} %collective-permute-done.1.left, ...), custom_call_target="tpu_custom_call" | custom-call | tf_op jit(solution)/shard_map/route/pallas_call | solution.py:397
  69.6 1.9 %collective-permute-start.4 = (f32[16,32,128]{2,1,0:T(8,128)S(1)}, f32[16,32,128]{2,1,0:T(8,128)S(1)}, u32[]{:S(2)}, u32[]{:S(2)}) collective-permute-start(f32[16,32,128]{2,1,0:T(8,128)S(1)} %get-tuple-element.17), channel_id=1, source_target_pairs={{0,1},{1,2},{2,3},{3,4},{4,5},{5,6},{6,7},{7,0},{8,9},{9,10},{10,1... | collective-permute-start | bytes 786440 | tf_op jit(solution)/shard_map/ppermute | solution.py:490
  71.5 0.2 collective-permute-start.5
  71.7 0.1 collective-permute-start.6
  71.8 2.5 %collective-permute-start.7 = (f32[1,32,128]{2,1,0:T(8,128)S(1)}, f32[1,32,128]{2,1,0:T(8,128)S(1)}, u32[]{:S(2)}, u32[]{:S(2)}) collective-permute-start(f32[1,32,128]{2,1,0:T(8,128)S(1)} %get-tuple-element.20), channel_id=1, source_target_pairs={{0,6},{1,7},{2,0},{3,1},{4,2},{5,3},{6,4},{7,5},{8,14},{9,15},{10,... | collective-permute-start | bytes 49160 | tf_op jit(solution)/shard_map/ppermute | solution.py:490
  74.3 3.9 %collective-permute-done.6.below2 = f32[1,32,128]{2,1,0:T(8,128)S(1)} collective-permute-done((f32[1,32,128]{2,1,0:T(8,128)S(1)}, f32[1,32,128]{2,1,0:T(8,128)S(1)}, u32[]{:S(2)}, u32[]{:S(2)}) %collective-permute-start.6) | collective-permute-done | bytes 16416 | tf_op jit(solution)/shard_map/ppermute | solution.py:490
  78.3 0.0 collective-permute-done.7.above2
  78.3 0.0 collective-permute-done.4.below
  78.3 0.0 collective-permute-done.5.above
  78.3 3.0 %stream.1 = f32[19,32,512]{2,1,0:T(8,128)} custom-call(f32[32,128]{1,0:T(8,128)S(1)} %get-tuple-element.13.goal, f32[19,32,512]{2,1,0:T(8,128)S(1)} %get-tuple-element.14.post, f32[16,32,128]{2,1,0:T(8,128)S(1)} %get-tuple-element.16.own, f32[16,32,128]{2,1,0:T(8,128)S(1)} %collective-permute-done.4.below, f32[16,32,128]{2,1,0:T(8,128)S(1)} %collective-permute-done.5.above, ...), custom_call_target="tpu_custom_call" | custom-call | tf_op jit(solution)/shard_map/stream/pallas_call | solution.py:478
  (1 shorter events, 0.0 us)
Async XLA Ops:
  52.3 1.3 %copy-start = (f32[32,19,512]{2,0,1:T(8,128)S(1)}, f32[32,19,512]{2,0,1:T(8,128)}, u32[]{:S(2)}) copy-start(f32[32,19,512]{2,0,1:T(8,128)} %param.7) | copy-start | bytes 3735556
  52.3 1.3 %copy-start.1 = (s32[32,6]{0,1:T(8,128)S(1)}, s32[32,6]{0,1:T(8,128)}, u32[]{:S(2)}) copy-start(s32[32,6]{0,1:T(8,128)} %param.8) | copy-start | bytes 2308
  56.8 9.6 %collective-permute-start.2 = (f32[16,32,128]{2,1,0:T(8,128)S(1)}, f32[16,32,128]{2,1,0:T(8,128)S(1)}, u32[]{:S(2)}, u32[]{:S(2)}) collective-permute-start(f32[16,32,128]{2,1,0:T(8,128)S(1)} %get-tuple-element.15.mine), channel_id=1, source_target_pairs={{0,120},{8,0},{16,8},{24,16},{32,24},{40,32},{48,40},{56,48},{64,5... | collective-permute-start | bytes 786440 | tf_op jit(solution)/shard_map/ppermute | solution.py:490
  58.2 10.6 %collective-permute-start.1 = (f32[16,32,128]{2,1,0:T(8,128)S(1)}, f32[16,32,128]{2,1,0:T(8,128)S(1)}, u32[]{:S(2)}, u32[]{:S(2)}) collective-permute-start(f32[16,32,128]{2,1,0:T(8,128)S(1)} %get-tuple-element.15.mine), channel_id=1, source_target_pairs={{0,8},{8,16},{16,24},{24,32},{32,40},{40,48},{48,56},{56,64},{64,7... | collective-permute-start | bytes 786440 | tf_op jit(solution)/shard_map/ppermute | solution.py:490
  58.3 5.7 %collective-permute-start.3 = (f32[1,32,128]{2,1,0:T(8,128)S(1)}, f32[1,32,128]{2,1,0:T(8,128)S(1)}, u32[]{:S(2)}, u32[]{:S(2)}) collective-permute-start(f32[1,32,128]{2,1,0:T(8,128)S(1)} %slice.3), channel_id=1, source_target_pairs={{0,112},{8,120},{16,0},{24,8},{32,16},{40,24},{48,32},{56,40},{64,... | collective-permute-start | bytes 49160 | tf_op jit(solution)/shard_map/ppermute | solution.py:490
  59.8 6.6 %collective-permute-start = (f32[1,32,128]{2,1,0:T(8,128)S(1)}, f32[1,32,128]{2,1,0:T(8,128)S(1)}, u32[]{:S(2)}, u32[]{:S(2)}) collective-permute-start(f32[1,32,128]{2,1,0:T(8,128)S(1)} %slice.3), channel_id=1, source_target_pairs={{0,16},{8,24},{16,32},{24,40},{32,48},{40,56},{48,64},{56,72},{64,... | collective-permute-start | bytes 49160 | tf_op jit(solution)/shard_map/ppermute | solution.py:490
  69.6 8.6 %collective-permute-start.4 = (f32[16,32,128]{2,1,0:T(8,128)S(1)}, f32[16,32,128]{2,1,0:T(8,128)S(1)}, u32[]{:S(2)}, u32[]{:S(2)}) collective-permute-start(f32[16,32,128]{2,1,0:T(8,128)S(1)} %get-tuple-element.17), channel_id=1, source_target_pairs={{0,1},{1,2},{2,3},{3,4},{4,5},{5,6},{6,7},{7,0},{8,9},{9,10},{10,1... | collective-permute-start | bytes 786440 | tf_op jit(solution)/shard_map/ppermute | solution.py:490
  71.5 6.8 %collective-permute-start.5 = (f32[16,32,128]{2,1,0:T(8,128)S(1)}, f32[16,32,128]{2,1,0:T(8,128)S(1)}, u32[]{:S(2)}, u32[]{:S(2)}) collective-permute-start(f32[16,32,128]{2,1,0:T(8,128)S(1)} %get-tuple-element.18), channel_id=1, source_target_pairs={{0,7},{1,0},{2,1},{3,2},{4,3},{5,4},{6,5},{7,6},{8,15},{9,8},{10,9... | collective-permute-start | bytes 786440 | tf_op jit(solution)/shard_map/ppermute | solution.py:490
  71.7 6.6 %collective-permute-start.6 = (f32[1,32,128]{2,1,0:T(8,128)S(1)}, f32[1,32,128]{2,1,0:T(8,128)S(1)}, u32[]{:S(2)}, u32[]{:S(2)}) collective-permute-start(f32[1,32,128]{2,1,0:T(8,128)S(1)} %get-tuple-element.19), channel_id=1, source_target_pairs={{0,2},{1,3},{2,4},{3,5},{4,6},{5,7},{6,0},{7,1},{8,10},{9,11},{10,... | collective-permute-start | bytes 49160 | tf_op jit(solution)/shard_map/ppermute | solution.py:490
  71.8 6.4 %collective-permute-start.7 = (f32[1,32,128]{2,1,0:T(8,128)S(1)}, f32[1,32,128]{2,1,0:T(8,128)S(1)}, u32[]{:S(2)}, u32[]{:S(2)}) collective-permute-start(f32[1,32,128]{2,1,0:T(8,128)S(1)} %get-tuple-element.20), channel_id=1, source_target_pairs={{0,6},{1,7},{2,0},{3,1},{4,2},{5,3},{6,4},{7,5},{8,14},{9,15},{10,... | collective-permute-start | bytes 49160 | tf_op jit(solution)/shard_map/ppermute | solution.py:490

commit v4 on v3

--- a/solution.py
+++ b/solution.py
@@ -51,7 +51,7 @@
     for r in range(0, nv, 128):
         ids = lax.broadcasted_iota(i32, (128, tri.shape[1]), 0) + r
         hit = (ids == tri[0:1, :]) | (ids == tri[1:2, :]) | (ids == tri[2:3, :])
-        st[r : r + 128, :] = hit.astype(f32).astype(bf16)
+        st[r : r + 128, :] = hit.astype(f32).astype(jnp.float8_e4m3fn)
     links = nt_dot(st[...], st[...])
     for c in copies[1:]:
         c.wait()
@@ -71,10 +71,16 @@
     x_hi = x.astype(bf16)
     x_lo = (x - x_hi.astype(f32)).astype(bf16)
     most = jnp.dot(jnp.concatenate([x_hi, x_lo], axis=0), s_hi, preferred_element_type=f32)
-    rest = jnp.dot(x_hi, s_lo, preferred_element_type=f32)
     for d in range(3):
         lo, hi = d * cells, (d + 1) * cells
-        force[d] = most[lo:hi] + most[3 * cells + lo : 3 * cells + hi] + rest[lo:hi]
+        force[d] = most[lo:hi] + most[3 * cells + lo : 3 * cells + hi]
+
+    @pl.when(jnp.max(jnp.abs(springs)) > 256.0)
+    def _():
+        rest = jnp.dot(x_hi, s_lo, preferred_element_type=f32)
+        for d in range(3):
+            force[d] = force[d] + rest[d * cells : (d + 1) * cells]
+
     sub = lax.broadcasted_iota(i32, (8, 128), 0)
     lane = lax.broadcasted_iota(i32, (8, 128), 1)
     slots = out.shape[0]
@@ -180,7 +186,7 @@
             pltpu.VMEM((3, triangles.shape[0]), i32),
             pltpu.VMEM((6, 32), i32),
             pltpu.SemaphoreType.DMA((6,)),
-            pltpu.VMEM((nv, triangles.shape[0]), bf16),
+            pltpu.VMEM((nv, triangles.shape[0]), jnp.float8_e4m3fn),
             pltpu.VMEM((3, cells, nv), f32),
             pltpu.VMEM((3, cells, nv), f32),
             pltpu.VMEM((16, 24, 128), f32),
@@ -195,11 +201,16 @@
     return jnp.take_along_axis(x, index, axis=1)
 
 
+def column(got, tile):
+    tiles = WIDE // 128
+    return got[pl.ds(tile, got.shape[0] // tiles, stride=tiles), :]
+
+
 def find(near, got, square):
     square[...] = jnp.full((128, 128), -1.0, f32)
     square[0:6, 0:32] = near[...].astype(f32)
     goal = jnp.transpose(square[...])[0:32]
-    known = got[:, 3200:3328]
+    known = column(got, 25)
     k_hi = known.astype(bf16)
     k_lo = (known - k_hi.astype(f32)).astype(bf16)
     lane = lax.broadcasted_iota(i32, (32, 128), 1)
@@ -218,10 +229,10 @@
 
 
 def collide_kernel(near, got, pops, post, table, goal, body, square):
-    slots = got.shape[0]
+    slots = got.shape[0] * 128 // WIDE
     goal[...] = find(near, got, square)
     lane = lax.broadcasted_iota(i32, (slots, 128), 1)
-    ids = got[:, 3072:3200]
+    ids = column(got, 24)
     picks = []
     for r in range(2):
         col = jnp.broadcast_to(ids[:, r : r + 1], (slots, 128))
@@ -230,7 +241,7 @@
     for n in range(3):
         total = jnp.zeros((32, 512), f32)
         for r in range(2):
-            part = got[:, r * 1536 + n * 512 : r * 1536 + (n + 1) * 512]
+            part = jnp.concatenate([column(got, 12 * r + 4 * n + a) for a in range(4)], axis=1)
             hi = part.astype(bf16)
             lo = (part - hi.astype(f32)).astype(bf16)
             total = total + jnp.dot(picks[r], hi, preferred_element_type=f32)
@@ -313,7 +324,7 @@
         table[EDGE_TILE, rows, :] = line
         return carry
 
-    lax.fori_loop(0, 4, group, 0)
+    lax.fori_loop(0, 4, group, 0, unroll=True)
 
 
 def collide(got, populations, neighbours):
@@ -502,7 +513,7 @@
     devices = lax.axis_size("gx") * lax.axis_size("gy")
     slots = spread(cell_owner[:, 0], cell_block, positions, stiffness, triangles, neighbours, devices)
     got = lax.all_to_all(slots, BOTH, split_axis=0, concat_axis=0, tiled=True)
-    post, table, goal = collide(got.reshape(devices, WIDE), populations, neighbours)
+    post, table, goal = collide(got.reshape(-1, 128), populations, neighbours)
     result = stream(goal, post, *exchange(table))
     return jnp.transpose(result, (1, 0, 2))
 

time: 81.5 us -> 78.6 us (0.964)
  Pallas kernels: 22 us -> 20.4 us
  local copies, waits for them, and re-layouts: 1.29 us -> 0.01 us
    unnamed x5 -> x4, local copies, waits for them, and re-layouts: 1.29 us -> 0.01 us
    pallas_call x1, Pallas kernels: 14.9 us -> 13.7 us  [spread(): pl.pallas_call(spread_kernel, out_shape=jax.ShapeDtypeStruct((devices, 1,...]
where the time goes in v4:
time: 78.6 us; the launch traced here: 78.5 us
  blocking collectives  37.4 us (48%)
  Pallas kernels  20.4 us (26%)
  waiting for transfers between devices  11.4 us (15%)
  starting transfers between devices  9.23 us (12%)
    all_to_all x1, blocking collectives, body(): got = lax.all_to_all(slots, BOTH, split_axis=0, concat_axis=0, tiled=True)  37.4 us
    pallas_call x1, Pallas kernels, spread(): pl.pallas_call(spread_kernel, out_shape=jax.ShapeDtypeStruct((devices, 1,...  13.7 us
    ppermute x8, waiting for transfers between devices, send(): lax.ppermute(array, axis, [(i, (i + step) % size) for i in range(size)])  11.4 us
    ppermute x8, starting transfers between devices, send(): lax.ppermute(array, axis, [(i, (i + step) % size) for i in range(size)])  9.23 us
    pallas_call x1, Pallas kernels, stream(): pl.pallas_call(stream_kernel, out_shape=jax.ShapeDtypeStruct((19, 32, 512...  3.05 us
    pallas_call x1, Pallas kernels, collide(): pl.pallas_call(collide_kernel, out_shape=(jax.ShapeDtypeStruct((19, 32, 5...  2.81 us
  transfers between devices with their start and end apart: 8, of which 4 were waited for; matrix products, arithmetic and copies ran while one was open for 0% of the time, Pallas kernels for 0%

profile of v4, /device:TPU:1, one launch (start us, length us, event | category | flops | bytes accessed | tf_op | source)
XLA Modules:
  0.0 78.5 jit_solution(7173874348328341185)
XLA Ops:
  0.0 13.7 %spread.1 = f32[128,1,3328]{2,1,0:T(1,128)S(1)} custom-call(s32[128]{0:T(128)} %bitcast.13, s32[128]{0:T(128)} %block_in.1, f32[128]{0:T(128)} %stiff_in.1, f32[3,642,128]{2,1,0:T(8,128)} %bitcast.11, s32[3,1280]{1,0:T(4,128)} %bitcast.12, s32[6,32]{1,0:T(8,128)} %bitcast.9), custom_call_target="tpu_custom_call" | custom-call | tf_op jit(solution)/shard_map/spread/pallas_call | solution.py:176
  13.7 0.0 copy-start
  13.7 0.0 copy-start.1
  13.7 37.4 %all_to_all.5 = f32[128,1,3328]{2,1,0:T(1,128)S(1)} all-to-all(f32[128,1,3328]{2,1,0:T(1,128)S(1)} %spread.1), channel_id=1, replica_groups=mesh['gx'=16,'gy'=8] {'gx','gy'}, dimensions={0} | all-to-all | bytes 3407872 | tf_op jit(solution)/shard_map/all_to_all | solution.py:515
  51.1 0.0 copy-done
  51.1 0.0 copy-done.1
  51.1 2.8 %collide.1 = (f32[19,32,512]{2,1,0:T(8,128)S(1)}, f32[16,32,128]{2,1,0:T(8,128)S(1)}, f32[32,128]{1,0:T(8,128)S(1)}) custom-call(s32[6,32]{1,0:T(8,128)S(1)} %bitcast.10, f32[3328,128]{1,0:T(8,128)S(1)} %bitcast.7, f32[19,32,512]{2,1,0:T(8,128)S(1)} %bitcast.8), custom_call_target="tpu_custom_call" | custom-call | tf_op jit(solution)/shard_map/collide/pallas_call | solution.py:332
  53.9 1.4 %collective-permute-start.2 = (f32[16,32,128]{2,1,0:T(8,128)S(1)}, f32[16,32,128]{2,1,0:T(8,128)S(1)}, u32[]{:S(2)}, u32[]{:S(2)}) collective-permute-start(f32[16,32,128]{2,1,0:T(8,128)S(1)} %get-tuple-element.15.mine), channel_id=1, source_target_pairs={{0,120},{8,0},{16,8},{24,16},{32,24},{40,32},{48,40},{56,48},{64,5... | collective-permute-start | bytes 786440 | tf_op jit(solution)/shard_map/ppermute | solution.py:501
  55.3 0.1 collective-permute-start.1
  55.5 1.5 %collective-permute-start.3 = (f32[1,32,128]{2,1,0:T(8,128)S(1)}, f32[1,32,128]{2,1,0:T(8,128)S(1)}, u32[]{:S(2)}, u32[]{:S(2)}) collective-permute-start(f32[1,32,128]{2,1,0:T(8,128)S(1)} %slice.3), channel_id=1, source_target_pairs={{0,112},{8,120},{16,0},{24,8},{32,16},{40,24},{48,32},{56,40},{64,... | collective-permute-start | bytes 49160 | tf_op jit(solution)/shard_map/ppermute | solution.py:501
  56.9 1.5 %collective-permute-start = (f32[1,32,128]{2,1,0:T(8,128)S(1)}, f32[1,32,128]{2,1,0:T(8,128)S(1)}, u32[]{:S(2)}, u32[]{:S(2)}) collective-permute-start(f32[1,32,128]{2,1,0:T(8,128)S(1)} %slice.3), channel_id=1, source_target_pairs={{0,16},{8,24},{16,32},{24,40},{32,48},{40,56},{48,64},{56,72},{64,... | collective-permute-start | bytes 49160 | tf_op jit(solution)/shard_map/ppermute | solution.py:501
  58.4 2.7 %collective-permute-done.3.right2 = f32[1,32,128]{2,1,0:T(8,128)S(1)} collective-permute-done((f32[1,32,128]{2,1,0:T(8,128)S(1)}, f32[1,32,128]{2,1,0:T(8,128)S(1)}, u32[]{:S(2)}, u32[]{:S(2)}) %collective-permute-start.3) | collective-permute-done | bytes 16416 | tf_op jit(solution)/shard_map/ppermute | solution.py:501
  61.1 2.4 %collective-permute-done.left2 = f32[1,32,128]{2,1,0:T(8,128)S(1)} collective-permute-done((f32[1,32,128]{2,1,0:T(8,128)S(1)}, f32[1,32,128]{2,1,0:T(8,128)S(1)}, u32[]{:S(2)}, u32[]{:S(2)}) %collective-permute-start) | collective-permute-done | bytes 16416 | tf_op jit(solution)/shard_map/ppermute | solution.py:501
  63.5 0.0 collective-permute-done.2.right
  63.5 2.4 %collective-permute-done.1.left = f32[16,32,128]{2,1,0:T(8,128)S(1)} collective-permute-done((f32[16,32,128]{2,1,0:T(8,128)S(1)}, f32[16,32,128]{2,1,0:T(8,128)S(1)}, u32[]{:S(2)}, u32[]{:S(2)}) %collective-permute-start.1) | collective-permute-done | bytes 262176 | tf_op jit(solution)/shard_map/ppermute | solution.py:501
  65.9 0.9 %route.1 = (f32[16,32,128]{2,1,0:T(8,128)S(1)}, f32[16,32,128]{2,1,0:T(8,128)S(1)}, f32[16,32,128]{2,1,0:T(8,128)S(1)}, f32[1,32,128]{2,1,0:T(8,128)S(1)}, f32[1,32,128]{2,1,0:T(8,128)S(1)}) custom-call(f32[1,32,128]{2,1,0:T(8,128)S(1)} %collective-permute-done.left2, f32[16,32,128]{2,1,0:T(8,128)S(1)} %collective-permute-done.1.left, ...), custom_call_target="tpu_custom_call" | custom-call | tf_op jit(solution)/shard_map/route/pallas_call | solution.py:408
  66.8 1.9 %collective-permute-start.4 = (f32[16,32,128]{2,1,0:T(8,128)S(1)}, f32[16,32,128]{2,1,0:T(8,128)S(1)}, u32[]{:S(2)}, u32[]{:S(2)}) collective-permute-start(f32[16,32,128]{2,1,0:T(8,128)S(1)} %get-tuple-element.17), channel_id=1, source_target_pairs={{0,1},{1,2},{2,3},{3,4},{4,5},{5,6},{6,7},{7,0},{8,9},{9,10},{10,1... | collective-permute-start | bytes 786440 | tf_op jit(solution)/shard_map/ppermute | solution.py:501
  68.7 0.2 collective-permute-start.5
  68.8 0.1 collective-permute-start.6
  69.0 2.5 %collective-permute-start.7 = (f32[1,32,128]{2,1,0:T(8,128)S(1)}, f32[1,32,128]{2,1,0:T(8,128)S(1)}, u32[]{:S(2)}, u32[]{:S(2)}) collective-permute-start(f32[1,32,128]{2,1,0:T(8,128)S(1)} %get-tuple-element.20), channel_id=1, source_target_pairs={{0,6},{1,7},{2,0},{3,1},{4,2},{5,3},{6,4},{7,5},{8,14},{9,15},{10,... | collective-permute-start | bytes 49160 | tf_op jit(solution)/shard_map/ppermute | solution.py:501
  71.5 3.9 %collective-permute-done.6.below2 = f32[1,32,128]{2,1,0:T(8,128)S(1)} collective-permute-done((f32[1,32,128]{2,1,0:T(8,128)S(1)}, f32[1,32,128]{2,1,0:T(8,128)S(1)}, u32[]{:S(2)}, u32[]{:S(2)}) %collective-permute-start.6) | collective-permute-done | bytes 16416 | tf_op jit(solution)/shard_map/ppermute | solution.py:501
  75.4 0.0 collective-permute-done.7.above2
  75.4 0.0 collective-permute-done.4.below
  75.4 0.0 collective-permute-done.5.above
  75.4 3.0 %stream.1 = f32[19,32,512]{2,1,0:T(8,128)} custom-call(f32[32,128]{1,0:T(8,128)S(1)} %get-tuple-element.13.goal, f32[19,32,512]{2,1,0:T(8,128)S(1)} %get-tuple-element.14.post, f32[16,32,128]{2,1,0:T(8,128)S(1)} %get-tuple-element.16.own, f32[16,32,128]{2,1,0:T(8,128)S(1)} %collective-permute-done.4.below, f32[16,32,128]{2,1,0:T(8,128)S(1)} %collective-permute-done.5.above, ...), custom_call_target="tpu_custom_call" | custom-call | tf_op jit(solution)/shard_map/stream/pallas_call | solution.py:489
  (1 shorter events, 0.0 us)
Async XLA Ops:
  13.7 37.4 %copy-start = (f32[32,19,512]{2,0,1:T(8,128)S(1)}, f32[32,19,512]{2,0,1:T(8,128)}, u32[]{:S(2)}) copy-start(f32[32,19,512]{2,0,1:T(8,128)} %param.7) | copy-start | bytes 3735556
  13.7 37.4 %copy-start.1 = (s32[32,6]{0,1:T(8,128)S(1)}, s32[32,6]{0,1:T(8,128)}, u32[]{:S(2)}) copy-start(s32[32,6]{0,1:T(8,128)} %param.8) | copy-start | bytes 2308
  53.9 9.6 %collective-permute-start.2 = (f32[16,32,128]{2,1,0:T(8,128)S(1)}, f32[16,32,128]{2,1,0:T(8,128)S(1)}, u32[]{:S(2)}, u32[]{:S(2)}) collective-permute-start(f32[16,32,128]{2,1,0:T(8,128)S(1)} %get-tuple-element.15.mine), channel_id=1, source_target_pairs={{0,120},{8,0},{16,8},{24,16},{32,24},{40,32},{48,40},{56,48},{64,5... | collective-permute-start | bytes 786440 | tf_op jit(solution)/shard_map/ppermute | solution.py:501
  55.3 10.6 %collective-permute-start.1 = (f32[16,32,128]{2,1,0:T(8,128)S(1)}, f32[16,32,128]{2,1,0:T(8,128)S(1)}, u32[]{:S(2)}, u32[]{:S(2)}) collective-permute-start(f32[16,32,128]{2,1,0:T(8,128)S(1)} %get-tuple-element.15.mine), channel_id=1, source_target_pairs={{0,8},{8,16},{16,24},{24,32},{32,40},{40,48},{48,56},{56,64},{64,7... | collective-permute-start | bytes 786440 | tf_op jit(solution)/shard_map/ppermute | solution.py:501
  55.5 5.6 %collective-permute-start.3 = (f32[1,32,128]{2,1,0:T(8,128)S(1)}, f32[1,32,128]{2,1,0:T(8,128)S(1)}, u32[]{:S(2)}, u32[]{:S(2)}) collective-permute-start(f32[1,32,128]{2,1,0:T(8,128)S(1)} %slice.3), channel_id=1, source_target_pairs={{0,112},{8,120},{16,0},{24,8},{32,16},{40,24},{48,32},{56,40},{64,... | collective-permute-start | bytes 49160 | tf_op jit(solution)/shard_map/ppermute | solution.py:501
  56.9 6.6 %collective-permute-start = (f32[1,32,128]{2,1,0:T(8,128)S(1)}, f32[1,32,128]{2,1,0:T(8,128)S(1)}, u32[]{:S(2)}, u32[]{:S(2)}) collective-permute-start(f32[1,32,128]{2,1,0:T(8,128)S(1)} %slice.3), channel_id=1, source_target_pairs={{0,16},{8,24},{16,32},{24,40},{32,48},{40,56},{48,64},{56,72},{64,... | collective-permute-start | bytes 49160 | tf_op jit(solution)/shard_map/ppermute | solution.py:501
  66.8 8.6 %collective-permute-start.4 = (f32[16,32,128]{2,1,0:T(8,128)S(1)}, f32[16,32,128]{2,1,0:T(8,128)S(1)}, u32[]{:S(2)}, u32[]{:S(2)}) collective-permute-start(f32[16,32,128]{2,1,0:T(8,128)S(1)} %get-tuple-element.17), channel_id=1, source_target_pairs={{0,1},{1,2},{2,3},{3,4},{4,5},{5,6},{6,7},{7,0},{8,9},{9,10},{10,1... | collective-permute-start | bytes 786440 | tf_op jit(solution)/shard_map/ppermute | solution.py:501
  68.7 6.8 %collective-permute-start.5 = (f32[16,32,128]{2,1,0:T(8,128)S(1)}, f32[16,32,128]{2,1,0:T(8,128)S(1)}, u32[]{:S(2)}, u32[]{:S(2)}) collective-permute-start(f32[16,32,128]{2,1,0:T(8,128)S(1)} %get-tuple-element.18), channel_id=1, source_target_pairs={{0,7},{1,0},{2,1},{3,2},{4,3},{5,4},{6,5},{7,6},{8,15},{9,8},{10,9... | collective-permute-start | bytes 786440 | tf_op jit(solution)/shard_map/ppermute | solution.py:501
  68.8 6.6 %collective-permute-start.6 = (f32[1,32,128]{2,1,0:T(8,128)S(1)}, f32[1,32,128]{2,1,0:T(8,128)S(1)}, u32[]{:S(2)}, u32[]{:S(2)}) collective-permute-start(f32[1,32,128]{2,1,0:T(8,128)S(1)} %get-tuple-element.19), channel_id=1, source_target_pairs={{0,2},{1,3},{2,4},{3,5},{4,6},{5,7},{6,0},{7,1},{8,10},{9,11},{10,... | collective-permute-start | bytes 49160 | tf_op jit(solution)/shard_map/ppermute | solution.py:501
  69.0 6.4 %collective-permute-start.7 = (f32[1,32,128]{2,1,0:T(8,128)S(1)}, f32[1,32,128]{2,1,0:T(8,128)S(1)}, u32[]{:S(2)}, u32[]{:S(2)}) collective-permute-start(f32[1,32,128]{2,1,0:T(8,128)S(1)} %get-tuple-element.20), channel_id=1, source_target_pairs={{0,6},{1,7},{2,0},{3,1},{4,2},{5,3},{6,4},{7,5},{8,14},{9,15},{10,... | collective-permute-start | bytes 49160 | tf_op jit(solution)/shard_map/ppermute | solution.py:501

commit v5 on v4

--- a/solution.py
+++ b/solution.py
@@ -198,7 +198,7 @@
 
 
 def lane_take(x, index):
-    return jnp.take_along_axis(x, index, axis=1)
+    return jnp.take_along_axis(x, index, axis=1, mode="promise_in_bounds")
 
 
 def column(got, tile):
@@ -223,14 +223,14 @@
             d1, d2 = [d for d in range(3) if vel[q][d]]
             if f1 == 2 * d1 + (1 if vel[q][d1] == 1 else 0):
                 f2 = 2 * d2 + (1 if vel[q][d2] == 1 else 0)
-                second = jnp.take_along_axis(rows, (f2 - 2) * 32 + lax.bitwise_and(safe, 31), axis=1)
+                second = lane_take(rows, (f2 - 2) * 32 + lax.bitwise_and(safe, 31))
                 goal = jnp.where(lane == 6 + n, jnp.where(first >= 0, second, -1.0), goal)
     return goal
 
 
 def collide_kernel(near, got, pops, post, table, goal, body, square):
     slots = got.shape[0] * 128 // WIDE
-    goal[...] = find(near, got, square)
+    found = find(near, got, square)
     lane = lax.broadcasted_iota(i32, (slots, 128), 1)
     ids = column(got, 24)
     picks = []
@@ -288,12 +288,11 @@
                 post[q + 1, rows, cut] = keep * f[q + 1] + (even - odd)
         for n in range(5):
             table[n, rows, :] = jnp.where(low, post[NEG[0][n], rows, 0:128], post[POS[0][n], rows, 384:512])
-            m = lanes % 64
-            first, second = m // 8, m % 8
+            first, second = (lanes >> 3) & 7, lanes & 7
             for ax in (1, 2):
                 picked = None
                 for a in range(4):
-                    inside = (first % 2) * 64
+                    inside = (first & 1) * 64
                     if ax == 1:
                         at_low, at_high = inside + second, inside + 56 + second
                     else:
@@ -302,14 +301,14 @@
                     val = jnp.where(
                         low, lane_take(post[NEG[ax][n], rows, cut], at_low), lane_take(post[POS[ax][n], rows, cut], at_high)
                     )
-                    picked = val if picked is None else jnp.where(first // 2 == a, val, picked)
+                    picked = val if picked is None else jnp.where(first >> 1 == a, val, picked)
                 table[5 * ax + n, rows, :] = picked
-        line = jnp.where(lanes < HAVE, pltpu.roll(goal[rows, :], IDS, 1), 1.0)
-        w = lanes % 8
+        line = jnp.ones((8, 128), f32)
+        w = lanes & 7
         for n, q in enumerate(EDGE_Q):
             ex, ey, ez = vel[q]
             at = [7 if e == 1 else 0 for e in vel[q]]
-            mine = lanes // 8 == n
+            mine = lanes >> 3 == n
             if ex:
                 a = 3 if ex == 1 else 0
                 base = 64 if ex == 1 else 0
@@ -317,14 +316,17 @@
                 val = lane_take(post[q, rows, 128 * a : 128 * (a + 1)], where_)
                 line = jnp.where(mine, val, line)
             else:
-                where_ = (w % 2) * 64 + at[1] * 8 + at[2]
+                where_ = (w & 1) * 64 + at[1] * 8 + at[2]
                 for a in range(4):
                     val = lane_take(post[q, rows, 128 * a : 128 * (a + 1)], where_)
-                    line = jnp.where(mine & (w // 2 == a), val, line)
+                    line = jnp.where(mine & (w >> 1 == a), val, line)
         table[EDGE_TILE, rows, :] = line
         return carry
 
     lax.fori_loop(0, 4, group, 0, unroll=True)
+    goal[...] = found
+    lane = lax.broadcasted_iota(i32, (32, 128), 1)
+    table[EDGE_TILE] = jnp.where((lane >= IDS) & (lane < HAVE), pltpu.roll(found, IDS, 1), table[EDGE_TILE])
 
 
 def collide(got, populations, neighbours):
@@ -394,7 +396,7 @@
             [jnp.concatenate([hot(h, 6 + n, dy) for dy in range(-2, 3)], axis=0) for h in range(2)], axis=1
         ).astype(bf16)
         moved = jnp.dot(picks, both, preferred_element_type=f32)
-        wanted = (lane // 8 == n) | (lane == HAVE + n)
+        wanted = (lane >> 3 == n) | (lane == HAVE + n)
         total = jnp.where(wanted, moved[:, 0:128] + moved[:, 128:256], total)
     for k, goal in enumerate((down2, down, own, up, up2)):
         goal[goal.shape[0] - 1] = total[32 * k : 32 * (k + 1)]
@@ -416,83 +418,126 @@
     )(left2, left, mine, right, right2)
 
 
-def stream_kernel(goal, post, own, below, above, below2, above2, out):
+def crossings(q, a):
     lanes = lax.broadcasted_iota(i32, (8, 128), 1)
-    jj = (lanes // 8) % 8
-    kk = lanes % 8
-
-    def group(g, carry):
-        rows = pl.ds(pl.multiple_of(g * 8, 8), 8)
-        near = goal[rows, :]
-        ghost = []
-        for ax in range(3):
-            have = lane_take(near, jnp.where(lanes < 64, 2 * ax + 1, 2 * ax)) >= 0.0
-            for t in range(5 * ax, 5 * ax + 5):
-                came = own[t, rows, :] + below[t, rows, :] + above[t, rows, :]
-                ghost.append(jnp.where(have, came, jnp.nan))
-        came = own[EDGE_TILE, rows, :] + below[EDGE_TILE, rows, :] + above[EDGE_TILE, rows, :]
-        came = came + below2[0, rows, :] + above2[0, rows, :]
-        have = lane_take(came, jnp.minimum(HAVE + lanes // 8, 127)) > 0.5
-        edges = jnp.where(have, came, jnp.nan)
-        out[0, rows, :] = post[0, rows, :]
+    coords = (2 * a + (lanes >> 6), (lanes >> 3) & 7, lanes & 7)
+    e = vel[q]
+    found = [None if e[d] == 0 else coords[d] == (0 if e[d] == 1 else 7) for d in range(3)]
+    if e[0] == 1 and a != 0 or e[0] == -1 and a != 3:
+        found[0] = None
+    return coords, found, [d for d in range(3) if found[d] is not None]
+
+
+def inside_kernel(post, most):
+    lanes = lax.broadcasted_iota(i32, (8, 128), 1)
+    for g in range(4):
+        rows = slice(8 * g, 8 * g + 8)
+        most[0, rows, :] = post[0, rows, :]
         for q in range(1, 19):
-            e = vel[q]
-            ex, ey, ez = e
+            ex, ey, ez = vel[q]
             shift = ex * 64 + ey * 8 + ez
-            tiles = [post[q, rows, 128 * a : 128 * (a + 1)] for a in range(4)]
-            rolled = [pltpu.roll(t, shift % 128, 1) for t in tiles]
+            rolled = [pltpu.roll(post[q, rows, 128 * a : 128 * (a + 1)], shift % 128, 1) for a in range(4)]
             for a in range(4):
                 if shift > 0:
                     val = jnp.where(lanes < shift, rolled[(a - 1) % 4], rolled[a])
                 else:
                     val = jnp.where(lanes >= 128 + shift, rolled[(a + 1) % 4], rolled[a])
-                ii = 2 * a + lanes // 64
-                back = post[opposite[q], rows, 128 * a : 128 * (a + 1)]
-                coords = (ii, jj, kk)
-                crossing = [None if e[d] == 0 else coords[d] == (0 if e[d] == 1 else 7) for d in range(3)]
-                if ex == 1 and a != 0 or ex == -1 and a != 3:
-                    crossing[0] = None
-                axes = [d for d in range(3) if crossing[d] is not None]
+                coords, crossing, axes = crossings(q, a)
                 if axes:
                     out_of = crossing[axes[0]]
                     for d in axes[1:]:
                         out_of = out_of | crossing[d]
-                    val = jnp.where(out_of, back, val)
+                    val = jnp.where(out_of, post[opposite[q], rows, 128 * a : 128 * (a + 1)], val)
+                most[q, rows, 128 * a : 128 * (a + 1)] = val
+
+
+def inside(post):
+    vmem = pl.BlockSpec(memory_space=pltpu.VMEM)
+    return pl.pallas_call(
+        inside_kernel,
+        out_shape=jax.ShapeDtypeStruct(post.shape, f32),
+        in_specs=[vmem],
+        out_specs=vmem,
+        compiler_params=pltpu.CompilerParams(vmem_limit_bytes=48 << 20),
+        name="inside",
+    )(post)
+
+
+def opened(ax):
+    lane = lax.broadcasted_iota(i32, (128, 512), 0)
+    site = lax.broadcasted_iota(i32, (128, 512), 1)
+    i, j, k = site >> 6, (site >> 3) & 7, site & 7
+    along, across = (k, j) if ax == 1 else (j, k)
+    wanted = jnp.where(lane < 64, 7, 0)
+    return ((i * 8 + along == (lane & 63)) & (across == wanted)).astype(f32).astype(bf16)
+
+
+def ghost_kernel(goal, most, own, below, above, below2, above2, result, out, ghost, sem):
+    lanes = lax.broadcasted_iota(i32, (8, 128), 1)
+    low = lax.broadcasted_iota(i32, (32, 128), 1) < 64
+    for ax in (1, 2):
+        other = 2 if ax == 1 else 1
+        shifted = []
+        for n in range(5):
+            t = 5 * ax + n
+            came = own[t] + below[t] + above[t]
+            steps = [(vel[q][0] * 8 + vel[q][other]) % 128 for q in (NEG[ax][n], POS[ax][n])]
+            both = [pltpu.roll(came, step, 1) if step else came for step in steps]
+            shifted.append(jnp.where(low, both[0], both[1]))
+        planes = jnp.concatenate(shifted, axis=0)
+        p_hi = planes.astype(bf16)
+        p_lo = (planes - p_hi.astype(f32)).astype(bf16)
+        to = opened(ax)
+        ghost[ax - 1] = jnp.dot(p_hi, to, preferred_element_type=f32) + jnp.dot(p_lo, to, preferred_element_type=f32)
+    leaving = []
+    for g in range(4):
+        rows = slice(8 * g, 8 * g + 8)
+        near = goal[rows, :]
+        there = [lane_take(near, jnp.full((8, 128), f, i32)) >= 0.0 for f in range(6)]
+        came = own[EDGE_TILE, rows, :] + below[EDGE_TILE, rows, :] + above[EDGE_TILE, rows, :]
+        came = came + below2[0, rows, :] + above2[0, rows, :]
+        have = lane_take(came, jnp.minimum(HAVE + (lanes >> 3), 127)) > 0.5
+        edges = jnp.where(have, came, jnp.nan)
+        out[0, rows, :] = most[0, rows, :]
+        for q in range(1, 19):
+            e = vel[q]
+            ex, ey, ez = e
+            for a in range(4):
+                val = most[q, rows, 128 * a : 128 * (a + 1)]
+                (ii, jj, kk), crossing, axes = crossings(q, a)
                 for d in axes:
                     n = (POS[d] if e[d] == 1 else NEG[d]).index(q)
-                    source = ghost[5 * d + n]
-                    base = 64 if e[d] == 1 else 0
                     if d == 0:
+                        source = own[n, rows, :] + below[n, rows, :] + above[n, rows, :]
                         brought = pltpu.roll(source, (64 + ey * 8 + ez) % 128, 1)
-                    elif d == 1:
-                        brought = lane_take(source, base + ((ii - ex) * 8 + kk - ez) % 64)
                     else:
-                        brought = lane_take(source, base + ((ii - ex) * 8 + jj - ey) % 64)
-                    use = crossing[d] & (brought == brought)
+                        brought = ghost[d - 1, 32 * n + 8 * g : 32 * n + 8 * g + 8, 128 * a : 128 * (a + 1)]
+                    use = crossing[d] & there[2 * d + (0 if e[d] == 1 else 1)]
                     for other in axes:
                         if other != d:
                             use = use & ~crossing[other]
                     val = jnp.where(use, brought, val)
                 if len(axes) == 2:
-                    n = q - 7
                     along = kk if ez == 0 else (jj if ey == 0 else ii)
-                    brought = lane_take(edges, 8 * n + along)
+                    brought = lane_take(edges, 8 * (q - 7) + along)
                     val = jnp.where(crossing[axes[0]] & crossing[axes[1]] & (brought == brought), brought, val)
                 out[q, rows, 128 * a : 128 * (a + 1)] = val
-        return carry
-
-    lax.fori_loop(0, 4, group, 0)
-
-
-def stream(goal, post, *parts):
+        leaving.append(pltpu.make_async_copy(out.at[:, rows, :], result.at[:, rows, :], sem.at[g]))
+        leaving[-1].start()
+    for c in leaving:
+        c.wait()
+
+
+def fill(goal, post, *parts):
     vmem = pl.BlockSpec(memory_space=pltpu.VMEM)
     return pl.pallas_call(
-        stream_kernel,
+        ghost_kernel,
         out_shape=jax.ShapeDtypeStruct((19, 32, 512), f32),
         in_specs=[vmem] * 7,
-        out_specs=vmem,
+        out_specs=pl.BlockSpec(memory_space=pltpu.HBM),
+        scratch_shapes=[pltpu.VMEM(post.shape, f32), pltpu.VMEM((2, 160, 512), f32), pltpu.SemaphoreType.DMA((4,))],
         compiler_params=pltpu.CompilerParams(vmem_limit_bytes=48 << 20),
-        name="stream",
+        name="fill",
     )(goal, post, *parts)
 
 
@@ -514,7 +559,7 @@
     slots = spread(cell_owner[:, 0], cell_block, positions, stiffness, triangles, neighbours, devices)
     got = lax.all_to_all(slots, BOTH, split_axis=0, concat_axis=0, tiled=True)
     post, table, goal = collide(got.reshape(-1, 128), populations, neighbours)
-    result = stream(goal, post, *exchange(table))
+    result = fill(goal, inside(post), *exchange(table))
     return jnp.transpose(result, (1, 0, 2))
 
 

time: 78.6 us -> 77.3 us (0.983)
  Pallas kernels: 20.4 us -> 19.4 us
    pallas_call x1 -> x2, Pallas kernels: 3.05 us -> 2.09 us  [the longest x1 1.72 us: fill(): pl.pallas_call(ghost_kernel, out_shape=jax.ShapeDtypeStruct((19, 32, 512)...]
where the time goes in v5:
time: 77.3 us; the launch traced here: 77.1 us
  blocking collectives  37.4 us (48%)
  Pallas kernels  19.4 us (25%)
  waiting for transfers between devices  11 us (14%)
  starting transfers between devices  9.23 us (12%)
    all_to_all x1, blocking collectives, body(): got = lax.all_to_all(slots, BOTH, split_axis=0, concat_axis=0, tiled=True)  37.4 us
    pallas_call x1, Pallas kernels, spread(): pl.pallas_call(spread_kernel, out_shape=jax.ShapeDtypeStruct((devices, 1,...  13.7 us
    ppermute x8, waiting for transfers between devices, send(): lax.ppermute(array, axis, [(i, (i + step) % size) for i in range(size)])  11 us
    ppermute x8, starting transfers between devices, send(): lax.ppermute(array, axis, [(i, (i + step) % size) for i in range(size)])  9.23 us
    pallas_call x1, Pallas kernels, collide(): pl.pallas_call(collide_kernel, out_shape=(jax.ShapeDtypeStruct((19, 32, 5...  2.78 us
    pallas_call x1, Pallas kernels, fill(): pl.pallas_call(ghost_kernel, out_shape=jax.ShapeDtypeStruct((19, 32, 512)...  1.72 us
  transfers between devices with their start and end apart: 8, of which 4 were waited for; matrix products, arithmetic and copies ran while one was open for 0% of the time, Pallas kernels for 0%

profile of v5, /device:TPU:1, one launch (start us, length us, event | category | flops | bytes accessed | tf_op | source)
XLA Modules:
  0.0 77.1 jit_solution(17827732474097995922)
XLA Ops:
  0.0 13.7 %spread.1 = f32[128,1,3328]{2,1,0:T(1,128)S(1)} custom-call(s32[128]{0:T(128)} %bitcast.13, s32[128]{0:T(128)} %block_in.1, f32[128]{0:T(128)} %stiff_in.1, f32[3,642,128]{2,1,0:T(8,128)} %bitcast.11, s32[3,1280]{1,0:T(4,128)} %bitcast.12, s32[6,32]{1,0:T(8,128)} %bitcast.9), custom_call_target="tpu_custom_call" | custom-call | tf_op jit(solution)/shard_map/spread/pallas_call | solution.py:176
  13.7 0.0 copy-start
  13.7 0.0 copy-start.1
  13.7 37.4 %all_to_all.5 = f32[128,1,3328]{2,1,0:T(1,128)S(1)} all-to-all(f32[128,1,3328]{2,1,0:T(1,128)S(1)} %spread.1), channel_id=1, replica_groups=mesh['gx'=16,'gy'=8] {'gx','gy'}, dimensions={0} | all-to-all | bytes 3407872 | tf_op jit(solution)/shard_map/all_to_all | solution.py:560
  51.1 0.0 copy-done
  51.1 0.0 copy-done.1
  51.1 2.8 %collide.1 = (f32[19,32,512]{2,1,0:T(8,128)S(1)}, f32[16,32,128]{2,1,0:T(8,128)S(1)}, f32[32,128]{1,0:T(8,128)S(1)}) custom-call(s32[6,32]{1,0:T(8,128)S(1)} %bitcast.10, f32[3328,128]{1,0:T(8,128)S(1)} %bitcast.7, f32[19,32,512]{2,1,0:T(8,128)S(1)} %bitcast.8), custom_call_target="tpu_custom_call" | custom-call | tf_op jit(solution)/shard_map/collide/pallas_call | solution.py:334
  53.9 1.4 %collective-permute-start.2 = (f32[16,32,128]{2,1,0:T(8,128)S(1)}, f32[16,32,128]{2,1,0:T(8,128)S(1)}, u32[]{:S(2)}, u32[]{:S(2)}) collective-permute-start(f32[16,32,128]{2,1,0:T(8,128)S(1)} %get-tuple-element.15.mine), channel_id=1, source_target_pairs={{0,120},{8,0},{16,8},{24,16},{32,24},{40,32},{48,40},{56,48},{64,5... | collective-permute-start | bytes 786440 | tf_op jit(solution)/shard_map/ppermute | solution.py:546
  55.3 0.1 collective-permute-start.1
  55.4 1.5 %collective-permute-start.3 = (f32[1,32,128]{2,1,0:T(8,128)S(1)}, f32[1,32,128]{2,1,0:T(8,128)S(1)}, u32[]{:S(2)}, u32[]{:S(2)}) collective-permute-start(f32[1,32,128]{2,1,0:T(8,128)S(1)} %slice.3), channel_id=1, source_target_pairs={{0,112},{8,120},{16,0},{24,8},{32,16},{40,24},{48,32},{56,40},{64,... | collective-permute-start | bytes 49160 | tf_op jit(solution)/shard_map/ppermute | solution.py:546
  56.9 1.5 %collective-permute-start = (f32[1,32,128]{2,1,0:T(8,128)S(1)}, f32[1,32,128]{2,1,0:T(8,128)S(1)}, u32[]{:S(2)}, u32[]{:S(2)}) collective-permute-start(f32[1,32,128]{2,1,0:T(8,128)S(1)} %slice.3), channel_id=1, source_target_pairs={{0,16},{8,24},{16,32},{24,40},{32,48},{40,56},{48,64},{56,72},{64,... | collective-permute-start | bytes 49160 | tf_op jit(solution)/shard_map/ppermute | solution.py:546
  58.4 2.7 %collective-permute-done.3.right2 = f32[1,32,128]{2,1,0:T(8,128)S(1)} collective-permute-done((f32[1,32,128]{2,1,0:T(8,128)S(1)}, f32[1,32,128]{2,1,0:T(8,128)S(1)}, u32[]{:S(2)}, u32[]{:S(2)}) %collective-permute-start.3) | collective-permute-done | bytes 16416 | tf_op jit(solution)/shard_map/ppermute | solution.py:546
  61.1 2.4 %collective-permute-done.left2 = f32[1,32,128]{2,1,0:T(8,128)S(1)} collective-permute-done((f32[1,32,128]{2,1,0:T(8,128)S(1)}, f32[1,32,128]{2,1,0:T(8,128)S(1)}, u32[]{:S(2)}, u32[]{:S(2)}) %collective-permute-start) | collective-permute-done | bytes 16416 | tf_op jit(solution)/shard_map/ppermute | solution.py:546
  63.5 0.0 collective-permute-done.2.right
  63.5 2.4 %collective-permute-done.1.left = f32[16,32,128]{2,1,0:T(8,128)S(1)} collective-permute-done((f32[16,32,128]{2,1,0:T(8,128)S(1)}, f32[16,32,128]{2,1,0:T(8,128)S(1)}, u32[]{:S(2)}, u32[]{:S(2)}) %collective-permute-start.1) | collective-permute-done | bytes 262176 | tf_op jit(solution)/shard_map/ppermute | solution.py:546
  65.9 0.9 %route.1 = (f32[16,32,128]{2,1,0:T(8,128)S(1)}, f32[16,32,128]{2,1,0:T(8,128)S(1)}, f32[16,32,128]{2,1,0:T(8,128)S(1)}, f32[1,32,128]{2,1,0:T(8,128)S(1)}, f32[1,32,128]{2,1,0:T(8,128)S(1)}) custom-call(f32[1,32,128]{2,1,0:T(8,128)S(1)} %collective-permute-done.left2, f32[16,32,128]{2,1,0:T(8,128)S(1)} %collective-permute-done.1.left, ...), custom_call_target="tpu_custom_call" | custom-call | tf_op jit(solution)/shard_map/route/pallas_call | solution.py:410
  66.8 1.9 %collective-permute-start.4 = (f32[16,32,128]{2,1,0:T(8,128)S(1)}, f32[16,32,128]{2,1,0:T(8,128)S(1)}, u32[]{:S(2)}, u32[]{:S(2)}) collective-permute-start(f32[16,32,128]{2,1,0:T(8,128)S(1)} %get-tuple-element.17), channel_id=1, source_target_pairs={{0,1},{1,2},{2,3},{3,4},{4,5},{5,6},{6,7},{7,0},{8,9},{9,10},{10,1... | collective-permute-start | bytes 786440 | tf_op jit(solution)/shard_map/ppermute | solution.py:546
  68.6 0.2 collective-permute-start.5
  68.8 0.1 collective-permute-start.6
  69.0 2.5 %collective-permute-start.7 = (f32[1,32,128]{2,1,0:T(8,128)S(1)}, f32[1,32,128]{2,1,0:T(8,128)S(1)}, u32[]{:S(2)}, u32[]{:S(2)}) collective-permute-start(f32[1,32,128]{2,1,0:T(8,128)S(1)} %get-tuple-element.20), channel_id=1, source_target_pairs={{0,6},{1,7},{2,0},{3,1},{4,2},{5,3},{6,4},{7,5},{8,14},{9,15},{10,... | collective-permute-start | bytes 49160 | tf_op jit(solution)/shard_map/ppermute | solution.py:546
  71.5 0.4 inside.1.most
  71.9 3.5 %collective-permute-done.6.below2 = f32[1,32,128]{2,1,0:T(8,128)S(1)} collective-permute-done((f32[1,32,128]{2,1,0:T(8,128)S(1)}, f32[1,32,128]{2,1,0:T(8,128)S(1)}, u32[]{:S(2)}, u32[]{:S(2)}) %collective-permute-start.6) | collective-permute-done | bytes 16416 | tf_op jit(solution)/shard_map/ppermute | solution.py:546
  75.4 0.0 collective-permute-done.7.above2
  75.4 0.0 collective-permute-done.4.below
  75.4 0.0 collective-permute-done.5.above
  75.4 1.7 %fill.1 = f32[19,32,512]{2,1,0:T(8,128)} custom-call(f32[32,128]{1,0:T(8,128)S(1)} %get-tuple-element.13.goal, f32[19,32,512]{2,1,0:T(8,128)S(1)} %inside.1.most, f32[16,32,128]{2,1,0:T(8,128)S(1)} %get-tuple-element.16.own, f32[16,32,128]{2,1,0:T(8,128)S(1)} %collective-permute-done.4.below, f32[16,32,128]{2,1,0:T(8,128)S(1)} %collective-permute-done.5.above, ...), custom_call_target="tpu_custom_call" | custom-call | tf_op jit(solution)/shard_map/fill/pallas_call | solution.py:533
  (1 shorter events, 0.0 us)
Async XLA Ops:
  13.7 37.4 %copy-start = (f32[32,19,512]{2,0,1:T(8,128)S(1)}, f32[32,19,512]{2,0,1:T(8,128)}, u32[]{:S(2)}) copy-start(f32[32,19,512]{2,0,1:T(8,128)} %param.7) | copy-start | bytes 3735556
  13.7 37.4 %copy-start.1 = (s32[32,6]{0,1:T(8,128)S(1)}, s32[32,6]{0,1:T(8,128)}, u32[]{:S(2)}) copy-start(s32[32,6]{0,1:T(8,128)} %param.8) | copy-start | bytes 2308
  53.9 9.6 %collective-permute-start.2 = (f32[16,32,128]{2,1,0:T(8,128)S(1)}, f32[16,32,128]{2,1,0:T(8,128)S(1)}, u32[]{:S(2)}, u32[]{:S(2)}) collective-permute-start(f32[16,32,128]{2,1,0:T(8,128)S(1)} %get-tuple-element.15.mine), channel_id=1, source_target_pairs={{0,120},{8,0},{16,8},{24,16},{32,24},{40,32},{48,40},{56,48},{64,5... | collective-permute-start | bytes 786440 | tf_op jit(solution)/shard_map/ppermute | solution.py:546
  55.3 10.6 %collective-permute-start.1 = (f32[16,32,128]{2,1,0:T(8,128)S(1)}, f32[16,32,128]{2,1,0:T(8,128)S(1)}, u32[]{:S(2)}, u32[]{:S(2)}) collective-permute-start(f32[16,32,128]{2,1,0:T(8,128)S(1)} %get-tuple-element.15.mine), channel_id=1, source_target_pairs={{0,8},{8,16},{16,24},{24,32},{32,40},{40,48},{48,56},{56,64},{64,7... | collective-permute-start | bytes 786440 | tf_op jit(solution)/shard_map/ppermute | solution.py:546
  55.4 5.6 %collective-permute-start.3 = (f32[1,32,128]{2,1,0:T(8,128)S(1)}, f32[1,32,128]{2,1,0:T(8,128)S(1)}, u32[]{:S(2)}, u32[]{:S(2)}) collective-permute-start(f32[1,32,128]{2,1,0:T(8,128)S(1)} %slice.3), channel_id=1, source_target_pairs={{0,112},{8,120},{16,0},{24,8},{32,16},{40,24},{48,32},{56,40},{64,... | collective-permute-start | bytes 49160 | tf_op jit(solution)/shard_map/ppermute | solution.py:546
  56.9 6.6 %collective-permute-start = (f32[1,32,128]{2,1,0:T(8,128)S(1)}, f32[1,32,128]{2,1,0:T(8,128)S(1)}, u32[]{:S(2)}, u32[]{:S(2)}) collective-permute-start(f32[1,32,128]{2,1,0:T(8,128)S(1)} %slice.3), channel_id=1, source_target_pairs={{0,16},{8,24},{16,32},{24,40},{32,48},{40,56},{48,64},{56,72},{64,... | collective-permute-start | bytes 49160 | tf_op jit(solution)/shard_map/ppermute | solution.py:546
  66.8 8.6 %collective-permute-start.4 = (f32[16,32,128]{2,1,0:T(8,128)S(1)}, f32[16,32,128]{2,1,0:T(8,128)S(1)}, u32[]{:S(2)}, u32[]{:S(2)}) collective-permute-start(f32[16,32,128]{2,1,0:T(8,128)S(1)} %get-tuple-element.17), channel_id=1, source_target_pairs={{0,1},{1,2},{2,3},{3,4},{4,5},{5,6},{6,7},{7,0},{8,9},{9,10},{10,1... | collective-permute-start | bytes 786440 | tf_op jit(solution)/shard_map/ppermute | solution.py:546
  68.6 6.8 %collective-permute-start.5 = (f32[16,32,128]{2,1,0:T(8,128)S(1)}, f32[16,32,128]{2,1,0:T(8,128)S(1)}, u32[]{:S(2)}, u32[]{:S(2)}) collective-permute-start(f32[16,32,128]{2,1,0:T(8,128)S(1)} %get-tuple-element.18), channel_id=1, source_target_pairs={{0,7},{1,0},{2,1},{3,2},{4,3},{5,4},{6,5},{7,6},{8,15},{9,8},{10,9... | collective-permute-start | bytes 786440 | tf_op jit(solution)/shard_map/ppermute | solution.py:546
  68.8 6.6 %collective-permute-start.6 = (f32[1,32,128]{2,1,0:T(8,128)S(1)}, f32[1,32,128]{2,1,0:T(8,128)S(1)}, u32[]{:S(2)}, u32[]{:S(2)}) collective-permute-start(f32[1,32,128]{2,1,0:T(8,128)S(1)} %get-tuple-element.19), channel_id=1, source_target_pairs={{0,2},{1,3},{2,4},{3,5},{4,6},{5,7},{6,0},{7,1},{8,10},{9,11},{10,... | collective-permute-start | bytes 49160 | tf_op jit(solution)/shard_map/ppermute | solution.py:546
  69.0 6.4 %collective-permute-start.7 = (f32[1,32,128]{2,1,0:T(8,128)S(1)}, f32[1,32,128]{2,1,0:T(8,128)S(1)}, u32[]{:S(2)}, u32[]{:S(2)}) collective-permute-start(f32[1,32,128]{2,1,0:T(8,128)S(1)} %get-tuple-element.20), channel_id=1, source_target_pairs={{0,6},{1,7},{2,0},{3,1},{4,2},{5,3},{6,4},{7,5},{8,14},{9,15},{10,... | collective-permute-start | bytes 49160 | tf_op jit(solution)/shard_map/ppermute | solution.py:546

commit v6 on v5

--- a/solution.py
+++ b/solution.py
@@ -214,11 +214,14 @@
     k_hi = known.astype(bf16)
     k_lo = (known - k_hi.astype(f32)).astype(bf16)
     lane = lax.broadcasted_iota(i32, (32, 128), 1)
-    for f1 in range(4):
-        first = jnp.broadcast_to(goal[:, f1 : f1 + 1], (32, 128)).astype(i32)
+    firsts = [lane_take(goal, jnp.full((32, 128), f1, i32)).astype(i32) for f1 in range(4)]
+    picks = [(lax.shift_right_logical(jnp.maximum(first, 0), 5) == lane).astype(f32) for first in firsts]
+    found = jnp.dot(
+        jnp.concatenate(picks, axis=0).astype(bf16), jnp.concatenate([k_hi, k_lo], axis=1), preferred_element_type=f32
+    )
+    for f1, first in enumerate(firsts):
         safe = jnp.maximum(first, 0)
-        pick = (lax.shift_right_logical(safe, 5) == lane).astype(f32).astype(bf16)
-        rows = jnp.dot(pick, k_hi, preferred_element_type=f32) + jnp.dot(pick, k_lo, preferred_element_type=f32)
+        rows = found[32 * f1 : 32 * (f1 + 1), 0:128] + found[32 * f1 : 32 * (f1 + 1), 128:256]
         for n, q in enumerate(EDGE_Q):
             d1, d2 = [d for d in range(3) if vel[q][d]]
             if f1 == 2 * d1 + (1 if vel[q][d1] == 1 else 0):
@@ -228,7 +231,7 @@
     return goal
 
 
-def collide_kernel(near, got, pops, post, table, goal, body, square):
+def collide_kernel(near, got, pops, post, table, edge, goal, body, square):
     slots = got.shape[0] * 128 // WIDE
     found = find(near, got, square)
     lane = lax.broadcasted_iota(i32, (slots, 128), 1)
@@ -326,7 +329,9 @@
     lax.fori_loop(0, 4, group, 0, unroll=True)
     goal[...] = found
     lane = lax.broadcasted_iota(i32, (32, 128), 1)
-    table[EDGE_TILE] = jnp.where((lane >= IDS) & (lane < HAVE), pltpu.roll(found, IDS, 1), table[EDGE_TILE])
+    lines = jnp.where((lane >= IDS) & (lane < HAVE), pltpu.roll(found, IDS, 1), table[EDGE_TILE])
+    table[EDGE_TILE] = lines
+    edge[0] = lines
 
 
 def collide(got, populations, neighbours):
@@ -336,10 +341,11 @@
         out_shape=(
             jax.ShapeDtypeStruct((19, 32, 512), f32),
             jax.ShapeDtypeStruct((NT, 32, 128), f32),
+            jax.ShapeDtypeStruct((1, 32, 128), f32),
             jax.ShapeDtypeStruct((32, 128), f32),
         ),
         in_specs=[vmem, vmem, vmem],
-        out_specs=(vmem, vmem, vmem),
+        out_specs=(vmem,) * 4,
         scratch_shapes=[
             pltpu.VMEM((3, 32, 512), f32),
             pltpu.VMEM((128, 128), f32),
@@ -546,8 +552,7 @@
     return lax.ppermute(array, axis, [(i, (i + step) % size) for i in range(size)])
 
 
-def exchange(table):
-    edge = table[EDGE_TILE : EDGE_TILE + 1]
+def exchange(table, edge):
     left, right = send(table, "gx", 1), send(table, "gx", -1)
     left2, right2 = send(edge, "gx", 2), send(edge, "gx", -2)
     down, own, up, down2, up2 = route(left2, left, table, right, right2)
@@ -558,8 +563,8 @@
     devices = lax.axis_size("gx") * lax.axis_size("gy")
     slots = spread(cell_owner[:, 0], cell_block, positions, stiffness, triangles, neighbours, devices)
     got = lax.all_to_all(slots, BOTH, split_axis=0, concat_axis=0, tiled=True)
-    post, table, goal = collide(got.reshape(-1, 128), populations, neighbours)
-    result = fill(goal, inside(post), *exchange(table))
+    post, table, edge, goal = collide(got.reshape(-1, 128), populations, neighbours)
+    result = fill(goal, inside(post), *exchange(table, edge))
     return jnp.transpose(result, (1, 0, 2))
 
 

time: 77.3 us -> 76.8 us (level)
  no operation moved by 1% of the time
where the time goes in v6:
time: 76.8 us; the launch traced here: 76.6 us
  blocking collectives  37.4 us (49%)
  Pallas kernels  18.9 us (25%)
  waiting for transfers between devices  11 us (14%)
  starting transfers between devices  9.22 us (12%)
    all_to_all x1, blocking collectives, body(): got = lax.all_to_all(slots, BOTH, split_axis=0, concat_axis=0, tiled=True)  37.4 us
    pallas_call x1, Pallas kernels, spread(): pl.pallas_call(spread_kernel, out_shape=jax.ShapeDtypeStruct((devices, 1,...  13.7 us
    ppermute x8, waiting for transfers between devices, send(): lax.ppermute(array, axis, [(i, (i + step) % size) for i in range(size)])  11 us
    ppermute x8, starting transfers between devices, send(): lax.ppermute(array, axis, [(i, (i + step) % size) for i in range(size)])  9.22 us
    pallas_call x1, Pallas kernels, collide(): pl.pallas_call(collide_kernel, out_shape=(jax.ShapeDtypeStruct((19, 32, 5...  2.26 us
    pallas_call x1, Pallas kernels, fill(): pl.pallas_call(ghost_kernel, out_shape=jax.ShapeDtypeStruct((19, 32, 512)...  1.72 us
  transfers between devices with their start and end apart: 8, of which 4 were waited for; matrix products, arithmetic and copies ran while one was open for 0% of the time, Pallas kernels for 0%

profile of v6, /device:TPU:1, one launch (start us, length us, event | category | flops | bytes accessed | tf_op | source)
XLA Modules:
  0.0 76.6 jit_solution(11164250176804450108)
XLA Ops:
  0.0 13.7 %spread.1 = f32[128,1,3328]{2,1,0:T(1,128)S(1)} custom-call(s32[128]{0:T(128)} %bitcast.13, s32[128]{0:T(128)} %block_in.1, f32[128]{0:T(128)} %stiff_in.1, f32[3,642,128]{2,1,0:T(8,128)} %bitcast.11, s32[3,1280]{1,0:T(4,128)} %bitcast.12, s32[6,32]{1,0:T(8,128)} %bitcast.9), custom_call_target="tpu_custom_call" | custom-call | tf_op jit(solution)/shard_map/spread/pallas_call | solution.py:176
  13.7 0.0 copy-start
  13.7 0.0 copy-start.1
  13.7 37.4 %all_to_all.5 = f32[128,1,3328]{2,1,0:T(1,128)S(1)} all-to-all(f32[128,1,3328]{2,1,0:T(1,128)S(1)} %spread.1), channel_id=1, replica_groups=mesh['gx'=16,'gy'=8] {'gx','gy'}, dimensions={0} | all-to-all | bytes 3407872 | tf_op jit(solution)/shard_map/all_to_all | solution.py:565
  51.1 0.0 copy-done
  51.1 0.0 copy-done.1
  51.1 2.3 %collide.1 = (f32[19,32,512]{2,1,0:T(8,128)S(1)}, f32[16,32,128]{2,1,0:T(8,128)S(1)}, f32[1,32,128]{2,1,0:T(8,128)S(1)}, f32[32,128]{1,0:T(8,128)S(1)}) custom-call(s32[6,32]{1,0:T(8,128)S(1)} %bitcast.10, f32[3328,128]{1,0:T(8,128)S(1)} %bitcast.7, f32[19,32,512]{2,1,0:T(8,128)S(1)} %bitcast.8), custom_call_target="tpu_custom_call" | custom-call | tf_op jit(solution)/shard_map/collide/pallas_call | solution.py:339
  53.4 1.4 %collective-permute-start.2 = (f32[16,32,128]{2,1,0:T(8,128)S(1)}, f32[16,32,128]{2,1,0:T(8,128)S(1)}, u32[]{:S(2)}, u32[]{:S(2)}) collective-permute-start(f32[16,32,128]{2,1,0:T(8,128)S(1)} %get-tuple-element.17.mine), channel_id=1, source_target_pairs={{0,120},{8,0},{16,8},{24,16},{32,24},{40,32},{48,40},{56,48},{64,5... | collective-permute-start | bytes 786440 | tf_op jit(solution)/shard_map/ppermute | solution.py:552
  54.8 0.1 collective-permute-start.1
  54.9 1.5 %collective-permute-start.3 = (f32[1,32,128]{2,1,0:T(8,128)S(1)}, f32[1,32,128]{2,1,0:T(8,128)S(1)}, u32[]{:S(2)}, u32[]{:S(2)}) collective-permute-start(f32[1,32,128]{2,1,0:T(8,128)S(1)} %get-tuple-element.16), channel_id=1, source_target_pairs={{0,112},{8,120},{16,0},{24,8},{32,16},{40,24},{48,32},{56,40},{64,... | collective-permute-start | bytes 49160 | tf_op jit(solution)/shard_map/ppermute | solution.py:552
  56.4 1.5 %collective-permute-start = (f32[1,32,128]{2,1,0:T(8,128)S(1)}, f32[1,32,128]{2,1,0:T(8,128)S(1)}, u32[]{:S(2)}, u32[]{:S(2)}) collective-permute-start(f32[1,32,128]{2,1,0:T(8,128)S(1)} %get-tuple-element.16), channel_id=1, source_target_pairs={{0,16},{8,24},{16,32},{24,40},{32,48},{40,56},{48,64},{56,72},{64,... | collective-permute-start | bytes 49160 | tf_op jit(solution)/shard_map/ppermute | solution.py:552
  57.9 2.7 %collective-permute-done.3.right2 = f32[1,32,128]{2,1,0:T(8,128)S(1)} collective-permute-done((f32[1,32,128]{2,1,0:T(8,128)S(1)}, f32[1,32,128]{2,1,0:T(8,128)S(1)}, u32[]{:S(2)}, u32[]{:S(2)}) %collective-permute-start.3) | collective-permute-done | bytes 16416 | tf_op jit(solution)/shard_map/ppermute | solution.py:552
  60.6 2.4 %collective-permute-done.left2 = f32[1,32,128]{2,1,0:T(8,128)S(1)} collective-permute-done((f32[1,32,128]{2,1,0:T(8,128)S(1)}, f32[1,32,128]{2,1,0:T(8,128)S(1)}, u32[]{:S(2)}, u32[]{:S(2)}) %collective-permute-start) | collective-permute-done | bytes 16416 | tf_op jit(solution)/shard_map/ppermute | solution.py:552
  62.9 0.0 collective-permute-done.2.right
  62.9 2.4 %collective-permute-done.1.left = f32[16,32,128]{2,1,0:T(8,128)S(1)} collective-permute-done((f32[16,32,128]{2,1,0:T(8,128)S(1)}, f32[16,32,128]{2,1,0:T(8,128)S(1)}, u32[]{:S(2)}, u32[]{:S(2)}) %collective-permute-start.1) | collective-permute-done | bytes 262176 | tf_op jit(solution)/shard_map/ppermute | solution.py:552
  65.4 0.9 %route.1 = (f32[16,32,128]{2,1,0:T(8,128)S(1)}, f32[16,32,128]{2,1,0:T(8,128)S(1)}, f32[16,32,128]{2,1,0:T(8,128)S(1)}, f32[1,32,128]{2,1,0:T(8,128)S(1)}, f32[1,32,128]{2,1,0:T(8,128)S(1)}) custom-call(f32[1,32,128]{2,1,0:T(8,128)S(1)} %collective-permute-done.left2, f32[16,32,128]{2,1,0:T(8,128)S(1)} %collective-permute-done.1.left, ...), custom_call_target="tpu_custom_call" | custom-call | tf_op jit(solution)/shard_map/route/pallas_call | solution.py:416
  66.2 1.9 %collective-permute-start.4 = (f32[16,32,128]{2,1,0:T(8,128)S(1)}, f32[16,32,128]{2,1,0:T(8,128)S(1)}, u32[]{:S(2)}, u32[]{:S(2)}) collective-permute-start(f32[16,32,128]{2,1,0:T(8,128)S(1)} %get-tuple-element.19), channel_id=1, source_target_pairs={{0,1},{1,2},{2,3},{3,4},{4,5},{5,6},{6,7},{7,0},{8,9},{9,10},{10,1... | collective-permute-start | bytes 786440 | tf_op jit(solution)/shard_map/ppermute | solution.py:552
  68.1 0.1 collective-permute-start.5
  68.3 0.1 collective-permute-start.6
  68.4 2.5 %collective-permute-start.7 = (f32[1,32,128]{2,1,0:T(8,128)S(1)}, f32[1,32,128]{2,1,0:T(8,128)S(1)}, u32[]{:S(2)}, u32[]{:S(2)}) collective-permute-start(f32[1,32,128]{2,1,0:T(8,128)S(1)} %get-tuple-element.22), channel_id=1, source_target_pairs={{0,6},{1,7},{2,0},{3,1},{4,2},{5,3},{6,4},{7,5},{8,14},{9,15},{10,... | collective-permute-start | bytes 49160 | tf_op jit(solution)/shard_map/ppermute | solution.py:552
  71.0 0.4 inside.1.most
  71.3 3.5 %collective-permute-done.6.below2 = f32[1,32,128]{2,1,0:T(8,128)S(1)} collective-permute-done((f32[1,32,128]{2,1,0:T(8,128)S(1)}, f32[1,32,128]{2,1,0:T(8,128)S(1)}, u32[]{:S(2)}, u32[]{:S(2)}) %collective-permute-start.6) | collective-permute-done | bytes 16416 | tf_op jit(solution)/shard_map/ppermute | solution.py:552
  74.9 0.0 collective-permute-done.7.above2
  74.9 0.0 collective-permute-done.4.below
  74.9 0.0 collective-permute-done.5.above
  74.9 1.7 %fill.1 = f32[19,32,512]{2,1,0:T(8,128)} custom-call(f32[32,128]{1,0:T(8,128)S(1)} %get-tuple-element.14.goal, f32[19,32,512]{2,1,0:T(8,128)S(1)} %inside.1.most, f32[16,32,128]{2,1,0:T(8,128)S(1)} %get-tuple-element.18.own, f32[16,32,128]{2,1,0:T(8,128)S(1)} %collective-permute-done.4.below, f32[16,32,128]{2,1,0:T(8,128)S(1)} %collective-permute-done.5.above, ...), custom_call_target="tpu_custom_call" | custom-call | tf_op jit(solution)/shard_map/fill/pallas_call | solution.py:539
Async XLA Ops:
  13.7 37.4 %copy-start = (f32[32,19,512]{2,0,1:T(8,128)S(1)}, f32[32,19,512]{2,0,1:T(8,128)}, u32[]{:S(2)}) copy-start(f32[32,19,512]{2,0,1:T(8,128)} %param.7) | copy-start | bytes 3735556
  13.7 37.4 %copy-start.1 = (s32[32,6]{0,1:T(8,128)S(1)}, s32[32,6]{0,1:T(8,128)}, u32[]{:S(2)}) copy-start(s32[32,6]{0,1:T(8,128)} %param.8) | copy-start | bytes 2308
  53.4 9.6 %collective-permute-start.2 = (f32[16,32,128]{2,1,0:T(8,128)S(1)}, f32[16,32,128]{2,1,0:T(8,128)S(1)}, u32[]{:S(2)}, u32[]{:S(2)}) collective-permute-start(f32[16,32,128]{2,1,0:T(8,128)S(1)} %get-tuple-element.17.mine), channel_id=1, source_target_pairs={{0,120},{8,0},{16,8},{24,16},{32,24},{40,32},{48,40},{56,48},{64,5... | collective-permute-start | bytes 786440 | tf_op jit(solution)/shard_map/ppermute | solution.py:552
  54.8 10.6 %collective-permute-start.1 = (f32[16,32,128]{2,1,0:T(8,128)S(1)}, f32[16,32,128]{2,1,0:T(8,128)S(1)}, u32[]{:S(2)}, u32[]{:S(2)}) collective-permute-start(f32[16,32,128]{2,1,0:T(8,128)S(1)} %get-tuple-element.17.mine), channel_id=1, source_target_pairs={{0,8},{8,16},{16,24},{24,32},{32,40},{40,48},{48,56},{56,64},{64,7... | collective-permute-start | bytes 786440 | tf_op jit(solution)/shard_map/ppermute | solution.py:552
  54.9 5.6 %collective-permute-start.3 = (f32[1,32,128]{2,1,0:T(8,128)S(1)}, f32[1,32,128]{2,1,0:T(8,128)S(1)}, u32[]{:S(2)}, u32[]{:S(2)}) collective-permute-start(f32[1,32,128]{2,1,0:T(8,128)S(1)} %get-tuple-element.16), channel_id=1, source_target_pairs={{0,112},{8,120},{16,0},{24,8},{32,16},{40,24},{48,32},{56,40},{64,... | collective-permute-start | bytes 49160 | tf_op jit(solution)/shard_map/ppermute | solution.py:552
  56.4 6.6 %collective-permute-start = (f32[1,32,128]{2,1,0:T(8,128)S(1)}, f32[1,32,128]{2,1,0:T(8,128)S(1)}, u32[]{:S(2)}, u32[]{:S(2)}) collective-permute-start(f32[1,32,128]{2,1,0:T(8,128)S(1)} %get-tuple-element.16), channel_id=1, source_target_pairs={{0,16},{8,24},{16,32},{24,40},{32,48},{40,56},{48,64},{56,72},{64,... | collective-permute-start | bytes 49160 | tf_op jit(solution)/shard_map/ppermute | solution.py:552
  66.2 8.6 %collective-permute-start.4 = (f32[16,32,128]{2,1,0:T(8,128)S(1)}, f32[16,32,128]{2,1,0:T(8,128)S(1)}, u32[]{:S(2)}, u32[]{:S(2)}) collective-permute-start(f32[16,32,128]{2,1,0:T(8,128)S(1)} %get-tuple-element.19), channel_id=1, source_target_pairs={{0,1},{1,2},{2,3},{3,4},{4,5},{5,6},{6,7},{7,0},{8,9},{9,10},{10,1... | collective-permute-start | bytes 786440 | tf_op jit(solution)/shard_map/ppermute | solution.py:552
  68.1 6.7 %collective-permute-start.5 = (f32[16,32,128]{2,1,0:T(8,128)S(1)}, f32[16,32,128]{2,1,0:T(8,128)S(1)}, u32[]{:S(2)}, u32[]{:S(2)}) collective-permute-start(f32[16,32,128]{2,1,0:T(8,128)S(1)} %get-tuple-element.20), channel_id=1, source_target_pairs={{0,7},{1,0},{2,1},{3,2},{4,3},{5,4},{6,5},{7,6},{8,15},{9,8},{10,9... | collective-permute-start | bytes 786440 | tf_op jit(solution)/shard_map/ppermute | solution.py:552
  68.3 6.6 %collective-permute-start.6 = (f32[1,32,128]{2,1,0:T(8,128)S(1)}, f32[1,32,128]{2,1,0:T(8,128)S(1)}, u32[]{:S(2)}, u32[]{:S(2)}) collective-permute-start(f32[1,32,128]{2,1,0:T(8,128)S(1)} %get-tuple-element.21), channel_id=1, source_target_pairs={{0,2},{1,3},{2,4},{3,5},{4,6},{5,7},{6,0},{7,1},{8,10},{9,11},{10,... | collective-permute-start | bytes 49160 | tf_op jit(solution)/shard_map/ppermute | solution.py:552
  68.4 6.4 %collective-permute-start.7 = (f32[1,32,128]{2,1,0:T(8,128)S(1)}, f32[1,32,128]{2,1,0:T(8,128)S(1)}, u32[]{:S(2)}, u32[]{:S(2)}) collective-permute-start(f32[1,32,128]{2,1,0:T(8,128)S(1)} %get-tuple-element.22), channel_id=1, source_target_pairs={{0,6},{1,7},{2,0},{3,1},{4,2},{5,3},{6,4},{7,5},{8,14},{9,15},{10,... | collective-permute-start | bytes 49160 | tf_op jit(solution)/shard_map/ppermute | solution.py:552

commit v7 on v6

--- a/solution.py
+++ b/solution.py
@@ -55,6 +55,25 @@
     links = nt_dot(st[...], st[...])
     for c in copies[1:]:
         c.wait()
+    sub = lax.broadcasted_iota(i32, (8, 128), 0)
+    lane = lax.broadcasted_iota(i32, (8, 128), 1)
+    slots = out.shape[0]
+    tail_row = jnp.full((8, 128), -1.0, f32)
+    table_row = jnp.zeros((8, 128), f32)
+    for f in range(4):
+        one_face = jnp.concatenate([near[f + 2 : f + 3, :].astype(f32), jnp.zeros((1, 96), f32)], axis=1)
+        one_face = jnp.broadcast_to(one_face, (8, 128))
+        table_row = jnp.where(lane // 32 == f, pltpu.roll(one_face, 32 * f, 1) if f else one_face, table_row)
+
+    def clear(t, carry):
+        for m in range(8):
+            out[t * 8 + m, :, 0:3072] = jnp.zeros((1, 3072), f32)
+            out[t * 8 + m, :, 3072:3200] = tail_row[0:1]
+            out[t * 8 + m, :, 3200:3328] = table_row[0:1]
+            count[t * 8 + m] = 0
+        return carry
+
+    lax.fori_loop(0, slots // 8, clear, 0)
     for r in range(0, nv, 128):
         for d in range(3):
             have = min(verts - r, 128)
@@ -81,25 +100,6 @@
         for d in range(3):
             force[d] = force[d] + rest[d * cells : (d + 1) * cells]
 
-    sub = lax.broadcasted_iota(i32, (8, 128), 0)
-    lane = lax.broadcasted_iota(i32, (8, 128), 1)
-    slots = out.shape[0]
-    tail_row = jnp.full((8, 128), -1.0, f32)
-    table_row = jnp.zeros((8, 128), f32)
-    for f in range(4):
-        one_face = jnp.concatenate([near[f + 2 : f + 3, :].astype(f32), jnp.zeros((1, 96), f32)], axis=1)
-        one_face = jnp.broadcast_to(one_face, (8, 128))
-        table_row = jnp.where(lane // 32 == f, pltpu.roll(one_face, 32 * f, 1) if f else one_face, table_row)
-
-    def clear(t, carry):
-        for m in range(8):
-            out[t * 8 + m, :, 0:3072] = jnp.zeros((1, 3072), f32)
-            out[t * 8 + m, :, 3072:3200] = tail_row[0:1]
-            out[t * 8 + m, :, 3200:3328] = table_row[0:1]
-            count[t * 8 + m] = 0
-        return carry
-
-    lax.fori_loop(0, slots // 8, clear, 0)
     sub8 = lax.broadcasted_iota(i32, (8, nv), 0)
     g_even = (2 * (sub8 % 4)).astype(f32)
     g_odd = g_even + 1.0

time: 76.8 us -> 76.7 us (level)
  no operation moved by 1% of the time
where the time goes in v7:
time: 76.7 us; the launch traced here: 76.6 us
  blocking collectives  37.4 us (49%)
  Pallas kernels  18.8 us (25%)
  waiting for transfers between devices  11 us (14%)
  starting transfers between devices  9.23 us (12%)
    all_to_all x1, blocking collectives, body(): got = lax.all_to_all(slots, BOTH, split_axis=0, concat_axis=0, tiled=True)  37.4 us
    pallas_call x1, Pallas kernels, spread(): pl.pallas_call(spread_kernel, out_shape=jax.ShapeDtypeStruct((devices, 1,...  13.6 us
    ppermute x8, waiting for transfers between devices, send(): lax.ppermute(array, axis, [(i, (i + step) % size) for i in range(size)])  11 us
    ppermute x8, starting transfers between devices, send(): lax.ppermute(array, axis, [(i, (i + step) % size) for i in range(size)])  9.23 us
    pallas_call x1, Pallas kernels, collide(): pl.pallas_call(collide_kernel, out_shape=(jax.ShapeDtypeStruct((19, 32, 5...  2.26 us
    pallas_call x1, Pallas kernels, fill(): pl.pallas_call(ghost_kernel, out_shape=jax.ShapeDtypeStruct((19, 32, 512)...  1.72 us
  transfers between devices with their start and end apart: 8, of which 4 were waited for; matrix products, arithmetic and copies ran while one was open for 0% of the time, Pallas kernels for 0%

profile of v7, /device:TPU:1, one launch (start us, length us, event | category | flops | bytes accessed | tf_op | source)
XLA Modules:
  0.0 76.6 jit_solution(14975629215878723350)
XLA Ops:
  0.0 13.6 %spread.1 = f32[128,1,3328]{2,1,0:T(1,128)S(1)} custom-call(s32[128]{0:T(128)} %bitcast.13, s32[128]{0:T(128)} %block_in.1, f32[128]{0:T(128)} %stiff_in.1, f32[3,642,128]{2,1,0:T(8,128)} %bitcast.11, s32[3,1280]{1,0:T(4,128)} %bitcast.12, s32[6,32]{1,0:T(8,128)} %bitcast.9), custom_call_target="tpu_custom_call" | custom-call | tf_op jit(solution)/shard_map/spread/pallas_call | solution.py:176
  13.6 0.0 copy-start
  13.7 0.0 copy-start.1
  13.7 37.4 %all_to_all.5 = f32[128,1,3328]{2,1,0:T(1,128)S(1)} all-to-all(f32[128,1,3328]{2,1,0:T(1,128)S(1)} %spread.1), channel_id=1, replica_groups=mesh['gx'=16,'gy'=8] {'gx','gy'}, dimensions={0} | all-to-all | bytes 3407872 | tf_op jit(solution)/shard_map/all_to_all | solution.py:565
  51.1 0.0 copy-done
  51.1 0.0 copy-done.1
  51.1 2.3 %collide.1 = (f32[19,32,512]{2,1,0:T(8,128)S(1)}, f32[16,32,128]{2,1,0:T(8,128)S(1)}, f32[1,32,128]{2,1,0:T(8,128)S(1)}, f32[32,128]{1,0:T(8,128)S(1)}) custom-call(s32[6,32]{1,0:T(8,128)S(1)} %bitcast.10, f32[3328,128]{1,0:T(8,128)S(1)} %bitcast.7, f32[19,32,512]{2,1,0:T(8,128)S(1)} %bitcast.8), custom_call_target="tpu_custom_call" | custom-call | tf_op jit(solution)/shard_map/collide/pallas_call | solution.py:339
  53.4 1.4 %collective-permute-start.2 = (f32[16,32,128]{2,1,0:T(8,128)S(1)}, f32[16,32,128]{2,1,0:T(8,128)S(1)}, u32[]{:S(2)}, u32[]{:S(2)}) collective-permute-start(f32[16,32,128]{2,1,0:T(8,128)S(1)} %get-tuple-element.17.mine), channel_id=1, source_target_pairs={{0,120},{8,0},{16,8},{24,16},{32,24},{40,32},{48,40},{56,48},{64,5... | collective-permute-start | bytes 786440 | tf_op jit(solution)/shard_map/ppermute | solution.py:552
  54.8 0.1 collective-permute-start.1
  54.9 1.5 %collective-permute-start.3 = (f32[1,32,128]{2,1,0:T(8,128)S(1)}, f32[1,32,128]{2,1,0:T(8,128)S(1)}, u32[]{:S(2)}, u32[]{:S(2)}) collective-permute-start(f32[1,32,128]{2,1,0:T(8,128)S(1)} %get-tuple-element.16), channel_id=1, source_target_pairs={{0,112},{8,120},{16,0},{24,8},{32,16},{40,24},{48,32},{56,40},{64,... | collective-permute-start | bytes 49160 | tf_op jit(solution)/shard_map/ppermute | solution.py:552
  56.4 1.5 %collective-permute-start = (f32[1,32,128]{2,1,0:T(8,128)S(1)}, f32[1,32,128]{2,1,0:T(8,128)S(1)}, u32[]{:S(2)}, u32[]{:S(2)}) collective-permute-start(f32[1,32,128]{2,1,0:T(8,128)S(1)} %get-tuple-element.16), channel_id=1, source_target_pairs={{0,16},{8,24},{16,32},{24,40},{32,48},{40,56},{48,64},{56,72},{64,... | collective-permute-start | bytes 49160 | tf_op jit(solution)/shard_map/ppermute | solution.py:552
  57.9 2.7 %collective-permute-done.3.right2 = f32[1,32,128]{2,1,0:T(8,128)S(1)} collective-permute-done((f32[1,32,128]{2,1,0:T(8,128)S(1)}, f32[1,32,128]{2,1,0:T(8,128)S(1)}, u32[]{:S(2)}, u32[]{:S(2)}) %collective-permute-start.3) | collective-permute-done | bytes 16416 | tf_op jit(solution)/shard_map/ppermute | solution.py:552
  60.5 2.4 %collective-permute-done.left2 = f32[1,32,128]{2,1,0:T(8,128)S(1)} collective-permute-done((f32[1,32,128]{2,1,0:T(8,128)S(1)}, f32[1,32,128]{2,1,0:T(8,128)S(1)}, u32[]{:S(2)}, u32[]{:S(2)}) %collective-permute-start) | collective-permute-done | bytes 16416 | tf_op jit(solution)/shard_map/ppermute | solution.py:552
  62.9 0.0 collective-permute-done.2.right
  62.9 2.4 %collective-permute-done.1.left = f32[16,32,128]{2,1,0:T(8,128)S(1)} collective-permute-done((f32[16,32,128]{2,1,0:T(8,128)S(1)}, f32[16,32,128]{2,1,0:T(8,128)S(1)}, u32[]{:S(2)}, u32[]{:S(2)}) %collective-permute-start.1) | collective-permute-done | bytes 262176 | tf_op jit(solution)/shard_map/ppermute | solution.py:552
  65.3 0.9 %route.1 = (f32[16,32,128]{2,1,0:T(8,128)S(1)}, f32[16,32,128]{2,1,0:T(8,128)S(1)}, f32[16,32,128]{2,1,0:T(8,128)S(1)}, f32[1,32,128]{2,1,0:T(8,128)S(1)}, f32[1,32,128]{2,1,0:T(8,128)S(1)}) custom-call(f32[1,32,128]{2,1,0:T(8,128)S(1)} %collective-permute-done.left2, f32[16,32,128]{2,1,0:T(8,128)S(1)} %collective-permute-done.1.left, ...), custom_call_target="tpu_custom_call" | custom-call | tf_op jit(solution)/shard_map/route/pallas_call | solution.py:416
  66.2 1.9 %collective-permute-start.4 = (f32[16,32,128]{2,1,0:T(8,128)S(1)}, f32[16,32,128]{2,1,0:T(8,128)S(1)}, u32[]{:S(2)}, u32[]{:S(2)}) collective-permute-start(f32[16,32,128]{2,1,0:T(8,128)S(1)} %get-tuple-element.19), channel_id=1, source_target_pairs={{0,1},{1,2},{2,3},{3,4},{4,5},{5,6},{6,7},{7,0},{8,9},{9,10},{10,1... | collective-permute-start | bytes 786440 | tf_op jit(solution)/shard_map/ppermute | solution.py:552
  68.1 0.2 collective-permute-start.5
  68.3 0.1 collective-permute-start.6
  68.4 2.5 %collective-permute-start.7 = (f32[1,32,128]{2,1,0:T(8,128)S(1)}, f32[1,32,128]{2,1,0:T(8,128)S(1)}, u32[]{:S(2)}, u32[]{:S(2)}) collective-permute-start(f32[1,32,128]{2,1,0:T(8,128)S(1)} %get-tuple-element.22), channel_id=1, source_target_pairs={{0,6},{1,7},{2,0},{3,1},{4,2},{5,3},{6,4},{7,5},{8,14},{9,15},{10,... | collective-permute-start | bytes 49160 | tf_op jit(solution)/shard_map/ppermute | solution.py:552
  70.9 0.4 inside.1.most
  71.3 3.5 %collective-permute-done.6.below2 = f32[1,32,128]{2,1,0:T(8,128)S(1)} collective-permute-done((f32[1,32,128]{2,1,0:T(8,128)S(1)}, f32[1,32,128]{2,1,0:T(8,128)S(1)}, u32[]{:S(2)}, u32[]{:S(2)}) %collective-permute-start.6) | collective-permute-done | bytes 16416 | tf_op jit(solution)/shard_map/ppermute | solution.py:552
  74.9 0.0 collective-permute-done.7.above2
  74.9 0.0 collective-permute-done.4.below
  74.9 0.0 collective-permute-done.5.above
  74.9 1.7 %fill.1 = f32[19,32,512]{2,1,0:T(8,128)} custom-call(f32[32,128]{1,0:T(8,128)S(1)} %get-tuple-element.14.goal, f32[19,32,512]{2,1,0:T(8,128)S(1)} %inside.1.most, f32[16,32,128]{2,1,0:T(8,128)S(1)} %get-tuple-element.18.own, f32[16,32,128]{2,1,0:T(8,128)S(1)} %collective-permute-done.4.below, f32[16,32,128]{2,1,0:T(8,128)S(1)} %collective-permute-done.5.above, ...), custom_call_target="tpu_custom_call" | custom-call | tf_op jit(solution)/shard_map/fill/pallas_call | solution.py:539
Async XLA Ops:
  13.6 37.4 %copy-start = (f32[32,19,512]{2,0,1:T(8,128)S(1)}, f32[32,19,512]{2,0,1:T(8,128)}, u32[]{:S(2)}) copy-start(f32[32,19,512]{2,0,1:T(8,128)} %param.7) | copy-start | bytes 3735556
  13.7 37.4 %copy-start.1 = (s32[32,6]{0,1:T(8,128)S(1)}, s32[32,6]{0,1:T(8,128)}, u32[]{:S(2)}) copy-start(s32[32,6]{0,1:T(8,128)} %param.8) | copy-start | bytes 2308
  53.4 9.6 %collective-permute-start.2 = (f32[16,32,128]{2,1,0:T(8,128)S(1)}, f32[16,32,128]{2,1,0:T(8,128)S(1)}, u32[]{:S(2)}, u32[]{:S(2)}) collective-permute-start(f32[16,32,128]{2,1,0:T(8,128)S(1)} %get-tuple-element.17.mine), channel_id=1, source_target_pairs={{0,120},{8,0},{16,8},{24,16},{32,24},{40,32},{48,40},{56,48},{64,5... | collective-permute-start | bytes 786440 | tf_op jit(solution)/shard_map/ppermute | solution.py:552
  54.8 10.6 %collective-permute-start.1 = (f32[16,32,128]{2,1,0:T(8,128)S(1)}, f32[16,32,128]{2,1,0:T(8,128)S(1)}, u32[]{:S(2)}, u32[]{:S(2)}) collective-permute-start(f32[16,32,128]{2,1,0:T(8,128)S(1)} %get-tuple-element.17.mine), channel_id=1, source_target_pairs={{0,8},{8,16},{16,24},{24,32},{32,40},{40,48},{48,56},{56,64},{64,7... | collective-permute-start | bytes 786440 | tf_op jit(solution)/shard_map/ppermute | solution.py:552
  54.9 5.6 %collective-permute-start.3 = (f32[1,32,128]{2,1,0:T(8,128)S(1)}, f32[1,32,128]{2,1,0:T(8,128)S(1)}, u32[]{:S(2)}, u32[]{:S(2)}) collective-permute-start(f32[1,32,128]{2,1,0:T(8,128)S(1)} %get-tuple-element.16), channel_id=1, source_target_pairs={{0,112},{8,120},{16,0},{24,8},{32,16},{40,24},{48,32},{56,40},{64,... | collective-permute-start | bytes 49160 | tf_op jit(solution)/shard_map/ppermute | solution.py:552
  56.4 6.6 %collective-permute-start = (f32[1,32,128]{2,1,0:T(8,128)S(1)}, f32[1,32,128]{2,1,0:T(8,128)S(1)}, u32[]{:S(2)}, u32[]{:S(2)}) collective-permute-start(f32[1,32,128]{2,1,0:T(8,128)S(1)} %get-tuple-element.16), channel_id=1, source_target_pairs={{0,16},{8,24},{16,32},{24,40},{32,48},{40,56},{48,64},{56,72},{64,... | collective-permute-start | bytes 49160 | tf_op jit(solution)/shard_map/ppermute | solution.py:552
  66.2 8.6 %collective-permute-start.4 = (f32[16,32,128]{2,1,0:T(8,128)S(1)}, f32[16,32,128]{2,1,0:T(8,128)S(1)}, u32[]{:S(2)}, u32[]{:S(2)}) collective-permute-start(f32[16,32,128]{2,1,0:T(8,128)S(1)} %get-tuple-element.19), channel_id=1, source_target_pairs={{0,1},{1,2},{2,3},{3,4},{4,5},{5,6},{6,7},{7,0},{8,9},{9,10},{10,1... | collective-permute-start | bytes 786440 | tf_op jit(solution)/shard_map/ppermute | solution.py:552
  68.1 6.8 %collective-permute-start.5 = (f32[16,32,128]{2,1,0:T(8,128)S(1)}, f32[16,32,128]{2,1,0:T(8,128)S(1)}, u32[]{:S(2)}, u32[]{:S(2)}) collective-permute-start(f32[16,32,128]{2,1,0:T(8,128)S(1)} %get-tuple-element.20), channel_id=1, source_target_pairs={{0,7},{1,0},{2,1},{3,2},{4,3},{5,4},{6,5},{7,6},{8,15},{9,8},{10,9... | collective-permute-start | bytes 786440 | tf_op jit(solution)/shard_map/ppermute | solution.py:552
  68.3 6.6 %collective-permute-start.6 = (f32[1,32,128]{2,1,0:T(8,128)S(1)}, f32[1,32,128]{2,1,0:T(8,128)S(1)}, u32[]{:S(2)}, u32[]{:S(2)}) collective-permute-start(f32[1,32,128]{2,1,0:T(8,128)S(1)} %get-tuple-element.21), channel_id=1, source_target_pairs={{0,2},{1,3},{2,4},{3,5},{4,6},{5,7},{6,0},{7,1},{8,10},{9,11},{10,... | collective-permute-start | bytes 49160 | tf_op jit(solution)/shard_map/ppermute | solution.py:552
  68.4 6.4 %collective-permute-start.7 = (f32[1,32,128]{2,1,0:T(8,128)S(1)}, f32[1,32,128]{2,1,0:T(8,128)S(1)}, u32[]{:S(2)}, u32[]{:S(2)}) collective-permute-start(f32[1,32,128]{2,1,0:T(8,128)S(1)} %get-tuple-element.22), channel_id=1, source_target_pairs={{0,6},{1,7},{2,0},{3,1},{4,2},{5,3},{6,4},{7,5},{8,14},{9,15},{10,... | collective-permute-start | bytes 49160 | tf_op jit(solution)/shard_map/ppermute | solution.py:552
